TPU v7x, 32 devices: a whole 2x2x4 slice. The times are simulated.
32 devices in a mesh: dp: 16 (over z, y, x), rep: 2 (over core).
Axes of the slice: x: 2, y: 2, z: 4, core: 2. Of those that a mesh axis runs over, the one named last changes fastest.
Arguments:
- patches: bfloat16 [192, 196, 768], P(('dp', 'rep')), may hold values from -6 to 6
- targets: bfloat16 [192, 196, 768], P(('dp', 'rep')), may hold values from -5.5 to 5.5
- keep: int32 [192, 49], P(('dp', 'rep')), may hold values from 0 to 195, as said below
- counts: int32 [16, 2], P('dp', 'rep'), may hold values from 1 to 6, as said below
- step: int32 [1], replicated, may hold values from 2 to 20
- master: float32 [1629760], P(('dp', 'rep')), may hold values from -2.5 to 2.5
- first: float32 [1629760], P(('dp', 'rep')), may hold values from -0.00046999087 to 0.00046999087
- second: float32 [1629760], P(('dp', 'rep')), may hold values from 1.5339682e-09 to 9.817396e-08
Outputs:
- new_master: float32 [1629760], P(('dp', 'rep'))
- new_first: float32 [1629760], P(('dp', 'rep'))
- new_second: float32 [1629760], P(('dp', 'rep'))
- copy: bfloat16 [1629760], P(('dp', 'rep'))
- loss: float32 [], replicated
- norm: float32 [], replicated
Inputs may be any that keep to these rules, and one draw needn't show every extreme that they name: `keep`: each row lists 49 distinct patch numbers of one image. A device's live image slots are its first counts[d, r]. In each aligned group of four devices along dp (for each r) exactly one device, never the first or last of the group, holds 3 to 6 live images; the others hold 1 or 2. Some device holds 6 in every draw.
All inputs are finite; a program needn't handle non-finite values.
Results may differ from a plain program's by a relative error of at most 0.0081.
Values may be sent and summed in bfloat16 or wider, within the bound.
A program may use at most 128 MiB of HBM per device.

v0:
```python
import functools
import itertools
import math

import jax
import jax.numpy as jnp
import numpy as np
from jax import lax
from jax.experimental import pallas as pl
from jax.experimental.pallas import tpu as pltpu
from jax.sharding import PartitionSpec as P

D = 192
HEADS = 3
FF = 768
E = 256
DHEADS = 8
DFF = 1024
PIX = 768
GRID = 14
VIS = 49
NP = 196

FLOAT = jnp.float32
BRAIN = jnp.bfloat16
CLIP = 0.05
BETA_ONE = 0.5
BETA_TWO = 0.5
LEARN = 0.01
DECAY = 0.05
EPSILON = 1e-08
LN_EPS = 1e-06

ROWS = 208
HOME = 64
LIVE_CAP = 3
PAIR = ((1,), (1,)), ((), ())
DEEP = ((0,), (0,)), ((), ())
LOG_TWO_E = 1.4426950408889634


def block_table(prefix, width, hidden, proj_fan, rate):
    return [
        (prefix + "ln1g", (width,), "gain", 1, rate),
        (prefix + "ln1b", (width,), "bias", 1, rate),
        (prefix + "qkv", (width, 3 * width), "matrix", width, rate),
        (prefix + "qvb", (2 * width,), "bias", 1, rate),
        (prefix + "proj", (width, width), "matrix", proj_fan, rate),
        (prefix + "projb", (width,), "bias", 1, rate),
        (prefix + "ln2g", (width,), "gain", 1, rate),
        (prefix + "ln2b", (width,), "bias", 1, rate),
        (prefix + "fc1", (width, hidden), "matrix", width, rate),
        (prefix + "fc1b", (hidden,), "bias", 1, rate),
        (prefix + "fc2", (hidden, width), "matrix", hidden, rate),
        (prefix + "fc2b", (width,), "bias", 1, rate),
    ]


def param_table():
    table = [("patch", (PIX, D), "matrix", PIX, 0.75), ("patchb", (D,), "bias", 1, 0.75)]
    table = table + block_table("enc_", D, FF, D // 4, 0.9)
    table = table + [
        ("encg", (D,), "gain", 1, 1.0),
        ("encb", (D,), "bias", 1, 1.0),
        ("embed", (D, E), "matrix", D, 1.0),
        ("embedb", (E,), "bias", 1, 1.0),
        ("mask", (E,), "token", 1, 1.0),
    ]
    table = table + block_table("dec_", E, DFF, E // 8, 1.0)
    table = table + [
        ("decg", (E,), "gain", 1, 1.0),
        ("decb", (E,), "bias", 1, 1.0),
        ("head", (E, PIX), "matrix", E, 1.0),
        ("headb", (PIX,), "bias", 1, 1.0),
    ]
    return table


MESH = pl.DeviceIdType.MESH
LANES = 128


def layout():
    table = {}
    offset = 0
    for name, shape, kind, fan, rate in param_table():
        table[name] = (offset, shape)
        offset += math.prod(shape)
    return table


class Plan:
    def __init__(self, length, count):
        self.length = length
        self.count = count
        self.outer = count // 8
        self.rows = -(-((LANES - 1 + length + LANES - 1) // LANES) // 16) * 16
        units = self.rows // 16
        first = max(1, min(round(0.389 * units), (units - 1) // 2))
        sizes = (first * 16, first * 16, self.rows - 2 * first * 16)
        starts = (0, sizes[0], sizes[0] + sizes[1])
        self.parts = tuple(zip(starts, sizes))
        self.orders = ("ACB", "ABC", "CBA")
        self.frame_rows = -(-(length * count) // LANES // 8 * 8) + 64

    def base(self, index):
        return index * self.length // LANES

    def lead(self, index):
        return index * self.length % LANES

    def used(self, index):
        return (self.lead(index) + self.length + LANES - 1) // LANES


def position():
    chip = lax.axis_index("dp")
    core = lax.axis_index("rep")
    return {"A": chip // 4, "B": chip // 2 % 2, "C": chip % 2, "r": core}


def device_of(place):
    return (place["A"] * 4 + place["B"] * 2 + place["C"], place["r"])


def moved(place, dim, value):
    changed = dict(place)
    changed[dim] = value
    return changed


def peer_values(place, dim, outer):
    if dim == "A":
        return [lax.rem(place["A"] + step, outer) for step in range(1, outer)]
    return [1 - place[dim]]


def source_values(place, dim, outer):
    if dim == "A":
        return [lax.rem(place["A"] + outer - step, outer) for step in range(1, outer)]
    return [1 - place[dim]]


def meet(places):
    barrier = pltpu.get_barrier_semaphore()
    for place in places:
        pl.semaphore_signal(barrier, inc=1, device_id=device_of(place), device_id_type=MESH)
    pl.semaphore_wait(barrier, len(places))


def neighbours(place, outer):
    found = []
    for dim in "ABCr":
        for value in peer_values(place, dim, outer):
            found.append(moved(place, dim, value))
    return found


class Sender:
    def __init__(self, send, recv):
        self.send, self.recv, self.used = send, recv, 0

    def start(self, source, target, place):
        copy = pltpu.make_async_remote_copy(
            src_ref=source,
            dst_ref=target,
            send_sem=self.send.at[self.used],
            recv_sem=self.recv.at[self.used],
            device_id=device_of(place),
            device_id_type=MESH,
        )
        self.used += 1
        copy.start()
        return copy


def lane_iota(rows):
    return lax.broadcasted_iota(jnp.int32, (rows, LANES), 1)


HUBS = (1, 2)


def others_of(hub):
    return [spot for spot in range(4) if spot != hub]


def gather_body(
    plan, counts_ref, keep_ref, x_ref, patches_ref, targets_ref,
    out_ref, seen_ref, tgt_ref, meta_ref,
    line, rolled, pixels, spare, send, recv, local, hand, taken
):
    outer, rows = plan.outer, plan.rows
    place = position()
    a, b, c, r = (place[dim] for dim in "ABCr")
    spot = b * 2 + c
    pixel_copy = pltpu.make_async_copy(patches_ref, pixels, local.at[0])
    pixel_copy.start()
    target_copy = pltpu.make_async_copy(
        targets_ref.at[pl.ds(0, LIVE_CAP)], tgt_ref.at[pl.ds(0, LIVE_CAP)], local.at[1]
    )
    target_copy.start()
    index = ((a * 2 + b) * 2 + c) * 2 + r
    lead = lax.rem(index * plan.length, LANES)
    line[...] = jnp.zeros_like(line)
    line[pl.ds(0, plan.length)] = x_ref[...]
    turned = pltpu.roll(line[...].reshape(rows, LANES), lead, 1)
    rolled[pl.ds(0, 8), :] = jnp.zeros((8, LANES), FLOAT)
    rolled[pl.ds(8, rows), :] = turned
    block = jnp.where(lane_iota(rows) >= lead, turned, rolled[pl.ds(7, rows), :])
    out_ref[a, b, c, r] = block.astype(BRAIN)
    meet(neighbours(place, outer) + [moved(moved(place, "B", 1 - b), "C", 1 - c)])
    sender = Sender(send, recv)
    everything = []

    def region(part, whole, fixed):
        start, size = plan.parts[part]
        index = []
        for dim, extent in (("A", outer), ("B", 2), ("C", 2)):
            if dim in fixed:
                index.append(fixed[dim])
            else:
                index.append(pl.ds(0, extent) if dim in whole else place[dim])
        return out_ref.at[(*index, r, pl.ds(start, size))]

    def hand_over(hub, number):
        other = others_of(hub)[number]
        target = {"A": a, "B": other // 2, "C": other % 2, "r": r}
        pairs = (
            (spare.at[number], seen_ref.at[2 + hub]),
            (meta_ref.at[0], meta_ref.at[hub]),
            (targets_ref.at[3 + number], tgt_ref.at[2 + hub]),
        )
        return [
            pltpu.make_async_remote_copy(
                src_ref=source,
                dst_ref=to,
                send_sem=hand.at[hub - 1, number, kind],
                recv_sem=taken.at[hub - 1, kind],
                device_id=device_of(target),
                device_id_type=MESH,
            )
            for kind, (source, to) in enumerate(pairs)
        ]

    fresh = [(part, "", [{}]) for part in range(3)]
    sibling = moved(place, "r", 1 - r)
    for phase in range(4):
        flights = []
        if phase < 3:
            for part in range(3):
                order = plan.orders[part]
                dim = order[phase]
                source = region(part, order[:phase], {})
                for value in peer_values(place, dim, outer):
                    flights.append(sender.start(source, source, moved(place, dim, value)))
        for part, whole, news in fresh:
            for fixed in news:
                source = region(part, whole, fixed)
                everything.append(sender.start(source, source, sibling))
        fresh = []
        if phase < 3:
            for part in range(3):
                order = plan.orders[part]
                dim = order[phase]
                news = [{dim: value} for value in source_values(place, dim, outer)]
                fresh.append((part, order[:phase], news))
        if phase == 0:
            lane = lane_iota(8)
            row = lax.broadcasted_iota(jnp.int32, (8, LANES), 0)
            mine = jnp.where((lane == LANES - 1) & (row == 0), counts_ref[0, 0].astype(FLOAT), -1.0)
            meta_ref[0] = mine
            meta_ref[0, pl.ds(0, keep_ref.shape[0]), pl.ds(0, VIS)] = keep_ref[...].astype(FLOAT)
            pixel_copy.wait()

            def visible(image):
                number = lax.broadcasted_iota(jnp.int32, (NP, HOME), 0).astype(FLOAT)
                where = (number == meta_ref[0, pl.ds(image, 1), :][:, :HOME]).astype(BRAIN)
                return dot(where, pixels[image], DEEP).astype(BRAIN)

            for hub in HUBS:

                @pl.when(spot == hub)
                def _(hub=hub):
                    for number in range(3):
                        spare[number] = visible(3 + number)
                    for number in range(3):
                        for copy in hand_over(hub, number):
                            copy.start()

            for image in range(LIVE_CAP):
                seen_ref[image] = visible(image)
        for copy in flights:
            copy.wait()
    for copy in everything:
        copy.wait()
    for hub in HUBS:

        @pl.when(spot == hub)
        def _(hub=hub):
            for number in range(3):
                for copy in hand_over(hub, number):
                    copy.wait_send()

        @pl.when(spot != hub)
        def _(hub=hub):
            for copy in hand_over(hub, 0):
                copy.wait_recv()

    target_copy.wait()


def gather_params(counts, keep, master, patches, targets, plan):
    outer, rows = plan.outer, plan.rows
    copies = 3 * (outer + 1 + outer + 2)
    vmem = pl.BlockSpec(memory_space=pltpu.VMEM)
    smem = pl.BlockSpec(memory_space=pltpu.SMEM)
    far = pl.BlockSpec(memory_space=pl.ANY)
    return pl.pallas_call(
        functools.partial(gather_body, plan),
        out_shape=(
            jax.ShapeDtypeStruct((outer, 2, 2, 2, rows, LANES), BRAIN),
            jax.ShapeDtypeStruct((5, HOME, PIX), BRAIN),
            jax.ShapeDtypeStruct((5, NP, PIX), BRAIN),
            jax.ShapeDtypeStruct((3, 8, LANES), FLOAT),
        ),
        in_specs=[smem, vmem, vmem, far, far],
        out_specs=(vmem,) * 4,
        scratch_shapes=[
            pltpu.VMEM((rows * LANES,), FLOAT),
            pltpu.VMEM((rows + 8, LANES), FLOAT),
            pltpu.VMEM(patches.shape, BRAIN),
            pltpu.VMEM((3, HOME, PIX), BRAIN),
            pltpu.SemaphoreType.DMA((copies,)),
            pltpu.SemaphoreType.DMA((copies,)),
            pltpu.SemaphoreType.DMA((2,)),
            pltpu.SemaphoreType.DMA((2, 3, 3)),
            pltpu.SemaphoreType.DMA((2, 3)),
        ],
        compiler_params=pltpu.CompilerParams(
            collective_id=0, has_side_effects=True, vmem_limit_bytes=40 << 20
        ),
    )(counts, keep, master, patches, targets)


def reduce_scratch(plan):
    shapes = []
    for part in range(3):
        size = plan.parts[part][1]
        left = list("ABC")
        for dim in reversed(plan.orders[part]):
            left.remove(dim)
            others = tuple(plan.outer if other == "A" else 2 for other in left)
            peers = plan.outer - 1 if dim == "A" else 1
            shapes.append(pltpu.VMEM((peers, *others, size, LANES), BRAIN))
            shapes.append(pltpu.VMEM((peers, *others, size, LANES), BRAIN))
            shapes.append(pltpu.VMEM((*others, size, LANES), FLOAT))
    return shapes


def in_segments(index, segments):
    inside = None
    for start, stop in segments:
        here = (index >= start) & (index < stop)
        inside = here if inside is None else inside | here
    return inside


def matrix_segments():
    found = []
    for name, shape, kind, fan, rate in param_table():
        if kind == "matrix":
            start = layout()[name][0]
            found.append((start, start + math.prod(shape)))
    return found


def reduce_body(
    plan, held_ref, loss_ref, grad_ref, total_out, scalars_out, *scratch
):
    outer, rows = plan.outer, plan.rows
    core_in, rolled, near, far, mine, send, recv = scratch[:7]
    held_refs = scratch[7:]
    place = position()
    a, b, c, r = (place[dim] for dim in "ABCr")
    digits = {"A": a, "B": b, "C": c}
    device = ((a * 2 + b) * 2 + c) * 2 + r
    lead = lax.rem(device * plan.length, LANES)
    group = [
        {"A": a, "B": (b + k // 4) % 2, "C": (c + k // 2 % 2) % 2, "r": (r + k % 2) % 2}
        for k in range(1, 8)
    ]
    column = [moved(place, "A", value) for value in peer_values(place, "A", outer)]
    meet(group + column)
    sender = Sender(send, recv)
    sibling = moved(place, "r", 1 - r)
    pending = []
    core = []
    for part in range(3):
        start, size = plan.parts[part]
        span = pl.ds(start, size)
        full = (pl.ds(0, outer), pl.ds(0, 2), pl.ds(0, 2))
        core.append(
            sender.start(
                grad_ref.at[(*full, 1 - r, span)], core_in.at[(*full, span)], sibling
            )
        )
    state = []
    for part in range(3):
        core[part].wait_recv()
        pending.append(core[part])
        start, size = plan.parts[part]
        span = pl.ds(start, size)

        def current(at, span=span):
            index = tuple(at[dim] for dim in "ABC")
            own = grad_ref[(*index, r, span)].astype(FLOAT)
            return own + core_in[(*index, span)].astype(FLOAT)

        state.append((list("ABC"), current))
    flights = [None] * 3

    def launch(part, phase):
        left, current = state[part]
        dim = plan.orders[part][2 - phase]
        staged, received, kept = held_refs[(part * 3 + phase) * 3 : (part * 3 + phase) * 3 + 3]
        others = [other for other in left if other != dim]
        extents = [outer if other == "A" else 2 for other in others]
        started = []
        for number, value in enumerate(peer_values(place, dim, outer)):
            for picks in itertools.product(*[range(extent) for extent in extents]):
                at = dict(zip(others, picks))
                at[dim] = value
                staged[(number, *picks)] = current(at).astype(BRAIN)
            copy = sender.start(
                staged.at[number], received.at[number], moved(place, dim, value)
            )
            started.append(copy)
            pending.append(copy)
        for picks in itertools.product(*[range(extent) for extent in extents]):
            at = dict(zip(others, picks))
            at[dim] = digits[dim]
            kept[picks] = current(at)
        flights[part] = started

        def after(at, kept=kept, received=received, others=tuple(others), count=len(started)):
            index = tuple(at[other] for other in others)
            total = kept[index]
            for number in range(count):
                total = total + received[(number, *index)].astype(FLOAT)
            return total

        state[part] = (others, after)

    for phase in range(3):
        for part in range(3):
            if phase > 0:
                for copy in flights[part]:
                    copy.wait_recv()
            launch(part, phase)
    position_in = lax.broadcasted_iota(jnp.int32, (rows, LANES), 0) * LANES + lane_iota(rows)
    for part in range(3):
        for copy in flights[part]:
            copy.wait_recv()
        start, size = plan.parts[part]
        left, current = state[part]
        rolled[pl.ds(start, size), :] = current({})
    rolled[pl.ds(rows, 8), :] = jnp.zeros((8, LANES), FLOAT)
    shift = lax.rem(LANES - lead, LANES)
    here = pltpu.roll(rolled[pl.ds(0, rows), :], shift, 1)
    below = pltpu.roll(rolled[pl.ds(1, rows), :], shift, 1)
    total = jnp.where(lane_iota(rows) < LANES - lead, here, below)
    total = jnp.where(position_in < plan.length, total, 0.0)
    squares = jnp.sum(total * total)
    lane = lane_iota(8)
    mine[...] = jnp.where(lane == 0, squares, 0.0)
    mine[...] = jnp.where(lane == 1, held_ref[0, 0].astype(FLOAT), mine[...])
    mine[...] = jnp.where(lane == 2, loss_ref[0], mine[...])
    spot = (b * 2 + c) * 2 + r
    near[spot] = mine[...]
    nears = [sender.start(mine, near.at[spot], other) for other in group]
    for copy in nears:
        copy.wait_recv()
    together = near[0]
    for other in range(1, 8):
        together = together + near[other]
    far[a] = together
    rolled[pl.ds(0, 8), :] = together
    fars = [sender.start(rolled.at[pl.ds(0, 8)], far.at[a], other) for other in column]
    for copy in fars:
        copy.wait_recv()
    whole = far[0]
    for other in range(1, outer):
        whole = whole + far[other]
    held = jnp.sum(jnp.where(lane == 1, whole, 0.0)[0:1, :])
    weight_total = held * (0.1 * VIS + (NP - VIS))
    scalars = whole[0:1, :]
    weights = jnp.full((1, LANES), weight_total)
    norms = jnp.sqrt(jnp.full((1, LANES), jnp.sum(jnp.where(lane[0:1] == 0, scalars, 0.0)))) / weights
    losses = jnp.full((1, LANES), jnp.sum(jnp.where(lane[0:1] == 2, scalars, 0.0))) / weights
    scalars_out[...] = jnp.where(lane[0:1] == 0, losses, jnp.where(lane[0:1] == 1, norms, weights))
    total_out[...] = total
    for copy in pending + nears + fars:
        copy.wait_send()


def reduce_grads(held, loss, grads, plan):
    outer, rows = plan.outer, plan.rows
    copies = 3 + 3 * (outer + 1) + 7 + outer - 1
    vmem = pl.BlockSpec(memory_space=pltpu.VMEM)
    smem = pl.BlockSpec(memory_space=pltpu.SMEM)
    return pl.pallas_call(
        functools.partial(reduce_body, plan),
        out_shape=(
            jax.ShapeDtypeStruct((rows, LANES), FLOAT),
            jax.ShapeDtypeStruct((1, LANES), FLOAT),
        ),
        in_specs=[smem, smem, vmem],
        out_specs=(vmem,) * 2,
        scratch_shapes=[
            pltpu.VMEM((outer, 2, 2, rows, LANES), BRAIN),
            pltpu.VMEM((rows + 8, LANES), FLOAT),
            pltpu.VMEM((8, 8, LANES), FLOAT),
            pltpu.VMEM((outer, 8, LANES), FLOAT),
            pltpu.VMEM((8, LANES), FLOAT),
            pltpu.SemaphoreType.DMA((copies,)),
            pltpu.SemaphoreType.DMA((copies,)),
            *reduce_scratch(plan),
        ],
        compiler_params=pltpu.CompilerParams(
            collective_id=1, has_side_effects=True, vmem_limit_bytes=56 << 20
        ),
    )(held, loss, grads)


def update_body(
    plan, step_ref, total_ref, scalars_ref, master_ref, first_ref, second_ref,
    master_out, first_out, second_out, copy_out, loss_out, norm_out, line
):
    rows, length = plan.rows, plan.length
    device = lax.axis_index("dp") * 2 + lax.axis_index("rep")
    position_in = lax.broadcasted_iota(jnp.int32, (rows, LANES), 0) * LANES + lane_iota(rows)
    flat = position_in + device * length
    table = layout()
    early, late = table["enc_ln1g"][0], table["encg"][0]
    rate_part = jnp.where(flat < early, 0.75, jnp.where(flat < late, 0.9, 1.0))
    decay_part = jnp.where(in_segments(flat, matrix_segments()), DECAY, 0.0)
    line[...] = jnp.zeros_like(line)
    line[pl.ds(0, length)] = master_ref[...]
    master = line[...].reshape(rows, LANES)
    line[pl.ds(0, length)] = first_ref[...]
    first = line[...].reshape(rows, LANES)
    line[pl.ds(0, length)] = second_ref[...]
    second = line[...].reshape(rows, LANES)
    loss_out[0, 0] = scalars_ref[0, 0]
    norm_out[0, 0] = scalars_ref[0, 1]
    norms = jnp.full((1, LANES), scalars_ref[0, 1])
    weights = jnp.full((1, LANES), scalars_ref[0, 2])
    gradient = total_ref[...] / weights
    clipped = gradient * jnp.minimum(1.0, CLIP / norms)
    fade = 1.0 / jnp.full((1, LANES), lax.shift_left(1, step_ref[0]).astype(FLOAT))
    new_first = BETA_ONE * first + (1.0 - BETA_ONE) * clipped
    new_second = BETA_TWO * second + (1.0 - BETA_TWO) * clipped * clipped
    first_hat = new_first / (1.0 - fade)
    second_hat = new_second / (1.0 - fade)
    new_master = master - LEARN * rate_part * (
        first_hat / (jnp.sqrt(second_hat) + EPSILON) + decay_part * master
    )
    master_out[...] = new_master.reshape(rows * LANES)[:length]
    first_out[...] = new_first.reshape(rows * LANES)[:length]
    second_out[...] = new_second.reshape(rows * LANES)[:length]
    copy_out[...] = new_master.reshape(rows * LANES)[:length].astype(BRAIN)


def update(step, total, scalars, master, first, second, plan):
    vmem = pl.BlockSpec(memory_space=pltpu.VMEM)
    smem = pl.BlockSpec(memory_space=pltpu.SMEM)
    flat = jax.ShapeDtypeStruct((plan.length,), FLOAT)
    single = jax.ShapeDtypeStruct((1, 1), FLOAT)
    return pl.pallas_call(
        functools.partial(update_body, plan),
        out_shape=(flat, flat, flat, jax.ShapeDtypeStruct((plan.length,), BRAIN), single, single),
        in_specs=[smem, vmem, smem, vmem, vmem, vmem],
        out_specs=(vmem, vmem, vmem, vmem, smem, smem),
        scratch_shapes=[pltpu.VMEM((plan.rows * LANES,), FLOAT)],
        compiler_params=pltpu.CompilerParams(vmem_limit_bytes=16 << 20),
    )(step, total, scalars, master, first, second)


def half_turn(frame, start, rows):
    here = pltpu.roll(frame[pl.ds(start, rows), :], 64, 1)
    below = pltpu.roll(frame[pl.ds(start + 1, rows), :], 64, 1)
    return jnp.where(lane_iota(rows) < 64, here, below)


def assemble(plan, slots, even, odd):
    for index in range(plan.count):
        base, used = plan.base(index), plan.used(index)
        a, rest = divmod(index, 8)
        block = slots[a, rest // 4, rest // 2 % 2, rest % 2].astype(FLOAT)[:used]
        if plan.lead(index):
            before = even[pl.ds(base, 1), :]
            even[pl.ds(base, used), :] = block
            even[pl.ds(base, 1), :] = before + block[0:1]
        else:
            even[pl.ds(base, used), :] = block
    span = 256
    total = (plan.frame_rows - 16) // span

    @pl.loop(0, total)
    def _(step):
        start = pl.multiple_of(step * span, span)
        odd[pl.ds(start, span), :] = half_turn(even, start, span)

    rest = plan.frame_rows - 16 - total * span
    odd[pl.ds(total * span, rest), :] = half_turn(even, total * span, rest)


def read_param(even, odd, name, target):
    offset, shape = layout()[name]
    rows, width = (1, shape[0]) if len(shape) == 1 else shape
    base, late = divmod(offset, LANES)
    frames = (even, odd) if late == 0 else (odd, even)
    whole, half = divmod(width, LANES)
    kind = target.dtype
    if rows == 1:
        for col in range(whole):
            target[:, pl.ds(col * LANES, LANES)] = frames[0][pl.ds(base + col, 1), :].astype(kind)
        if half:
            tail = frames[0][pl.ds(base + whole, 1), :]
            target[:, pl.ds(whole * LANES, half)] = tail[:, :half].astype(kind)
        return
    if not half:
        for col in range(whole):
            piece = frames[0][pl.ds(base + col, rows, stride=whole), :]
            target[:, pl.ds(col * LANES, LANES)] = piece.astype(kind)
        return
    stride = 2 * width // LANES
    shift = whole + (1 if late else 0)

    def interleave(scratch):
        for col in range(whole + 1):
            size = LANES if col < whole else half
            upper = frames[0][pl.ds(base + col, rows // 2, stride=stride), :]
            lower = frames[1][pl.ds(base + shift + col, rows // 2, stride=stride), :]
            scratch[pl.ds(0, rows // 2, stride=2), :] = upper
            scratch[pl.ds(1, rows // 2, stride=2), :] = lower
            target[:, pl.ds(col * LANES, size)] = scratch[...][:, :size].astype(kind)

    pl.run_scoped(interleave, pltpu.VMEM((rows, LANES), FLOAT))


def write_grad(even, odd, name, value):
    offset, shape = layout()[name]
    rows, width = (1, shape[0]) if len(shape) == 1 else shape
    base, late = divmod(offset, LANES)
    frames = (even, odd) if late == 0 else (odd, even)
    whole, half = divmod(width, LANES)

    def columns():
        for col in range(0, whole, 2):
            size = min(2, whole - col) * LANES
            both = value(col * LANES, size)
            for part in range(size // LANES):
                yield col + part, both[:, part * LANES : (part + 1) * LANES]
        if half:
            tail = value(whole * LANES, half)
            yield whole, jnp.concatenate([tail, jnp.zeros((rows, LANES - half), FLOAT)], axis=1)

    if rows == 1:
        for col, piece in columns():
            frames[0][pl.ds(base + col, 1), :] = piece
        return
    if not half:
        for col, piece in columns():
            frames[0][pl.ds(base + col, rows, stride=whole), :] = piece
        return
    stride = 2 * width // LANES
    shift = whole + (1 if late else 0)

    def interleave(scratch):
        for col, piece in columns():
            scratch[...] = piece
            upper = scratch[pl.ds(0, rows // 2, stride=2), :]
            lower = scratch[pl.ds(1, rows // 2, stride=2), :]
            frames[0][pl.ds(base + col, rows // 2, stride=stride), :] = upper
            frames[1][pl.ds(base + shift + col, rows // 2, stride=stride), :] = lower

    pl.run_scoped(interleave, pltpu.VMEM((rows, LANES), FLOAT))


def emit_slots(plan, even, odd, slots):
    for index in range(plan.count):
        base, used = plan.base(index), plan.used(index)
        a, rest = divmod(index, 8)
        spot = (a, rest // 4, rest // 2 % 2, rest % 2)
        here = pltpu.roll(odd[pl.ds(base + 8, plan.rows), :], 64, 1)
        above = pltpu.roll(odd[pl.ds(base + 7, plan.rows), :], 64, 1)
        late = jnp.where(lane_iota(plan.rows) < 64, above, here)
        slots[spot] = (even[pl.ds(base, plan.rows), :] + late).astype(BRAIN)


def dot(left, right, dims=(((1,), (0,)), ((), ()))):
    return lax.dot_general(left, right, dims, preferred_element_type=FLOAT)


def place_table(count, rows, width):
    quarter = width // 4
    omega = 1.0 / 10000.0 ** (np.arange(quarter) / quarter)
    index = np.arange(count)
    across = (index // GRID)[:, None] * omega
    along = (index % GRID)[:, None] * omega
    table = np.zeros((rows, width), np.float32)
    table[:count] = np.concatenate(
        [np.sin(across), np.cos(across), np.sin(along), np.cos(along)], axis=-1
    )
    return table


def split_two(value):
    upper = value.astype(BRAIN)
    return upper, (value - upper.astype(FLOAT)).astype(BRAIN)


def norm_parts(value):
    center = value - jnp.mean(value, axis=-1, keepdims=True)
    spread = lax.rsqrt(jnp.mean(center * center, axis=-1, keepdims=True) + LN_EPS)
    return center * spread, spread


def norm_back(grad, value, gain):
    unit, spread = norm_parts(value)
    d_gain = jnp.sum(grad * unit, axis=0, keepdims=True)
    d_shift = jnp.sum(grad, axis=0, keepdims=True)
    scaled = grad * gain
    middle = jnp.mean(scaled, axis=-1, keepdims=True)
    along = jnp.mean(scaled * unit, axis=-1, keepdims=True)
    return spread * (scaled - middle - unit * along), d_gain, d_shift


def gelu_parts(value):
    half = 0.5 + 0.5 * lax.erf(value * 0.7071067811865476)
    bell = jnp.exp2(value * value * (-0.5 * LOG_TWO_E)) * 0.3989422804014327
    return value * half, half + value * bell


def head_only(value, head, size):
    lane = lax.broadcasted_iota(jnp.int32, value.shape, 1)
    inside = (lane >= head * size) & (lane < (head + 1) * size)
    return jnp.where(inside, value, jnp.zeros_like(value))


def attend(t_ref, chance_ref, usable, width, heads):
    size = width // heads
    query, keys = t_ref[:, pl.ds(0, width)], t_ref[:, pl.ds(width, width)]
    values = t_ref[:, pl.ds(2 * width, width)].T
    factor = size ** (-0.5) * LOG_TWO_E
    mixed = []
    for head in range(heads):
        raw = dot(head_only(keys, head, size), query, PAIR)
        raw = jnp.where(usable, raw, -1e30)
        top = jnp.max(raw, axis=0, keepdims=True)
        power = jnp.exp2((raw - top) * factor)
        chance = power * (1.0 / jnp.sum(power, axis=0, keepdims=True))
        chance_ref[head] = chance
        mixed.append(dot(values[head * size : (head + 1) * size], chance.astype(BRAIN)))
    return jnp.concatenate(mixed, axis=0).astype(BRAIN).T


def attend_back(d_mixed, t_ref, dt_ref, chance_ref, width, heads):
    size = width // heads
    scale = size ** (-0.5)
    query, keys = t_ref[:, pl.ds(0, width)], t_ref[:, pl.ds(width, width)]
    values = t_ref[:, pl.ds(2 * width, width)]
    across = keys.T
    d_query = []
    d_keys = d_values = None
    for head in range(heads):
        chance = chance_ref[head]
        d_here = head_only(d_mixed, head, size)
        d_chance = dot(head_only(values, head, size), d_mixed, PAIR)
        along = jnp.sum(chance * d_chance, axis=0, keepdims=True)
        d_scores = (chance * (d_chance - along)).astype(BRAIN)
        part = dot(chance.astype(BRAIN), d_here)
        d_values = part if d_values is None else d_values + part
        part = dot(d_scores, head_only(query, head, size))
        d_keys = part if d_keys is None else d_keys + part
        d_query.append(dot(across[head * size : (head + 1) * size], d_scores))
    d_query = (jnp.concatenate(d_query, axis=0) * scale).astype(BRAIN).T
    dt_ref[:, pl.ds(0, width)] = d_query
    dt_ref[:, pl.ds(width, width)] = (d_keys * scale).astype(BRAIN)
    dt_ref[:, pl.ds(2 * width, width)] = d_values.astype(BRAIN)


class Weights:
    def __init__(self, refs):
        self.refs = dict(zip(layout(), refs))

    def __call__(self, name):
        return self.refs[name][...]


def block_ahead(hidden, keep, weights, prefix, heads, usable):
    width = hidden.shape[1]
    keep["x"][...] = hidden
    unit, unused = norm_parts(hidden)
    normed = (unit * weights(prefix + "ln1g") + weights(prefix + "ln1b")).astype(BRAIN)
    keep["a"][...] = normed
    bias = weights(prefix + "qvb")
    t_ref = keep["t"]
    for part in range(3):
        cols = pl.ds(part * width, width)
        value = dot(normed, weights.refs[prefix + "qkv"][:, cols])
        if part != 1:
            value = value + bias[:, (part // 2) * width : (part // 2 + 1) * width]
        t_ref[:, cols] = value.astype(BRAIN)
    mixed = attend(t_ref, keep["p"], usable, width, heads)
    keep["o"][...] = mixed
    middle = hidden + (dot(mixed, weights(prefix + "proj")) + weights(prefix + "projb"))
    keep["m"][...] = middle
    unit, unused = norm_parts(middle)
    second = (unit * weights(prefix + "ln2g") + weights(prefix + "ln2b")).astype(BRAIN)
    keep["b"][...] = second
    inner = dot(second, weights(prefix + "fc1")) + weights(prefix + "fc1b")
    active, slope = gelu_parts(inner)
    keep["s"][...] = slope
    keep["g"][...] = active.astype(BRAIN)
    return middle + (dot(keep["g"][...], weights(prefix + "fc2")) + weights(prefix + "fc2b"))


def block_home(grad, keep, weights, prefix, heads, sums):
    width = grad.shape[1]
    d_branch = grad.astype(BRAIN)
    keep["dz"][...] = d_branch
    d_inner = (dot(d_branch, weights(prefix + "fc2"), PAIR) * keep["s"][...]).astype(BRAIN)
    keep["du"][...] = d_inner
    d_second = dot(d_inner, weights(prefix + "fc1"), PAIR)
    d_middle, d_gain, d_shift = norm_back(d_second, keep["m"][...], weights(prefix + "ln2g"))
    sums(prefix + "ln2g", d_gain)
    sums(prefix + "ln2b", d_shift)
    d_middle = d_middle + grad
    d_output = d_middle.astype(BRAIN)
    keep["dy"][...] = d_output
    d_mixed = dot(d_output, weights(prefix + "proj"), PAIR).astype(BRAIN)
    attend_back(d_mixed, keep["t"], keep["dt"], keep["p"], width, heads)
    d_normed = dot(keep["dt"][...], weights(prefix + "qkv"), PAIR)
    d_hidden, d_gain, d_shift = norm_back(d_normed, keep["x"][...], weights(prefix + "ln1g"))
    sums(prefix + "ln1g", d_gain)
    sums(prefix + "ln1b", d_shift)
    return d_middle + d_hidden


def kept_shapes(count, rows, width, hidden, heads):
    return {
        "x": (False, (rows, width), FLOAT),
        "a": (True, (rows, width), BRAIN),
        "t": (False, (rows, 3 * width), BRAIN),
        "p": (False, (heads, rows, rows), FLOAT),
        "o": (True, (rows, width), BRAIN),
        "m": (False, (rows, width), FLOAT),
        "b": (True, (rows, width), BRAIN),
        "s": (False, (rows, hidden), FLOAT),
        "g": (True, (rows, hidden), BRAIN),
        "dz": (True, (rows, width), BRAIN),
        "du": (True, (rows, hidden), BRAIN),
        "dy": (True, (rows, width), BRAIN),
        "dt": (True, (rows, 3 * width), BRAIN),
    }


def kept_scratch(count, rows, width, hidden, heads):
    shapes = []
    for every, shape, kind in kept_shapes(count, rows, width, hidden, heads).values():
        shapes.append(pltpu.VMEM(((count,) + shape) if every and count > 1 else shape, kind))
    return shapes


def kept_view(refs, count, rows, width, hidden, heads, image=None):
    view = {}
    table = kept_shapes(count, rows, width, hidden, heads)
    for ref, (name, (every, shape, kind)) in zip(refs, table.items()):
        view[name] = ref.at[image] if every and count > 1 and image is not None else ref
    return view


def block_grads(keep, prefix, emit):
    def rows_of(name):
        value = keep[name][...]
        return value.reshape(-1, value.shape[-1])

    for left, right, name, bias in (
        ("g", "dz", "fc2", "fc2b"),
        ("b", "du", "fc1", "fc1b"),
        ("o", "dy", "proj", "projb"),
        ("a", "dt", "qkv", "qvb"),
    ):
        emit(prefix + name, prefix + bias, rows_of(left), rows_of(right))


def step_body(plan, counts_ref, slots, seen_ref, tgt_ref, meta_ref, spot_enc, spot_dec, grad_out, loss_out, *scratch):
    names = list(layout())
    even, odd, sums_ref, y_hi, y_lo, dy_home, final_all, dpred_all = scratch[:8]
    weights = Weights(scratch[8 : 8 + len(names)])
    enc_refs = scratch[8 + len(names) : 8 + len(names) + 13]
    dec_refs = scratch[8 + len(names) + 13 :]
    assemble(plan, slots, even, odd)
    for name in names:
        read_param(even, odd, name, weights.refs[name])
    even[...] = jnp.zeros_like(even)
    odd[...] = jnp.zeros_like(odd)
    view = odd.at[pl.ds(8, plan.frame_rows)]
    sums_ref[...] = jnp.zeros_like(sums_ref)
    order = {name: number for number, name in enumerate(names)}

    def add_sum(name, value):
        sums_ref[pl.ds(order[name], 1), pl.ds(0, value.shape[1])] += value

    spot = lax.rem(lax.axis_index("dp"), 4)
    own = counts_ref[0, 0]
    lane = lane_iota(8)
    row = lax.broadcasted_iota(jnp.int32, (8, LANES), 0)

    def count_of(hub):
        return jnp.sum(jnp.where((lane == 127) & (row == 0), meta_ref[hub], 0.0)).astype(jnp.int32)

    one, two = count_of(1), count_of(2)
    from_one = jnp.where(spot == 0, 3, jnp.where(spot == 2, 4, 5))
    from_two = jnp.where(spot == 0, 3, jnp.where(spot == 1, 4, 5))
    use_one = (spot == 2) | ((spot != 1) & (one > 2))
    third = jnp.where(own > 2, 2, jnp.where(use_one, 3, 4))
    third_row = jnp.where(own > 2, 2, jnp.where(use_one, from_one, from_two))
    third_count = jnp.where(own > 2, own, jnp.where(use_one, one, two))
    third_meta = jnp.where(own > 2, 0, jnp.where(use_one, 1, 2))

    def pick(image):
        last = image == 2
        source = jnp.where(last, third, image)
        line = jnp.where(last, third_row, image)
        live = jnp.where(last, third_count, own) > line
        kept = meta_ref[jnp.where(last, third_meta, 0), pl.ds(line, 1), :][:, :HOME]
        return source, kept, live.astype(FLOAT)

    def placement(kept):
        number = lax.broadcasted_iota(jnp.int32, (ROWS, HOME), 0).astype(FLOAT)
        return (number == kept).astype(FLOAT)

    visible, begin = [], []
    for image in range(LIVE_CAP):
        source, kept, live = pick(image)
        where = placement(kept).astype(BRAIN)
        visible.append(seen_ref[source])
        begin.append(dot(where, spot_enc[0], DEEP) + dot(where, spot_enc[1], DEEP))
    visible = jnp.concatenate(visible, axis=0)
    begin = jnp.concatenate(begin, axis=0)
    enc_rows = LIVE_CAP * HOME
    enc_shape = (1, enc_rows, D, FF, HEADS)
    enc = kept_view(enc_refs, *enc_shape)
    down = lax.broadcasted_iota(jnp.int32, (enc_rows, enc_rows), 0)
    over = lax.broadcasted_iota(jnp.int32, (enc_rows, enc_rows), 1)
    usable = (down // HOME == over // HOME) & (down % HOME < VIS)
    first_in = dot(visible, weights("patch")) + weights("patchb") + begin
    encoded = block_ahead(first_in, enc, weights, "enc_", HEADS, usable)
    unit, unused = norm_parts(encoded)
    encoder_out = (unit * weights("encg") + weights("encb")).astype(BRAIN)
    embedded = dot(encoder_out, weights("embed")) + weights("embedb")
    upper, lower = split_two(embedded)
    for image in range(LIVE_CAP):
        y_hi[image] = upper[image * HOME : (image + 1) * HOME]
        y_lo[image] = lower[image * HOME : (image + 1) * HOME]
    dec_shape = (LIVE_CAP, ROWS, E, DFF, DHEADS)
    real = lax.broadcasted_iota(jnp.int32, (ROWS, 1), 0) < NP
    usable_dec = lax.broadcasted_iota(jnp.int32, (ROWS, ROWS), 0) < NP

    def one_image(image, total):
        source, kept, live = pick(image)
        where = placement(kept)
        seen = jnp.sum(where, axis=1, keepdims=True)
        where = where.astype(BRAIN)
        grid_in = dot(where, y_hi[image]) + dot(where, y_lo[image])
        grid_in = grid_in + (1.0 - seen) * weights("mask") + spot_dec[...]
        keep = kept_view(dec_refs, *dec_shape, image)
        decoded = block_ahead(grid_in, keep, weights, "dec_", DHEADS, usable_dec)
        unit, unused = norm_parts(decoded)
        final = (unit * weights("decg") + weights("decb")).astype(BRAIN)
        final_all[image] = final
        predicted = dot(final, weights("head")) + weights("headb")
        weight = jnp.where(real, (1.0 - 0.9 * seen) * live, 0.0)
        error = predicted[:NP] - tgt_ref[source].astype(FLOAT)
        weighted = error * weight[:NP]
        total = total + jnp.sum(weighted * error, axis=0, keepdims=True)
        dpred_all[image, pl.ds(0, NP)] = (weighted * (2.0 / PIX)).astype(BRAIN)
        dpred_all[image, pl.ds(NP, ROWS - NP)] = jnp.zeros((ROWS - NP, PIX), BRAIN)
        d_final = dot(dpred_all[image], weights("head"), PAIR)
        d_decoded, d_gain, d_shift = norm_back(d_final, decoded, weights("decg"))
        add_sum("decg", d_gain)
        add_sum("decb", d_shift)
        d_grid = block_home(d_decoded, keep, weights, "dec_", DHEADS, add_sum)
        add_sum("mask", jnp.sum((1.0 - seen) * d_grid, axis=0, keepdims=True))
        dy_home[image] = dot(where, d_grid.astype(BRAIN), DEEP).astype(BRAIN)
        return total

    total = lax.fori_loop(0, LIVE_CAP, one_image, jnp.zeros((1, PIX), FLOAT))
    loss_out[0] = jnp.sum(total) * (1.0 / PIX)

    def emit(name, bias, left, right):
        ones = jnp.ones((16, right.shape[0]), BRAIN)
        summed = dot(ones, right)[0:1]
        if bias.endswith("qvb"):
            width = summed.shape[1] // 3
            summed = jnp.concatenate([summed[:, :width], summed[:, 2 * width :]], axis=1)
        write_grad(even, view, bias, lambda start, size: summed[:, start : start + size])
        turned = left.T
        write_grad(even, view, name, lambda start, size: dot(turned, right[:, start : start + size]))

    d_embedded = dy_home[...].reshape(enc_rows, E)
    emit("embed", "embedb", encoder_out, d_embedded)
    d_seen = dot(d_embedded, weights("embed"), PAIR).astype(BRAIN).astype(FLOAT)
    d_encoded, d_gain, d_shift = norm_back(d_seen, encoded, weights("encg"))
    add_sum("encg", d_gain)
    add_sum("encb", d_shift)
    d_first = block_home(d_encoded, enc, weights, "enc_", HEADS, add_sum).astype(BRAIN)
    emit("patch", "patchb", visible, d_first)
    block_grads(enc, "enc_", emit)
    block_grads(kept_view(dec_refs, *dec_shape), "dec_", emit)
    emit("head", "headb", final_all[...].reshape(-1, E), dpred_all[...].reshape(-1, PIX))
    for name, (offset, shape) in layout().items():
        if name[-4:] in ("ln1g", "ln1b", "ln2g", "ln2b", "encg", "encb", "decg", "decb", "mask"):
            write_grad(
                even,
                view,
                name,
                lambda start, size, name=name: sums_ref[pl.ds(order[name], 1), pl.ds(start, size)],
            )
    emit_slots(plan, even, odd, grad_out)


def weight_scratch():
    shapes = []
    for name, (offset, shape) in layout().items():
        if len(shape) == 1:
            shapes.append(pltpu.VMEM((1, *shape), FLOAT))
        else:
            shapes.append(pltpu.VMEM(shape, BRAIN))
    return shapes


def local_step(counts, slots, seen, targets, meta, plan):
    vmem = pl.BlockSpec(memory_space=pltpu.VMEM)
    smem = pl.BlockSpec(memory_space=pltpu.SMEM)
    table = place_table(NP, ROWS, D)
    upper = table.astype(BRAIN)
    spot_enc = jnp.asarray(np.stack([upper, (table - upper.astype(np.float32)).astype(BRAIN)]))
    spot_dec = jnp.asarray(place_table(NP, ROWS, E))
    return pl.pallas_call(
        functools.partial(step_body, plan),
        out_shape=(
            jax.ShapeDtypeStruct((plan.outer, 2, 2, 2, plan.rows, LANES), BRAIN),
            jax.ShapeDtypeStruct((1,), FLOAT),
        ),
        in_specs=[smem] + [vmem] * 6,
        out_specs=(vmem, smem),
        scratch_shapes=[
            pltpu.VMEM((plan.frame_rows, LANES), FLOAT),
            pltpu.VMEM((plan.frame_rows + 8, LANES), FLOAT),
            pltpu.VMEM((48, E), FLOAT),
            pltpu.VMEM((LIVE_CAP, HOME, E), BRAIN),
            pltpu.VMEM((LIVE_CAP, HOME, E), BRAIN),
            pltpu.VMEM((LIVE_CAP, HOME, E), BRAIN),
            pltpu.VMEM((LIVE_CAP, ROWS, E), BRAIN),
            pltpu.VMEM((LIVE_CAP, ROWS, PIX), BRAIN),
            *weight_scratch(),
            *kept_scratch(1, LIVE_CAP * HOME, D, FF, HEADS),
            *kept_scratch(LIVE_CAP, ROWS, E, DFF, DHEADS),
        ],
        compiler_params=pltpu.CompilerParams(vmem_limit_bytes=58 << 20),
    )(counts, slots, seen, targets, meta, spot_enc, spot_dec)


def on_device(patches, targets, keep, counts, step, master, first, second):
    plan = Plan(master.shape[0], lax.axis_size(("dp", "rep")))
    slots, seen, wanted, meta = gather_params(counts, keep, master, patches, targets, plan)
    grads, loss = local_step(counts, slots, seen, wanted, meta, plan)
    total, scalars = reduce_grads(counts, loss, grads, plan)
    outs = update(step, total, scalars, master, first, second, plan)
    return (*outs[:4], outs[4].reshape(()), outs[5].reshape(()))


def solution(mesh):
    return jax.shard_map(
        on_device,
        mesh=mesh,
        in_specs=(
            P(("dp", "rep"), None, None),
            P(("dp", "rep"), None, None),
            P(("dp", "rep"), None),
            P("dp", "rep"),
            P(),
            P(("dp", "rep")),
            P(("dp", "rep")),
            P(("dp", "rep")),
        ),
        out_specs=(
            P(("dp", "rep")),
            P(("dp", "rep")),
            P(("dp", "rep")),
            P(("dp", "rep")),
            P(),
            P(),
        ),
        check_vma=False,
    )
```

profile of v0, /device:TPU:0, one launch (start us, length us, event | category | flops | bytes accessed | tf_op | source)
XLA Modules:
  0.0 139.9 jit_solution(9192606433038039779)
XLA Ops:
  1.3 0.0 copy-start.1
  1.3 1.5 %copy-done.1 = bf16[6,196,768]{2,1,0:T(8,128)(2,1)S(1)} copy-done((bf16[6,196,768]{2,1,0:T(8,128)(2,1)S(1)}, bf16[6,196,768]{2,1,0:T(8,128)(2,1)}, u32[]{:S(2)}) %copy-start.1) | copy-done | bytes 1806360
  2.8 0.0 copy-start.2
  2.8 1.5 %copy-done.2 = bf16[6,196,768]{2,1,0:T(8,128)(2,1)S(1)} copy-done((bf16[6,196,768]{2,1,0:T(8,128)(2,1)S(1)}, bf16[6,196,768]{2,1,0:T(8,128)(2,1)}, u32[]{:S(2)}) %copy-start.2) | copy-done | bytes 1806360
  4.3 0.0 copy-start.4
  4.3 0.9 copy-done.4
  5.2 0.0 copy-start.11
  5.2 0.7 copy-done.11
  5.9 39.1 %shard_map.145 = (bf16[4,2,2,2,400,128]{5,4,3,2,1,0:T(8,128)(2,1)S(1)}, bf16[5,64,768]{2,1,0:T(8,128)(2,1)S(1)}, bf16[5,196,768]{2,1,0:T(8,128)(2,1)S(1)}, f32[3,8,128]{2,1,0:T(8,128)S(1)}) custom-call(s32[1,1]{1,0:T(1,128)S(6)} %copy.16.counts_ref.held_ref, s32[6,49]{1,0:T(8,128)S(1)} %copy-done.11, f32[50930]{0:T(1024)S(1)} %copy-done.4, ...), custom_call_target="tpu_custom_call" | custom-call | tf_op jit(solution)/shard_map/pallas_call | solution.py:319
  45.0 0.0 copy-start
  45.0 1.7 %copy-done = bf16[4,2,2,2,400,128]{5,4,3,2,1,0:T(8,128)(2,1)} copy-done((bf16[4,2,2,2,400,128]{5,4,3,2,1,0:T(8,128)(2,1)}, bf16[4,2,2,2,400,128]{5,4,3,2,1,0:T(8,128)(2,1)S(1)}, u32[]{:S(2)}) %copy-start) | copy-done | bytes 3276824
  46.7 0.0 copy-start.3
  46.7 1.1 copy-done.3
  47.9 0.0 copy-start.6
  47.9 0.9 copy-done.6
  48.7 0.0 copy-start.10
  48.7 0.6 copy-done.10
  49.3 46.1 %shard_map.146 = (bf16[4,2,2,2,400,128]{5,4,3,2,1,0:T(8,128)(2,1)}, f32[1]{0:T(128)}) custom-call(s32[1,1]{1,0:T(1,128)S(6)} %copy.16.counts_ref.held_ref, bf16[4,2,2,2,400,128]{5,4,3,2,1,0:T(8,128)(2,1)} %copy-done, bf16[5,64,768]{2,1,0:T(8,128)(2,1)} %copy-done.6, bf16[5,196,768]{2,1,0:T(8,128)(2,1)} %copy-done.3, f32[3,8,128]{2,1,0:T(8,128)} %copy-done.10, ...), custom_call_target="tpu_custom_call" | custom-call | tf_op jit(solution)/shard_map/pallas_call | solution.py:1054
  95.4 0.0 copy-start.5
  95.5 0.0 copy-start.7
  95.5 0.0 copy-start.8
  95.5 39.9 %shard_map.147 = (f32[400,128]{1,0:T(8,128)}, f32[1,128]{1,0:T(1,128)}) custom-call(s32[1,1]{1,0:T(1,128)S(6)} %copy.16.counts_ref.held_ref, f32[1]{0:T(128)} %get-tuple-element.24.loss_ref, bf16[4,2,2,2,400,128]{5,4,3,2,1,0:T(8,128)(2,1)} %get-tuple-element.25.grad_ref), custom_call_target="tpu_custom_call" | custom-call | tf_op jit(solution)/shard_map/pallas_call | solution.py:512
  136.0 0.0 copy-done.5
  136.0 0.0 copy-done.7
  136.0 0.0 copy-done.8
  136.0 0.0 copy-start.9
  136.0 0.9 copy-done.9
  137.0 0.0 copy-start.12
  137.0 0.6 copy-done.12
  137.5 2.2 %shard_map.148 = (f32[50930]{0:T(1024)}, f32[50930]{0:T(1024)}, f32[50930]{0:T(1024)}, bf16[50930]{0:T(1024)(128)(2,1)}, f32[1,1]{1,0:T(1,128)}, /*index=5*/f32[1,1]{1,0:T(1,128)}) custom-call(s32[1]{0:T(128)S(6)} %copy.17.step_ref, f32[400,128]{1,0:T(8,128)S(1)} %copy-done.9, f32[1,128]{1,0:T(1,128)S(1)} %copy-done.12, f32[50930]{0:T(1024)S(1)} %copy-done.5, ...), custom_call_target="tpu_custom_call" | custom-call | tf_op jit(solution)/shard_map/pallas_call | solution.py:580
Async XLA Ops:
  1.3 1.5 %copy-start.1 = (bf16[6,196,768]{2,1,0:T(8,128)(2,1)S(1)}, bf16[6,196,768]{2,1,0:T(8,128)(2,1)}, u32[]{:S(2)}) copy-start(bf16[6,196,768]{2,1,0:T(8,128)(2,1)} %patches_ref.1) | copy-start | bytes 5419012
  2.8 1.5 %copy-start.2 = (bf16[6,196,768]{2,1,0:T(8,128)(2,1)S(1)}, bf16[6,196,768]{2,1,0:T(8,128)(2,1)}, u32[]{:S(2)}) copy-start(bf16[6,196,768]{2,1,0:T(8,128)(2,1)} %targets_ref.1) | copy-start | bytes 5419012
  4.3 0.9 copy-start.4
  5.2 0.7 copy-start.11
  45.0 1.7 %copy-start = (bf16[4,2,2,2,400,128]{5,4,3,2,1,0:T(8,128)(2,1)}, bf16[4,2,2,2,400,128]{5,4,3,2,1,0:T(8,128)(2,1)S(1)}, u32[]{:S(2)}) copy-start(bf16[4,2,2,2,400,128]{5,4,3,2,1,0:T(8,128)(2,1)S(1)} %get-tuple-element.20.slots) | copy-start | bytes 9830404
  46.7 1.1 copy-start.3
  47.9 0.9 copy-start.6
  48.7 0.6 copy-start.10
  95.4 40.6 %copy-start.5 = (f32[50930]{0:T(1024)S(1)}, f32[50930]{0:T(1024)}, u32[]{:S(2)}) copy-start(f32[50930]{0:T(1024)} %master_ref.1) | copy-start | bytes 611164
  95.5 40.6 %copy-start.7 = (f32[50930]{0:T(1024)S(1)}, f32[50930]{0:T(1024)}, u32[]{:S(2)}) copy-start(f32[50930]{0:T(1024)} %first_ref.1) | copy-start | bytes 611164
  95.5 40.5 %copy-start.8 = (f32[50930]{0:T(1024)S(1)}, f32[50930]{0:T(1024)}, u32[]{:S(2)}) copy-start(f32[50930]{0:T(1024)} %second_ref.1) | copy-start | bytes 611164
  136.0 0.9 copy-start.9
  137.0 0.6 copy-start.12
where the time goes:
time: 140 us
  Pallas kernels  127 us (91%)
  local copies, waits for them, and re-layouts  10.4 us (7%)
  between operations  2.19 us (2%)
    pallas_call x1, Pallas kernels, local_step(): pl.pallas_call(functools.partial(step_body, plan), out_shape=(jax.ShapeDt...  46.1 us
    pallas_call x1, Pallas kernels, reduce_grads(): pl.pallas_call(functools.partial(reduce_body, plan), out_shape=(jax.Shape...  39.9 us
    pallas_call x1, Pallas kernels, gather_params(): pl.pallas_call(functools.partial(gather_body, plan), out_shape=(jax.Shape...  39.1 us
    unnamed x26, local copies, waits for them, and re-layouts  10.4 us

commit v1 on v0

--- a/solution.py
+++ b/solution.py
@@ -148,12 +148,13 @@
     pl.semaphore_wait(barrier, len(places))
 
 
-def neighbours(place, outer):
-    found = []
-    for dim in "ABCr":
-        for value in peer_values(place, dim, outer):
-            found.append(moved(place, dim, value))
-    return found
+def partners(place, outer):
+    a, b, c, r = (place[dim] for dim in "ABCr")
+    group = [
+        {"A": a, "B": (b + k // 4) % 2, "C": (c + k // 2 % 2) % 2, "r": (r + k % 2) % 2}
+        for k in range(1, 8)
+    ]
+    return group, [moved(place, "A", value) for value in peer_values(place, "A", outer)]
 
 
 class Sender:
@@ -209,7 +210,8 @@
     rolled[pl.ds(8, rows), :] = turned
     block = jnp.where(lane_iota(rows) >= lead, turned, rolled[pl.ds(7, rows), :])
     out_ref[a, b, c, r] = block.astype(BRAIN)
-    meet(neighbours(place, outer) + [moved(moved(place, "B", 1 - b), "C", 1 - c)])
+    group, column = partners(place, outer)
+    meet(group + column)
     sender = Sender(send, recv)
     everything = []
 
@@ -310,39 +312,6 @@
     target_copy.wait()
 
 
-def gather_params(counts, keep, master, patches, targets, plan):
-    outer, rows = plan.outer, plan.rows
-    copies = 3 * (outer + 1 + outer + 2)
-    vmem = pl.BlockSpec(memory_space=pltpu.VMEM)
-    smem = pl.BlockSpec(memory_space=pltpu.SMEM)
-    far = pl.BlockSpec(memory_space=pl.ANY)
-    return pl.pallas_call(
-        functools.partial(gather_body, plan),
-        out_shape=(
-            jax.ShapeDtypeStruct((outer, 2, 2, 2, rows, LANES), BRAIN),
-            jax.ShapeDtypeStruct((5, HOME, PIX), BRAIN),
-            jax.ShapeDtypeStruct((5, NP, PIX), BRAIN),
-            jax.ShapeDtypeStruct((3, 8, LANES), FLOAT),
-        ),
-        in_specs=[smem, vmem, vmem, far, far],
-        out_specs=(vmem,) * 4,
-        scratch_shapes=[
-            pltpu.VMEM((rows * LANES,), FLOAT),
-            pltpu.VMEM((rows + 8, LANES), FLOAT),
-            pltpu.VMEM(patches.shape, BRAIN),
-            pltpu.VMEM((3, HOME, PIX), BRAIN),
-            pltpu.SemaphoreType.DMA((copies,)),
-            pltpu.SemaphoreType.DMA((copies,)),
-            pltpu.SemaphoreType.DMA((2,)),
-            pltpu.SemaphoreType.DMA((2, 3, 3)),
-            pltpu.SemaphoreType.DMA((2, 3)),
-        ],
-        compiler_params=pltpu.CompilerParams(
-            collective_id=0, has_side_effects=True, vmem_limit_bytes=40 << 20
-        ),
-    )(counts, keep, master, patches, targets)
-
-
 def reduce_scratch(plan):
     shapes = []
     for part in range(3):
@@ -386,12 +355,7 @@
     digits = {"A": a, "B": b, "C": c}
     device = ((a * 2 + b) * 2 + c) * 2 + r
     lead = lax.rem(device * plan.length, LANES)
-    group = [
-        {"A": a, "B": (b + k // 4) % 2, "C": (c + k // 2 % 2) % 2, "r": (r + k % 2) % 2}
-        for k in range(1, 8)
-    ]
-    column = [moved(place, "A", value) for value in peer_values(place, "A", outer)]
-    meet(group + column)
+    group, column = partners(place, outer)
     sender = Sender(send, recv)
     sibling = moved(place, "r", 1 - r)
     pending = []
@@ -504,35 +468,6 @@
         copy.wait_send()
 
 
-def reduce_grads(held, loss, grads, plan):
-    outer, rows = plan.outer, plan.rows
-    copies = 3 + 3 * (outer + 1) + 7 + outer - 1
-    vmem = pl.BlockSpec(memory_space=pltpu.VMEM)
-    smem = pl.BlockSpec(memory_space=pltpu.SMEM)
-    return pl.pallas_call(
-        functools.partial(reduce_body, plan),
-        out_shape=(
-            jax.ShapeDtypeStruct((rows, LANES), FLOAT),
-            jax.ShapeDtypeStruct((1, LANES), FLOAT),
-        ),
-        in_specs=[smem, smem, vmem],
-        out_specs=(vmem,) * 2,
-        scratch_shapes=[
-            pltpu.VMEM((outer, 2, 2, rows, LANES), BRAIN),
-            pltpu.VMEM((rows + 8, LANES), FLOAT),
-            pltpu.VMEM((8, 8, LANES), FLOAT),
-            pltpu.VMEM((outer, 8, LANES), FLOAT),
-            pltpu.VMEM((8, LANES), FLOAT),
-            pltpu.SemaphoreType.DMA((copies,)),
-            pltpu.SemaphoreType.DMA((copies,)),
-            *reduce_scratch(plan),
-        ],
-        compiler_params=pltpu.CompilerParams(
-            collective_id=1, has_side_effects=True, vmem_limit_bytes=56 << 20
-        ),
-    )(held, loss, grads)
-
-
 def update_body(
     plan, step_ref, total_ref, scalars_ref, master_ref, first_ref, second_ref,
     master_out, first_out, second_out, copy_out, loss_out, norm_out, line
@@ -1044,22 +979,76 @@
     return shapes
 
 
-def local_step(counts, slots, seen, targets, meta, plan):
+def whole_body(
+    plan, counts_ref, keep_ref, x_ref, patches_ref, targets_ref, enc_table, dec_table,
+    total_out, scalars_out, *scratch
+):
+    scratch = list(scratch)
+
+    def take(count):
+        taken = scratch[:count]
+        del scratch[:count]
+        return taken
+
+    (slots, seen, tgt, meta, grad, loss, spot_enc, spot_dec, tables) = take(9)
+    copies = [
+        pltpu.make_async_copy(enc_table, spot_enc, tables.at[0]),
+        pltpu.make_async_copy(dec_table, spot_dec, tables.at[1]),
+    ]
+    for copy in copies:
+        copy.start()
+    gather_body(
+        plan, counts_ref, keep_ref, x_ref, patches_ref, targets_ref, slots, seen, tgt, meta, *take(9)
+    )
+    for copy in copies:
+        copy.wait()
+    names = len(layout())
+    step_body(
+        plan, counts_ref, slots, seen, tgt, meta, spot_enc, spot_dec, grad, loss, *take(8 + names + 26)
+    )
+    reduce_body(plan, counts_ref, loss, grad, total_out, scalars_out, *scratch)
+
+
+def whole_step(counts, keep, master, patches, targets, plan):
+    outer, rows = plan.outer, plan.rows
     vmem = pl.BlockSpec(memory_space=pltpu.VMEM)
     smem = pl.BlockSpec(memory_space=pltpu.SMEM)
+    far = pl.BlockSpec(memory_space=pl.ANY)
     table = place_table(NP, ROWS, D)
     upper = table.astype(BRAIN)
     spot_enc = jnp.asarray(np.stack([upper, (table - upper.astype(np.float32)).astype(BRAIN)]))
     spot_dec = jnp.asarray(place_table(NP, ROWS, E))
+    block = pltpu.VMEM((outer, 2, 2, 2, rows, LANES), BRAIN)
+    out_copies = 3 * (outer + 1 + outer + 2)
+    home_copies = 3 + 3 * (outer + 1) + 7 + outer - 1
+    dma = pltpu.SemaphoreType.DMA
     return pl.pallas_call(
-        functools.partial(step_body, plan),
+        functools.partial(whole_body, plan),
         out_shape=(
-            jax.ShapeDtypeStruct((plan.outer, 2, 2, 2, plan.rows, LANES), BRAIN),
-            jax.ShapeDtypeStruct((1,), FLOAT),
+            jax.ShapeDtypeStruct((rows, LANES), FLOAT),
+            jax.ShapeDtypeStruct((1, LANES), FLOAT),
         ),
-        in_specs=[smem] + [vmem] * 6,
-        out_specs=(vmem, smem),
+        in_specs=[smem, vmem, vmem, far, far, far, far],
+        out_specs=(vmem, vmem),
         scratch_shapes=[
+            block,
+            pltpu.VMEM((5, HOME, PIX), BRAIN),
+            pltpu.VMEM((5, NP, PIX), BRAIN),
+            pltpu.VMEM((3, 8, LANES), FLOAT),
+            block,
+            pltpu.SMEM((1,), FLOAT),
+            pltpu.VMEM(spot_enc.shape, BRAIN),
+            pltpu.VMEM(spot_dec.shape, FLOAT),
+            dma((2,)),
+            pltpu.VMEM((rows * LANES,), FLOAT),
+            pltpu.VMEM((rows + 8, LANES), FLOAT),
+            pltpu.VMEM(patches.shape, BRAIN),
+            pltpu.VMEM((3, HOME, PIX), BRAIN),
+            dma((out_copies,)),
+            dma((out_copies,)),
+            dma((2,)),
+            dma((2, 3, 3)),
+            dma((2, 3)),
             pltpu.VMEM((plan.frame_rows, LANES), FLOAT),
             pltpu.VMEM((plan.frame_rows + 8, LANES), FLOAT),
             pltpu.VMEM((48, E), FLOAT),
@@ -1071,16 +1060,24 @@
             *weight_scratch(),
             *kept_scratch(1, LIVE_CAP * HOME, D, FF, HEADS),
             *kept_scratch(LIVE_CAP, ROWS, E, DFF, DHEADS),
+            pltpu.VMEM((outer, 2, 2, rows, LANES), BRAIN),
+            pltpu.VMEM((rows + 8, LANES), FLOAT),
+            pltpu.VMEM((8, 8, LANES), FLOAT),
+            pltpu.VMEM((outer, 8, LANES), FLOAT),
+            pltpu.VMEM((8, LANES), FLOAT),
+            dma((home_copies,)),
+            dma((home_copies,)),
+            *reduce_scratch(plan),
         ],
-        compiler_params=pltpu.CompilerParams(vmem_limit_bytes=58 << 20),
-    )(counts, slots, seen, targets, meta, spot_enc, spot_dec)
+        compiler_params=pltpu.CompilerParams(
+            collective_id=0, has_side_effects=True, vmem_limit_bytes=60 << 20
+        ),
+    )(counts, keep, master, patches, targets, spot_enc, spot_dec)
 
 
 def on_device(patches, targets, keep, counts, step, master, first, second):
     plan = Plan(master.shape[0], lax.axis_size(("dp", "rep")))
-    slots, seen, wanted, meta = gather_params(counts, keep, master, patches, targets, plan)
-    grads, loss = local_step(counts, slots, seen, wanted, meta, plan)
-    total, scalars = reduce_grads(counts, loss, grads, plan)
+    total, scalars = whole_step(counts, keep, master, patches, targets, plan)
     outs = update(step, total, scalars, master, first, second, plan)
     return (*outs[:4], outs[4].reshape(()), outs[5].reshape(()))
 

time: 140 us -> 124 us (0.89)
  local copies, waits for them, and re-layouts: 10.4 us -> 1.61 us
  Pallas kernels: 127 us -> 120 us
    unnamed x26 -> x10, local copies, waits for them, and re-layouts: 10.4 us -> 1.61 us
    pallas_call x3 -> x1, Pallas kernels: 125 us -> 117 us  [whole_step(): pl.pallas_call(functools.partial(whole_body, plan), out_shape=(jax.ShapeD...]
where the time goes in v1:
time: 124 us; the launch traced here: 123 us
  Pallas kernels  120 us (97%)
  between operations  2.15 us (2%)
  local copies, waits for them, and re-layouts  1.61 us (1%)
    pallas_call x1, Pallas kernels, whole_step(): pl.pallas_call(functools.partial(whole_body, plan), out_shape=(jax.ShapeD...  117 us

profile of v1, /device:TPU:0, one launch (start us, length us, event | category | flops | bytes accessed | tf_op | source)
XLA Modules:
  0.0 123.3 jit_solution(15103128425161445393)
XLA Ops:
  1.9 0.0 copy-start
  1.9 0.0 copy-start.1
  1.9 0.0 copy-start.2
  2.0 117.4 %shard_map.145 = (f32[400,128]{1,0:T(8,128)}, f32[1,128]{1,0:T(1,128)}) custom-call(s32[1,1]{1,0:T(1,128)S(6)} %copy.16.counts_ref, s32[6,49]{1,0:T(8,128)} %keep_ref.1, f32[50930]{0:T(1024)} %master_ref.1, bf16[6,196,768]{2,1,0:T(8,128)(2,1)} %patches_ref.1, bf16[6,196,768]{2,1,0:T(8,128)(2,1)} %targets_ref.1, ...), custom_call_target="tpu_custom_call" | custom-call | tf_op jit(solution)/shard_map/pallas_call | solution.py:1025
  119.3 0.0 copy-done
  119.3 0.0 copy-done.1
  119.3 0.0 copy-done.2
  119.3 0.0 copy-start.3
  119.4 0.9 copy-done.3
  120.3 0.0 copy-start.4
  120.3 0.7 copy-done.4
  121.0 2.2 %shard_map.146 = (f32[50930]{0:T(1024)}, f32[50930]{0:T(1024)}, f32[50930]{0:T(1024)}, bf16[50930]{0:T(1024)(128)(2,1)}, f32[1,1]{1,0:T(1,128)}, /*index=5*/f32[1,1]{1,0:T(1,128)}) custom-call(s32[1]{0:T(128)S(6)} %copy.17.step_ref, f32[400,128]{1,0:T(8,128)S(1)} %copy-done.3, f32[1,128]{1,0:T(1,128)S(1)} %copy-done.4, f32[50930]{0:T(1024)S(1)} %copy-done, ...), custom_call_target="tpu_custom_call" | custom-call | tf_op jit(solution)/shard_map/pallas_call | solution.py:515
Async XLA Ops:
  1.9 117.4 %copy-start = (f32[50930]{0:T(1024)S(1)}, f32[50930]{0:T(1024)}, u32[]{:S(2)}) copy-start(f32[50930]{0:T(1024)} %master_ref.1) | copy-start | bytes 611164
  1.9 117.4 %copy-start.1 = (f32[50930]{0:T(1024)S(1)}, f32[50930]{0:T(1024)}, u32[]{:S(2)}) copy-start(f32[50930]{0:T(1024)} %first_ref.1) | copy-start | bytes 611164
  1.9 117.4 %copy-start.2 = (f32[50930]{0:T(1024)S(1)}, f32[50930]{0:T(1024)}, u32[]{:S(2)}) copy-start(f32[50930]{0:T(1024)} %second_ref.1) | copy-start | bytes 611164
  119.3 0.9 copy-start.3
  120.3 0.7 copy-start.4

commit v2 on v1

--- a/solution.py
+++ b/solution.py
@@ -93,34 +93,60 @@
     def __init__(self, length, count):
         self.length = length
         self.count = count
-        self.outer = count // 8
-        self.rows = -(-((LANES - 1 + length + LANES - 1) // LANES) // 16) * 16
-        units = self.rows // 16
-        first = max(1, min(round(0.389 * units), (units - 1) // 2))
-        sizes = (first * 16, first * 16, self.rows - 2 * first * 16)
-        starts = (0, sizes[0], sizes[0] + sizes[1])
-        self.parts = tuple(zip(starts, sizes))
-        self.orders = ("ACB", "ABC", "CBA")
-        self.frame_rows = -(-(length * count) // LANES // 8 * 8) + 64
+        self.outer = count // 16
+        self.lines = -(-length // LANES // 8 * 8)
+        self.rows = -(-(7 + (2 * LANES - 2 + length) // LANES) // 16) * 16
+        self.split = layout()["embed"][0]
+        if self.outer > 2:
+            self.parts, self.orders = ((0, self.rows),), ("LCB",)
+        else:
+            units = self.rows // 16
+            first, second = round(0.385 * units), round(0.346 * units)
+            sizes = (first * 16, second * 16, (units - first - second) * 16)
+            self.parts = ((0, sizes[0]), (sizes[0], sizes[1]), (sizes[0] + sizes[1], sizes[2]))
+            self.orders = ("LCB", "BLC", "CBL")
+        self.first_late = -(-self.split // length)
+        self.edge = -(-self.split // (16 * length))
+        last = self.first_late - 1
+        self.border = (self.base(last) + self.used(last) + 1 + 7) // 8 * 8 + 8
+        self.frame_rows = (length * count // LANES + 7) // 8 * 8 + self.rows + 16
+
+    def late(self, index):
+        return index >= self.first_late
+
+    def start(self, index):
+        return index * self.length - (64 if self.late(index) else 0)
 
     def base(self, index):
-        return index * self.length // LANES
+        return self.start(index) // LANES
 
     def lead(self, index):
-        return index * self.length % LANES
+        return self.start(index) % LANES
 
     def used(self, index):
         return (self.lead(index) + self.length + LANES - 1) // LANES
+
+    def own(self, index):
+        start = index * self.length - jnp.where(index >= self.first_late, 64, 0)
+        return lax.rem(lax.div(start, LANES), 8), lax.rem(start, LANES)
+
+
+def spot_of(index):
+    return (index // 16, index // 8 % 2, index // 4 % 2, index // 2 % 2, index % 2)
 
 
 def position():
     chip = lax.axis_index("dp")
     core = lax.axis_index("rep")
-    return {"A": chip // 4, "B": chip // 2 % 2, "C": chip % 2, "r": core}
+    return {"H": chip // 8, "L": chip // 4 % 2, "B": chip // 2 % 2, "C": chip % 2, "r": core}
+
+
+def index_of(place):
+    return (((place["H"] * 2 + place["L"]) * 2 + place["B"]) * 2 + place["C"]) * 2 + place["r"]
 
 
 def device_of(place):
-    return (place["A"] * 4 + place["B"] * 2 + place["C"], place["r"])
+    return (((place["H"] * 2 + place["L"]) * 2 + place["B"]) * 2 + place["C"], place["r"])
 
 
 def moved(place, dim, value):
@@ -129,16 +155,11 @@
     return changed
 
 
-def peer_values(place, dim, outer):
-    if dim == "A":
-        return [lax.rem(place["A"] + step, outer) for step in range(1, outer)]
-    return [1 - place[dim]]
-
-
-def source_values(place, dim, outer):
-    if dim == "A":
-        return [lax.rem(place["A"] + outer - step, outer) for step in range(1, outer)]
-    return [1 - place[dim]]
+def flipped(place, dims):
+    changed = dict(place)
+    for dim in dims:
+        changed[dim] = 1 - place[dim]
+    return changed
 
 
 def meet(places):
@@ -149,12 +170,22 @@
 
 
 def partners(place, outer):
-    a, b, c, r = (place[dim] for dim in "ABCr")
-    group = [
-        {"A": a, "B": (b + k // 4) % 2, "C": (c + k // 2 % 2) % 2, "r": (r + k % 2) % 2}
-        for k in range(1, 8)
-    ]
-    return group, [moved(place, "A", value) for value in peer_values(place, "A", outer)]
+    group = []
+    for number in range(1, 16):
+        dims = [dim for bit, dim in enumerate("rCBL") if number >> bit & 1]
+        group.append(flipped(place, dims))
+    column = [moved(place, "H", lax.rem(place["H"] + step, outer)) for step in range(1, outer)]
+    return group, column
+
+
+def branches(order):
+    nodes = []
+    for count in range(len(order) + 1):
+        for dims in itertools.combinations(order, count):
+            reach = max([order.index(dim) for dim in dims], default=-1)
+            nodes.append((reach, count, "".join(dims), order[reach + 1 :]))
+    nodes.sort(key=lambda node: node[:2])
+    return [(dims, onward) for reach, count, dims, onward in nodes]
 
 
 class Sender:
@@ -186,145 +217,317 @@
     return [spot for spot in range(4) if spot != hub]
 
 
-def gather_body(
-    plan, counts_ref, keep_ref, x_ref, patches_ref, targets_ref,
-    out_ref, seen_ref, tgt_ref, meta_ref,
-    line, rolled, pixels, spare, send, recv, local, hand, taken
-):
-    outer, rows = plan.outer, plan.rows
-    place = position()
-    a, b, c, r = (place[dim] for dim in "ABCr")
-    spot = b * 2 + c
-    pixel_copy = pltpu.make_async_copy(patches_ref, pixels, local.at[0])
-    pixel_copy.start()
-    target_copy = pltpu.make_async_copy(
-        targets_ref.at[pl.ds(0, LIVE_CAP)], tgt_ref.at[pl.ds(0, LIVE_CAP)], local.at[1]
-    )
-    target_copy.start()
-    index = ((a * 2 + b) * 2 + c) * 2 + r
-    lead = lax.rem(index * plan.length, LANES)
+def hand_over(place, hub, number, pairs, hand, taken):
+    other = others_of(hub)[number]
+    target = {**place, "B": other // 2, "C": other % 2}
+    return [
+        pltpu.make_async_remote_copy(
+            src_ref=source,
+            dst_ref=to,
+            send_sem=hand.at[hub - 1, number, kind],
+            recv_sem=taken.at[hub - 1, kind],
+            device_id=device_of(target),
+            device_id_type=MESH,
+        )
+        for kind, (source, to) in pairs.items()
+    ]
+
+
+class Handing:
+    def __init__(self, place, spare, seen_ref, meta_ref, targets_ref, tgt_ref, hand, taken):
+        self.place, self.hand, self.taken = place, hand, taken
+        self.spot = place["B"] * 2 + place["C"]
+        self.refs = (spare, seen_ref, meta_ref, targets_ref, tgt_ref)
+
+    def copies(self, hub, number, kinds):
+        spare, seen_ref, meta_ref, targets_ref, tgt_ref = self.refs
+        pairs = {
+            0: (spare.at[number], seen_ref.at[2 + hub]),
+            1: (meta_ref.at[0], meta_ref.at[hub]),
+            2: (targets_ref.at[3 + number], tgt_ref.at[hub]),
+        }
+        pairs = {kind: pairs[kind] for kind in kinds}
+        return hand_over(self.place, hub, number, pairs, self.hand, self.taken)
+
+    def on_hub(self, act):
+        for hub in HUBS:
+
+            @pl.when(self.spot == hub)
+            def _(hub=hub):
+                act(hub)
+
+    def start(self, kinds):
+        def act(hub):
+            for number in range(3):
+                for copy in self.copies(hub, number, kinds):
+                    copy.start()
+
+        self.on_hub(act)
+
+    def receive(self, kinds):
+        for hub in HUBS:
+
+            @pl.when(self.spot != hub)
+            def _(hub=hub):
+                for copy in self.copies(hub, 0, kinds):
+                    copy.wait_recv()
+
+    def finish(self, kinds):
+        def act(hub):
+            for number in range(3):
+                for copy in self.copies(hub, number, kinds):
+                    copy.wait_send()
+
+        self.on_hub(act)
+
+
+def own_block(plan, device, x_ref, line, rolled):
+    rows, lines = plan.rows, plan.lines
+    skip, lead = plan.own(device)
     line[...] = jnp.zeros_like(line)
     line[pl.ds(0, plan.length)] = x_ref[...]
-    turned = pltpu.roll(line[...].reshape(rows, LANES), lead, 1)
-    rolled[pl.ds(0, 8), :] = jnp.zeros((8, LANES), FLOAT)
-    rolled[pl.ds(8, rows), :] = turned
-    block = jnp.where(lane_iota(rows) >= lead, turned, rolled[pl.ds(7, rows), :])
-    out_ref[a, b, c, r] = block.astype(BRAIN)
+    turned = pltpu.roll(line[...].reshape(lines, LANES), lead, 1)
+    rolled[...] = jnp.zeros_like(rolled)
+    rolled[pl.ds(8 + skip, lines), :] = turned
+    upper, lower = rolled[pl.ds(8, rows), :], rolled[pl.ds(7, rows), :]
+    return jnp.where(lane_iota(rows) >= lead, upper, lower).astype(BRAIN)
+
+
+def gather_body(plan, place, out_ref, sender, between):
+    outer = plan.outer
+    high = place["H"]
+    sibling = flipped(place, "r")
+    count = len(plan.parts)
+
+    def region(value, part, fixed, free=""):
+        start, size = plan.parts[part]
+        index = [value]
+        for dim in "LBC":
+            if dim in free:
+                index.append(pl.ds(0, 2))
+            else:
+                index.append(1 - place[dim] if dim in fixed else place[dim])
+        return out_ref.at[(*index, place["r"], pl.ds(start, size))]
+
+    column = []
+    for part in range(count):
+        for step in range(1, outer):
+            source = region(high, part, "")
+            target = moved(place, "H", lax.rem(high + step, outer))
+            column.append((step, part, sender.start(source, source, target)))
+    flights, onwards, siblings = {}, [], []
+
+    values = [lax.rem(high + outer - step, outer) for step in range(outer)]
+
+    def spread(number, part, dims, onward):
+        for dim in onward:
+            source = region(values[number], part, dims)
+            copy = sender.start(source, source, flipped(place, dim))
+            flights[number, part, frozenset(dims + dim)] = copy
+            onwards.append(copy)
+
+    for number in range(outer):
+        for part in range(count):
+            if number > 0:
+                for step, which, copy in column:
+                    if step == number and which == part:
+                        copy.wait_recv()
+            spread(number, part, "", plan.orders[part])
+        between(number)
+    trees = [branches(order) for order in plan.orders]
+    for place_in_tree in range(len(trees[0])):
+        for number, value in enumerate(values):
+            for part in range(count):
+                dims, onward = trees[part][place_in_tree]
+                order = plan.orders[part]
+                if dims:
+                    flights[number, part, frozenset(dims)].wait_recv()
+                    spread(number, part, dims, onward)
+                reach = order.index(dims[-1]) if dims else -1
+                if place_in_tree + 1 == len(trees[0]) or (
+                    order.index(trees[part][place_in_tree + 1][0][-1]) > reach
+                ):
+                    fixed = order[reach] if dims else ""
+                    source = region(value, part, fixed, order[: max(reach, 0)])
+                    siblings.append(sender.start(source, source, sibling))
+        between(outer + place_in_tree)
+    for copy in siblings:
+        copy.wait_recv()
+    return [copy for step, part, copy in column] + onwards + siblings
+
+
+class Reducer:
+    def __init__(self, plan, place, grad_ref, core_in, tree_in, column_in, own_ref, sender, columns):
+        self.plan, self.place, self.sender = plan, place, sender
+        self.grad_ref, self.core_in, self.tree_in = grad_ref, core_in, tree_in
+        self.column_in, self.own_ref, self.columns = column_in, own_ref, columns
+        self.cores = {}
+        self.pending = []
+        self.trees = [branches(order) for order in plan.orders]
+        self.flights = {}
+
+    def share(self, value):
+        place = self.place
+        for part, (start, size) in enumerate(self.plan.parts):
+            whole = (value, pl.ds(0, 2), pl.ds(0, 2), pl.ds(0, 2))
+            span = pl.ds(start, size)
+            copy = self.sender.start(
+                self.grad_ref.at[(*whole, 1 - place["r"], span)],
+                self.core_in.at[(*whole, span)],
+                flipped(place, "r"),
+            )
+            self.cores[value, part] = copy
+            self.pending.append(copy)
+
+    def stage(self, value, reach):
+        plan, place = self.plan, self.place
+        steps = []
+        for part in range(len(plan.parts)):
+            order = plan.orders[part]
+            nodes = [
+                (dims, onward)
+                for dims, onward in reversed(self.trees[part])
+                if (order.index(dims[-1]) if dims else -1) == reach
+            ]
+            steps.append([(part, *node) for node in nodes])
+        for group in zip(*steps):
+            for part, dims, onward in group:
+                self.node(value, part, dims, onward)
+
+    def node(self, value, part, dims, onward):
+        plan, place = self.plan, self.place
+        start, size = plan.parts[part]
+        span = pl.ds(start, size)
+        if (value, part) in self.cores:
+            self.cores.pop((value, part)).wait_recv()
+        for dim in onward:
+            self.flights.pop((value, part, frozenset(dims + dim))).wait_recv()
+        index = [value] + [1 - place[dim] if dim in dims else place[dim] for dim in "LBC"]
+        total = self.grad_ref[(*index, place["r"], span)].astype(FLOAT)
+        total = total + self.core_in[(*index, span)].astype(FLOAT)
+        order = plan.orders[part]
+
+        def number(dims):
+            return sum(1 << "LBC".index(dim) for dim in dims)
+
+        for dim in onward:
+            total = total + self.tree_in[value, number(dims + dim), span].astype(FLOAT)
+        mine = self.grad_ref.at[(*index, place["r"], span)]
+        if dims:
+            mine[...] = total.astype(BRAIN)
+            copy = self.sender.start(
+                mine, self.tree_in.at[value, number(dims), span], flipped(place, dims[-1])
+            )
+            self.flights[value, part, frozenset(dims)] = copy
+            self.pending.append(copy)
+            return
+        high = place["H"]
+
+        @pl.when(high == value)
+        def _():
+            self.own_ref[span, :] = total
+
+        @pl.when(high != value)
+        def _():
+            mine[...] = total.astype(BRAIN)
+            self.column(value, part).start()
+
+    def column(self, value, part):
+        plan, place = self.plan, self.place
+        start, size = plan.parts[part]
+        send, recv = self.columns
+        index = (value, place["L"], place["B"], place["C"], place["r"], pl.ds(start, size))
+        return pltpu.make_async_remote_copy(
+            src_ref=self.grad_ref.at[index],
+            dst_ref=self.column_in.at[place["H"], pl.ds(start, size)],
+            send_sem=send.at[value, part],
+            recv_sem=recv.at[place["H"], part],
+            device_id=device_of(moved(place, "H", value)),
+            device_id_type=MESH,
+        )
+
+    def arrival(self, source, part):
+        plan, place = self.plan, self.place
+        start, size = plan.parts[part]
+        send, recv = self.columns
+        return pltpu.make_async_remote_copy(
+            src_ref=self.own_in(part),
+            dst_ref=self.column_in.at[source, pl.ds(start, size)],
+            send_sem=send.at[source, part],
+            recv_sem=recv.at[source, part],
+            device_id=device_of(moved(place, "H", source)),
+            device_id_type=MESH,
+        )
+
+    def own_in(self, part):
+        place = self.place
+        start, size = self.plan.parts[part]
+        index = (0, place["L"], place["B"], place["C"], place["r"], pl.ds(start, size))
+        return self.grad_ref.at[index]
+
+    def finish(self):
+        plan, place = self.plan, self.place
+        for part, (start, size) in enumerate(plan.parts):
+            for source in range(plan.outer):
+
+                @pl.when(place["H"] != source)
+                def _(part=part, source=source, start=start, size=size):
+                    self.arrival(source, part).wait_recv()
+                    span = pl.ds(start, size)
+                    self.own_ref[span, :] += self.column_in[source, span].astype(FLOAT)
+
+    def close(self):
+        plan, place = self.plan, self.place
+        for copy in self.pending:
+            copy.wait_send()
+        for part in range(len(plan.parts)):
+            for value in range(plan.outer):
+
+                @pl.when(place["H"] != value)
+                def _(part=part, value=value):
+                    self.column(value, part).wait_send()
+
+
+def finish_body(plan, place, held_ref, loss_ref, own_ref, total_out, scalars_out, turned, near, far, mine, sender):
+    outer, rows, lines = plan.outer, plan.rows, plan.lines
     group, column = partners(place, outer)
-    meet(group + column)
-    sender = Sender(send, recv)
-    everything = []
-
-    def region(part, whole, fixed):
-        start, size = plan.parts[part]
-        index = []
-        for dim, extent in (("A", outer), ("B", 2), ("C", 2)):
-            if dim in fixed:
-                index.append(fixed[dim])
-            else:
-                index.append(pl.ds(0, extent) if dim in whole else place[dim])
-        return out_ref.at[(*index, r, pl.ds(start, size))]
-
-    def hand_over(hub, number):
-        other = others_of(hub)[number]
-        target = {"A": a, "B": other // 2, "C": other % 2, "r": r}
-        pairs = (
-            (spare.at[number], seen_ref.at[2 + hub]),
-            (meta_ref.at[0], meta_ref.at[hub]),
-            (targets_ref.at[3 + number], tgt_ref.at[2 + hub]),
-        )
-        return [
-            pltpu.make_async_remote_copy(
-                src_ref=source,
-                dst_ref=to,
-                send_sem=hand.at[hub - 1, number, kind],
-                recv_sem=taken.at[hub - 1, kind],
-                device_id=device_of(target),
-                device_id_type=MESH,
-            )
-            for kind, (source, to) in enumerate(pairs)
-        ]
-
-    fresh = [(part, "", [{}]) for part in range(3)]
-    sibling = moved(place, "r", 1 - r)
-    for phase in range(4):
-        flights = []
-        if phase < 3:
-            for part in range(3):
-                order = plan.orders[part]
-                dim = order[phase]
-                source = region(part, order[:phase], {})
-                for value in peer_values(place, dim, outer):
-                    flights.append(sender.start(source, source, moved(place, dim, value)))
-        for part, whole, news in fresh:
-            for fixed in news:
-                source = region(part, whole, fixed)
-                everything.append(sender.start(source, source, sibling))
-        fresh = []
-        if phase < 3:
-            for part in range(3):
-                order = plan.orders[part]
-                dim = order[phase]
-                news = [{dim: value} for value in source_values(place, dim, outer)]
-                fresh.append((part, order[:phase], news))
-        if phase == 0:
-            lane = lane_iota(8)
-            row = lax.broadcasted_iota(jnp.int32, (8, LANES), 0)
-            mine = jnp.where((lane == LANES - 1) & (row == 0), counts_ref[0, 0].astype(FLOAT), -1.0)
-            meta_ref[0] = mine
-            meta_ref[0, pl.ds(0, keep_ref.shape[0]), pl.ds(0, VIS)] = keep_ref[...].astype(FLOAT)
-            pixel_copy.wait()
-
-            def visible(image):
-                number = lax.broadcasted_iota(jnp.int32, (NP, HOME), 0).astype(FLOAT)
-                where = (number == meta_ref[0, pl.ds(image, 1), :][:, :HOME]).astype(BRAIN)
-                return dot(where, pixels[image], DEEP).astype(BRAIN)
-
-            for hub in HUBS:
-
-                @pl.when(spot == hub)
-                def _(hub=hub):
-                    for number in range(3):
-                        spare[number] = visible(3 + number)
-                    for number in range(3):
-                        for copy in hand_over(hub, number):
-                            copy.start()
-
-            for image in range(LIVE_CAP):
-                seen_ref[image] = visible(image)
-        for copy in flights:
-            copy.wait()
-    for copy in everything:
-        copy.wait()
-    for hub in HUBS:
-
-        @pl.when(spot == hub)
-        def _(hub=hub):
-            for number in range(3):
-                for copy in hand_over(hub, number):
-                    copy.wait_send()
-
-        @pl.when(spot != hub)
-        def _(hub=hub):
-            for copy in hand_over(hub, 0):
-                copy.wait_recv()
-
-    target_copy.wait()
-
-
-def reduce_scratch(plan):
-    shapes = []
-    for part in range(3):
-        size = plan.parts[part][1]
-        left = list("ABC")
-        for dim in reversed(plan.orders[part]):
-            left.remove(dim)
-            others = tuple(plan.outer if other == "A" else 2 for other in left)
-            peers = plan.outer - 1 if dim == "A" else 1
-            shapes.append(pltpu.VMEM((peers, *others, size, LANES), BRAIN))
-            shapes.append(pltpu.VMEM((peers, *others, size, LANES), BRAIN))
-            shapes.append(pltpu.VMEM((*others, size, LANES), FLOAT))
-    return shapes
+    skip, lead = plan.own(index_of(place))
+    position_in = lax.broadcasted_iota(jnp.int32, (lines, LANES), 0) * LANES + lane_iota(lines)
+    shift = lax.rem(LANES - lead, LANES)
+    turned[pl.ds(0, rows), :] = pltpu.roll(own_ref[...], shift, 1)
+    here, below = turned[pl.ds(skip, lines), :], turned[pl.ds(skip + 1, lines), :]
+    total = jnp.where(lane_iota(lines) < LANES - lead, here, below)
+    total = jnp.where(position_in < plan.length, total, 0.0)
+    squares = jnp.sum(total * total)
+    lane = lane_iota(8)
+    stats = jnp.where(lane == 0, squares, 0.0)
+    stats = jnp.where(lane == 1, held_ref[0, 0].astype(FLOAT), stats)
+    mine[0] = jnp.where(lane == 2, loss_ref[0], stats)
+    spot = ((place["L"] * 2 + place["B"]) * 2 + place["C"]) * 2 + place["r"]
+    near[spot] = mine[0]
+    nears = [sender.start(mine.at[0], near.at[spot], other) for other in group]
+    total_out[...] = total
+    for copy in nears:
+        copy.wait_recv()
+    together = near[0]
+    for other in range(1, 16):
+        together = together + near[other]
+    far[place["H"]] = together
+    mine[1] = together
+    fars = [sender.start(mine.at[1], far.at[place["H"]], other) for other in column]
+    for copy in fars:
+        copy.wait_recv()
+    whole = far[0]
+    for other in range(1, outer):
+        whole = whole + far[other]
+    row = whole[0:1, :]
+    lane = lane[0:1]
+    held = jnp.sum(jnp.where(lane == 1, row, 0.0))
+    weights = jnp.full((1, LANES), held * (0.1 * VIS + (NP - VIS)))
+    norms = jnp.sqrt(jnp.full((1, LANES), jnp.sum(jnp.where(lane == 0, row, 0.0)))) / weights
+    losses = jnp.full((1, LANES), jnp.sum(jnp.where(lane == 2, row, 0.0))) / weights
+    scalars_out[...] = jnp.where(lane == 0, losses, jnp.where(lane == 1, norms, weights))
+    return nears + fars
 
 
 def in_segments(index, segments):
@@ -344,135 +547,11 @@
     return found
 
 
-def reduce_body(
-    plan, held_ref, loss_ref, grad_ref, total_out, scalars_out, *scratch
-):
-    outer, rows = plan.outer, plan.rows
-    core_in, rolled, near, far, mine, send, recv = scratch[:7]
-    held_refs = scratch[7:]
-    place = position()
-    a, b, c, r = (place[dim] for dim in "ABCr")
-    digits = {"A": a, "B": b, "C": c}
-    device = ((a * 2 + b) * 2 + c) * 2 + r
-    lead = lax.rem(device * plan.length, LANES)
-    group, column = partners(place, outer)
-    sender = Sender(send, recv)
-    sibling = moved(place, "r", 1 - r)
-    pending = []
-    core = []
-    for part in range(3):
-        start, size = plan.parts[part]
-        span = pl.ds(start, size)
-        full = (pl.ds(0, outer), pl.ds(0, 2), pl.ds(0, 2))
-        core.append(
-            sender.start(
-                grad_ref.at[(*full, 1 - r, span)], core_in.at[(*full, span)], sibling
-            )
-        )
-    state = []
-    for part in range(3):
-        core[part].wait_recv()
-        pending.append(core[part])
-        start, size = plan.parts[part]
-        span = pl.ds(start, size)
-
-        def current(at, span=span):
-            index = tuple(at[dim] for dim in "ABC")
-            own = grad_ref[(*index, r, span)].astype(FLOAT)
-            return own + core_in[(*index, span)].astype(FLOAT)
-
-        state.append((list("ABC"), current))
-    flights = [None] * 3
-
-    def launch(part, phase):
-        left, current = state[part]
-        dim = plan.orders[part][2 - phase]
-        staged, received, kept = held_refs[(part * 3 + phase) * 3 : (part * 3 + phase) * 3 + 3]
-        others = [other for other in left if other != dim]
-        extents = [outer if other == "A" else 2 for other in others]
-        started = []
-        for number, value in enumerate(peer_values(place, dim, outer)):
-            for picks in itertools.product(*[range(extent) for extent in extents]):
-                at = dict(zip(others, picks))
-                at[dim] = value
-                staged[(number, *picks)] = current(at).astype(BRAIN)
-            copy = sender.start(
-                staged.at[number], received.at[number], moved(place, dim, value)
-            )
-            started.append(copy)
-            pending.append(copy)
-        for picks in itertools.product(*[range(extent) for extent in extents]):
-            at = dict(zip(others, picks))
-            at[dim] = digits[dim]
-            kept[picks] = current(at)
-        flights[part] = started
-
-        def after(at, kept=kept, received=received, others=tuple(others), count=len(started)):
-            index = tuple(at[other] for other in others)
-            total = kept[index]
-            for number in range(count):
-                total = total + received[(number, *index)].astype(FLOAT)
-            return total
-
-        state[part] = (others, after)
-
-    for phase in range(3):
-        for part in range(3):
-            if phase > 0:
-                for copy in flights[part]:
-                    copy.wait_recv()
-            launch(part, phase)
-    position_in = lax.broadcasted_iota(jnp.int32, (rows, LANES), 0) * LANES + lane_iota(rows)
-    for part in range(3):
-        for copy in flights[part]:
-            copy.wait_recv()
-        start, size = plan.parts[part]
-        left, current = state[part]
-        rolled[pl.ds(start, size), :] = current({})
-    rolled[pl.ds(rows, 8), :] = jnp.zeros((8, LANES), FLOAT)
-    shift = lax.rem(LANES - lead, LANES)
-    here = pltpu.roll(rolled[pl.ds(0, rows), :], shift, 1)
-    below = pltpu.roll(rolled[pl.ds(1, rows), :], shift, 1)
-    total = jnp.where(lane_iota(rows) < LANES - lead, here, below)
-    total = jnp.where(position_in < plan.length, total, 0.0)
-    squares = jnp.sum(total * total)
-    lane = lane_iota(8)
-    mine[...] = jnp.where(lane == 0, squares, 0.0)
-    mine[...] = jnp.where(lane == 1, held_ref[0, 0].astype(FLOAT), mine[...])
-    mine[...] = jnp.where(lane == 2, loss_ref[0], mine[...])
-    spot = (b * 2 + c) * 2 + r
-    near[spot] = mine[...]
-    nears = [sender.start(mine, near.at[spot], other) for other in group]
-    for copy in nears:
-        copy.wait_recv()
-    together = near[0]
-    for other in range(1, 8):
-        together = together + near[other]
-    far[a] = together
-    rolled[pl.ds(0, 8), :] = together
-    fars = [sender.start(rolled.at[pl.ds(0, 8)], far.at[a], other) for other in column]
-    for copy in fars:
-        copy.wait_recv()
-    whole = far[0]
-    for other in range(1, outer):
-        whole = whole + far[other]
-    held = jnp.sum(jnp.where(lane == 1, whole, 0.0)[0:1, :])
-    weight_total = held * (0.1 * VIS + (NP - VIS))
-    scalars = whole[0:1, :]
-    weights = jnp.full((1, LANES), weight_total)
-    norms = jnp.sqrt(jnp.full((1, LANES), jnp.sum(jnp.where(lane[0:1] == 0, scalars, 0.0)))) / weights
-    losses = jnp.full((1, LANES), jnp.sum(jnp.where(lane[0:1] == 2, scalars, 0.0))) / weights
-    scalars_out[...] = jnp.where(lane[0:1] == 0, losses, jnp.where(lane[0:1] == 1, norms, weights))
-    total_out[...] = total
-    for copy in pending + nears + fars:
-        copy.wait_send()
-
-
 def update_body(
     plan, step_ref, total_ref, scalars_ref, master_ref, first_ref, second_ref,
     master_out, first_out, second_out, copy_out, loss_out, norm_out, line
 ):
-    rows, length = plan.rows, plan.length
+    rows, length = plan.lines, plan.length
     device = lax.axis_index("dp") * 2 + lax.axis_index("rep")
     position_in = lax.broadcasted_iota(jnp.int32, (rows, LANES), 0) * LANES + lane_iota(rows)
     flat = position_in + device * length
@@ -517,38 +596,45 @@
         out_shape=(flat, flat, flat, jax.ShapeDtypeStruct((plan.length,), BRAIN), single, single),
         in_specs=[smem, vmem, smem, vmem, vmem, vmem],
         out_specs=(vmem, vmem, vmem, vmem, smem, smem),
-        scratch_shapes=[pltpu.VMEM((plan.rows * LANES,), FLOAT)],
+        scratch_shapes=[pltpu.VMEM((plan.lines * LANES,), FLOAT)],
         compiler_params=pltpu.CompilerParams(vmem_limit_bytes=16 << 20),
     )(step, total, scalars, master, first, second)
 
 
-def half_turn(frame, start, rows):
-    here = pltpu.roll(frame[pl.ds(start, rows), :], 64, 1)
-    below = pltpu.roll(frame[pl.ds(start + 1, rows), :], 64, 1)
-    return jnp.where(lane_iota(rows) < 64, here, below)
-
-
 def assemble(plan, slots, even, odd):
+    filled = 0
     for index in range(plan.count):
-        base, used = plan.base(index), plan.used(index)
-        a, rest = divmod(index, 8)
-        block = slots[a, rest // 4, rest // 2 % 2, rest % 2].astype(FLOAT)[:used]
-        if plan.lead(index):
-            before = even[pl.ds(base, 1), :]
-            even[pl.ds(base, used), :] = block
-            even[pl.ds(base, 1), :] = before + block[0:1]
+        if index == plan.first_late:
+            even[pl.ds(filled, plan.border - filled), :] = jnp.zeros((plan.border - filled, LANES), FLOAT)
+            half_turn(plan, even, odd)
+            filled = plan.border
+        frame = odd if plan.late(index) else even
+        start = plan.base(index) // 8 * 8
+        rows = -(-(plan.base(index) - start + plan.used(index)) // 8) * 8
+        block = slots[(*spot_of(index), pl.ds(0, plan.rows))].astype(FLOAT)
+        if start < filled:
+            frame[pl.ds(start, 8), :] += block[:8]
+            frame[pl.ds(start + 8, rows - 8), :] = block[8:rows]
         else:
-            even[pl.ds(base, used), :] = block
+            frame[pl.ds(start, rows), :] = block[:rows]
+        filled = start + rows
+
+
+def half_turn(plan, even, odd):
+    total = plan.border - 8
     span = 256
-    total = (plan.frame_rows - 16) // span
-
-    @pl.loop(0, total)
+
+    def turn(start, rows):
+        here = pltpu.roll(even[pl.ds(start, rows), :], 64, 1)
+        below = pltpu.roll(even[pl.ds(start + 1, rows), :], 64, 1)
+        odd[pl.ds(start, rows), :] = jnp.where(lane_iota(rows) < 64, here, below)
+
+    @pl.loop(0, total // span)
     def _(step):
-        start = pl.multiple_of(step * span, span)
-        odd[pl.ds(start, span), :] = half_turn(even, start, span)
-
-    rest = plan.frame_rows - 16 - total * span
-    odd[pl.ds(total * span, rest), :] = half_turn(even, total * span, rest)
+        turn(pl.multiple_of(step * span, span), span)
+
+    if total % span:
+        turn(total // span * span, total % span)
 
 
 def read_param(even, odd, name, target):
@@ -624,15 +710,25 @@
     pl.run_scoped(interleave, pltpu.VMEM((rows, LANES), FLOAT))
 
 
-def emit_slots(plan, even, odd, slots):
-    for index in range(plan.count):
-        base, used = plan.base(index), plan.used(index)
-        a, rest = divmod(index, 8)
-        spot = (a, rest // 4, rest // 2 % 2, rest % 2)
-        here = pltpu.roll(odd[pl.ds(base + 8, plan.rows), :], 64, 1)
-        above = pltpu.roll(odd[pl.ds(base + 7, plan.rows), :], 64, 1)
-        late = jnp.where(lane_iota(plan.rows) < 64, above, here)
-        slots[spot] = (even[pl.ds(base, plan.rows), :] + late).astype(BRAIN)
+def clear_frames(plan, even, odd):
+    even[...] = jnp.zeros_like(even)
+    odd[pl.ds(0, plan.border + 16), :] = jnp.zeros((plan.border + 16, LANES), FLOAT)
+    table = layout()
+    final = (table["headb"][0] // LANES) // 8 * 8
+    odd[pl.ds(final, odd.shape[0] - final), :] = jnp.zeros((odd.shape[0] - final, LANES), FLOAT)
+
+
+def emit_slots(plan, even, odd, slots, values):
+    rows = plan.rows
+    for index in range(values[0] * 16, values[-1] * 16 + 16):
+        start = plan.base(index) // 8 * 8
+        if plan.late(index):
+            block = odd[pl.ds(start + 8, rows), :]
+        else:
+            here = pltpu.roll(odd[pl.ds(start + 8, rows), :], 64, 1)
+            above = pltpu.roll(odd[pl.ds(start + 7, rows), :], 64, 1)
+            block = even[pl.ds(start, rows), :] + jnp.where(lane_iota(rows) < 64, above, here)
+        slots[spot_of(index)] = block.astype(BRAIN)
 
 
 def dot(left, right, dims=(((1,), (0,)), ((), ()))):
@@ -832,17 +928,123 @@
         emit(prefix + name, prefix + bias, rows_of(left), rows_of(right))
 
 
-def step_body(plan, counts_ref, slots, seen_ref, tgt_ref, meta_ref, spot_enc, spot_dec, grad_out, loss_out, *scratch):
+NORMS = ("ln1g", "ln1b", "ln2g", "ln2b", "encg", "encb", "decg", "decb", "mask")
+
+
+class Images:
+    def __init__(self, place, counts_ref, meta_ref):
+        spot = place["B"] * 2 + place["C"]
+        self.meta_ref = meta_ref
+        self.own = counts_ref[0, 0]
+        lane = lane_iota(8)
+        row = lax.broadcasted_iota(jnp.int32, (8, LANES), 0)
+
+        def count_of(hub):
+            corner = jnp.where((lane == LANES - 1) & (row == 0), meta_ref[hub], 0.0)
+            return jnp.sum(corner).astype(jnp.int32)
+
+        one, two = count_of(1), count_of(2)
+        from_one = jnp.where(spot == 0, 3, jnp.where(spot == 2, 4, 5))
+        from_two = jnp.where(spot == 0, 3, jnp.where(spot == 1, 4, 5))
+        use_one = (spot == 2) | ((spot != 1) & (one > 2))
+        mine = self.own > 2
+
+        def choose(own, first, second):
+            return jnp.where(mine, own, jnp.where(use_one, first, second))
+
+        self.third = choose(2, 3, 4)
+        self.third_row = choose(2, from_one, from_two)
+        self.third_count = choose(self.own, one, two)
+        self.third_meta = choose(0, 1, 2)
+
+    def __call__(self, image):
+        last = image == 2
+        source = jnp.where(last, self.third, image)
+        line = jnp.where(last, self.third_row, image)
+        live = jnp.where(last, self.third_count, self.own) > line
+        kept = self.meta_ref[jnp.where(last, self.third_meta, 0), pl.ds(line, 1), :][:, :HOME]
+        return source, kept, live.astype(FLOAT)
+
+
+def placement(kept, rows):
+    number = lax.broadcasted_iota(jnp.int32, (rows, HOME), 0).astype(FLOAT)
+    return (number == kept).astype(FLOAT)
+
+
+def whole_body(
+    plan, counts_ref, keep_ref, x_ref, patches_ref, targets_ref, enc_table, dec_table,
+    total_out, scalars_out, *scratch
+):
+    scratch = list(scratch)
+
+    def take(count):
+        taken = scratch[:count]
+        del scratch[:count]
+        return taken
+
     names = list(layout())
-    even, odd, sums_ref, y_hi, y_lo, dy_home, final_all, dpred_all = scratch[:8]
-    weights = Weights(scratch[8 : 8 + len(names)])
-    enc_refs = scratch[8 + len(names) : 8 + len(names) + 13]
-    dec_refs = scratch[8 + len(names) + 13 :]
+    slots, seen_ref, tgt_own, tgt_ref, wanted, meta_ref, grad_ref, loss_ref = take(8)
+    spot_enc, spot_dec, local = take(3)
+    line, rolled, pixels, spare, send, recv, hand, taken = take(8)
+    even, odd, sums_ref, y_hi, y_lo, dy_home, final_all, dpred_all = take(8)
+    weights = Weights(take(len(names)))
+    enc_refs, dec_refs = take(13), take(13)
+    core_in, tree_in, column_in, own_ref, turned, near, far, mine, column_send, column_recv = take(10)
+
+    place = position()
+    device = index_of(place)
+    copies = [
+        pltpu.make_async_copy(patches_ref, pixels, local.at[0]),
+        pltpu.make_async_copy(enc_table, spot_enc, local.at[1]),
+        pltpu.make_async_copy(dec_table, spot_dec, local.at[2]),
+        pltpu.make_async_copy(
+            targets_ref.at[pl.ds(0, LIVE_CAP - 1)], tgt_own, local.at[3]
+        ),
+        pltpu.make_async_copy(targets_ref.at[LIVE_CAP - 1], tgt_ref.at[0], local.at[4]),
+    ]
+    for copy in copies:
+        copy.start()
+    slots[(place["H"], place["L"], place["B"], place["C"], place["r"])] = own_block(
+        plan, device, x_ref, line, rolled
+    )
+    group, column = partners(place, plan.outer)
+    meet(group + column)
+    sender = Sender(send, recv)
+    handing = Handing(place, spare, seen_ref, meta_ref, targets_ref, tgt_ref, hand, taken)
+
+    def between(stage):
+        if stage:
+            return
+        lane = lane_iota(8)
+        row = lax.broadcasted_iota(jnp.int32, (8, LANES), 0)
+        held = counts_ref[0, 0].astype(FLOAT)
+        meta_ref[0] = jnp.where((lane == LANES - 1) & (row == 0), held, -1.0)
+        meta_ref[0, pl.ds(0, keep_ref.shape[0]), pl.ds(0, VIS)] = keep_ref[...].astype(FLOAT)
+        copies[0].wait()
+
+        def visible(image):
+            where = placement(meta_ref[0, pl.ds(image, 1), :][:, :HOME], NP).astype(BRAIN)
+            return dot(where, pixels[image], DEEP).astype(BRAIN)
+
+        def prepare(hub):
+            for number in range(3):
+                spare[number] = visible(3 + number)
+
+        handing.on_hub(prepare)
+        handing.start((0, 1))
+        for image in range(LIVE_CAP):
+            seen_ref[image] = visible(image)
+
+    pending = gather_body(plan, place, slots, sender, between)
+    handing.start((2,))
+    handing.receive((0, 1))
+    for copy in copies[1:]:
+        copy.wait()
+
     assemble(plan, slots, even, odd)
     for name in names:
         read_param(even, odd, name, weights.refs[name])
-    even[...] = jnp.zeros_like(even)
-    odd[...] = jnp.zeros_like(odd)
+    clear_frames(plan, even, odd)
     view = odd.at[pl.ds(8, plan.frame_rows)]
     sums_ref[...] = jnp.zeros_like(sums_ref)
     order = {name: number for number, name in enumerate(names)}
@@ -850,39 +1052,12 @@
     def add_sum(name, value):
         sums_ref[pl.ds(order[name], 1), pl.ds(0, value.shape[1])] += value
 
-    spot = lax.rem(lax.axis_index("dp"), 4)
-    own = counts_ref[0, 0]
-    lane = lane_iota(8)
-    row = lax.broadcasted_iota(jnp.int32, (8, LANES), 0)
-
-    def count_of(hub):
-        return jnp.sum(jnp.where((lane == 127) & (row == 0), meta_ref[hub], 0.0)).astype(jnp.int32)
-
-    one, two = count_of(1), count_of(2)
-    from_one = jnp.where(spot == 0, 3, jnp.where(spot == 2, 4, 5))
-    from_two = jnp.where(spot == 0, 3, jnp.where(spot == 1, 4, 5))
-    use_one = (spot == 2) | ((spot != 1) & (one > 2))
-    third = jnp.where(own > 2, 2, jnp.where(use_one, 3, 4))
-    third_row = jnp.where(own > 2, 2, jnp.where(use_one, from_one, from_two))
-    third_count = jnp.where(own > 2, own, jnp.where(use_one, one, two))
-    third_meta = jnp.where(own > 2, 0, jnp.where(use_one, 1, 2))
-
-    def pick(image):
-        last = image == 2
-        source = jnp.where(last, third, image)
-        line = jnp.where(last, third_row, image)
-        live = jnp.where(last, third_count, own) > line
-        kept = meta_ref[jnp.where(last, third_meta, 0), pl.ds(line, 1), :][:, :HOME]
-        return source, kept, live.astype(FLOAT)
-
-    def placement(kept):
-        number = lax.broadcasted_iota(jnp.int32, (ROWS, HOME), 0).astype(FLOAT)
-        return (number == kept).astype(FLOAT)
+    pick = Images(place, counts_ref, meta_ref)
 
     visible, begin = [], []
     for image in range(LIVE_CAP):
         source, kept, live = pick(image)
-        where = placement(kept).astype(BRAIN)
+        where = placement(kept, ROWS).astype(BRAIN)
         visible.append(seen_ref[source])
         begin.append(dot(where, spot_enc[0], DEEP) + dot(where, spot_enc[1], DEEP))
     visible = jnp.concatenate(visible, axis=0)
@@ -908,7 +1083,7 @@
 
     def one_image(image, total):
         source, kept, live = pick(image)
-        where = placement(kept)
+        where = placement(kept, ROWS)
         seen = jnp.sum(where, axis=1, keepdims=True)
         where = where.astype(BRAIN)
         grid_in = dot(where, y_hi[image]) + dot(where, y_lo[image])
@@ -920,7 +1095,17 @@
         final_all[image] = final
         predicted = dot(final, weights("head")) + weights("headb")
         weight = jnp.where(real, (1.0 - 0.9 * seen) * live, 0.0)
-        error = predicted[:NP] - tgt_ref[source].astype(FLOAT)
+
+        @pl.when(image == LIVE_CAP - 1)
+        def _():
+            handing.receive((2,))
+            wanted[...] = tgt_ref[pick.third - 2]
+
+        @pl.when(image < LIVE_CAP - 1)
+        def _():
+            wanted[...] = tgt_own[image]
+
+        error = predicted[:NP] - wanted[...].astype(FLOAT)
         weighted = error * weight[:NP]
         total = total + jnp.sum(weighted * error, axis=0, keepdims=True)
         dpred_all[image, pl.ds(0, NP)] = (weighted * (2.0 / PIX)).astype(BRAIN)
@@ -935,7 +1120,7 @@
         return total
 
     total = lax.fori_loop(0, LIVE_CAP, one_image, jnp.zeros((1, PIX), FLOAT))
-    loss_out[0] = jnp.sum(total) * (1.0 / PIX)
+    loss_ref[0] = jnp.sum(total) * (1.0 / PIX)
 
     def emit(name, bias, left, right):
         ones = jnp.ones((16, right.shape[0]), BRAIN)
@@ -947,26 +1132,55 @@
         turned = left.T
         write_grad(even, view, name, lambda start, size: dot(turned, right[:, start : start + size]))
 
+    def emit_norms(prefixes):
+        for name in names:
+            if name.endswith(NORMS) and name.startswith(prefixes):
+                row = pl.ds(order[name], 1)
+                write_grad(even, view, name, lambda start, size, row=row: sums_ref[row, pl.ds(start, size)])
+
     d_embedded = dy_home[...].reshape(enc_rows, E)
     emit("embed", "embedb", encoder_out, d_embedded)
+    block_grads(kept_view(dec_refs, *dec_shape), "dec_", emit)
+    emit("head", "headb", final_all[...].reshape(-1, E), dpred_all[...].reshape(-1, PIX))
+    emit_norms(("dec", "mask"))
+    late_values = list(range(plan.edge, plan.outer))
+    early_values = list(range(plan.edge))
+    emit_slots(plan, even, odd, grad_ref, late_values)
+    reducer = Reducer(
+        plan, place, grad_ref, core_in, tree_in, column_in, own_ref, sender, (column_send, column_recv)
+    )
+
+    def stage(values, reach):
+        for value in values:
+            reducer.stage(value, reach)
+
+    for value in late_values:
+        reducer.share(value)
     d_seen = dot(d_embedded, weights("embed"), PAIR).astype(BRAIN).astype(FLOAT)
     d_encoded, d_gain, d_shift = norm_back(d_seen, encoded, weights("encg"))
     add_sum("encg", d_gain)
     add_sum("encb", d_shift)
+    stage(late_values, 2)
     d_first = block_home(d_encoded, enc, weights, "enc_", HEADS, add_sum).astype(BRAIN)
+    stage(late_values, 1)
     emit("patch", "patchb", visible, d_first)
+    stage(late_values, 0)
     block_grads(enc, "enc_", emit)
-    block_grads(kept_view(dec_refs, *dec_shape), "dec_", emit)
-    emit("head", "headb", final_all[...].reshape(-1, E), dpred_all[...].reshape(-1, PIX))
-    for name, (offset, shape) in layout().items():
-        if name[-4:] in ("ln1g", "ln1b", "ln2g", "ln2b", "encg", "encb", "decg", "decb", "mask"):
-            write_grad(
-                even,
-                view,
-                name,
-                lambda start, size, name=name: sums_ref[pl.ds(order[name], 1), pl.ds(start, size)],
-            )
-    emit_slots(plan, even, odd, grad_out)
+    emit_norms(("enc",))
+    stage(late_values, -1)
+    emit_slots(plan, even, odd, grad_ref, early_values)
+    for value in early_values:
+        reducer.share(value)
+    for reach in (2, 1, 0, -1):
+        stage(early_values, reach)
+    reducer.finish()
+    pending += finish_body(
+        plan, place, counts_ref, loss_ref, own_ref, total_out, scalars_out, turned, near, far, mine, sender
+    )
+    reducer.close()
+    handing.finish((0, 1, 2))
+    for copy in pending:
+        copy.wait_send()
 
 
 def weight_scratch():
@@ -979,38 +1193,15 @@
     return shapes
 
 
-def whole_body(
-    plan, counts_ref, keep_ref, x_ref, patches_ref, targets_ref, enc_table, dec_table,
-    total_out, scalars_out, *scratch
-):
-    scratch = list(scratch)
-
-    def take(count):
-        taken = scratch[:count]
-        del scratch[:count]
-        return taken
-
-    (slots, seen, tgt, meta, grad, loss, spot_enc, spot_dec, tables) = take(9)
-    copies = [
-        pltpu.make_async_copy(enc_table, spot_enc, tables.at[0]),
-        pltpu.make_async_copy(dec_table, spot_dec, tables.at[1]),
-    ]
-    for copy in copies:
-        copy.start()
-    gather_body(
-        plan, counts_ref, keep_ref, x_ref, patches_ref, targets_ref, slots, seen, tgt, meta, *take(9)
-    )
-    for copy in copies:
-        copy.wait()
-    names = len(layout())
-    step_body(
-        plan, counts_ref, slots, seen, tgt, meta, spot_enc, spot_dec, grad, loss, *take(8 + names + 26)
-    )
-    reduce_body(plan, counts_ref, loss, grad, total_out, scalars_out, *scratch)
+def copies_used(plan):
+    parts = len(plan.parts)
+    spread = parts * (plan.outer - 1) + parts * plan.outer * (7 + 4)
+    home = parts * plan.outer * (1 + 7)
+    return spread + home + 15 + plan.outer - 1
 
 
 def whole_step(counts, keep, master, patches, targets, plan):
-    outer, rows = plan.outer, plan.rows
+    outer, rows, lines = plan.outer, plan.rows, plan.lines
     vmem = pl.BlockSpec(memory_space=pltpu.VMEM)
     smem = pl.BlockSpec(memory_space=pltpu.SMEM)
     far = pl.BlockSpec(memory_space=pl.ANY)
@@ -1018,14 +1209,13 @@
     upper = table.astype(BRAIN)
     spot_enc = jnp.asarray(np.stack([upper, (table - upper.astype(np.float32)).astype(BRAIN)]))
     spot_dec = jnp.asarray(place_table(NP, ROWS, E))
-    block = pltpu.VMEM((outer, 2, 2, 2, rows, LANES), BRAIN)
-    out_copies = 3 * (outer + 1 + outer + 2)
-    home_copies = 3 + 3 * (outer + 1) + 7 + outer - 1
+    block = pltpu.VMEM((outer, 2, 2, 2, 2, rows, LANES), BRAIN)
     dma = pltpu.SemaphoreType.DMA
+    copies = copies_used(plan)
     return pl.pallas_call(
         functools.partial(whole_body, plan),
         out_shape=(
-            jax.ShapeDtypeStruct((rows, LANES), FLOAT),
+            jax.ShapeDtypeStruct((lines, LANES), FLOAT),
             jax.ShapeDtypeStruct((1, LANES), FLOAT),
         ),
         in_specs=[smem, vmem, vmem, far, far, far, far],
@@ -1033,23 +1223,24 @@
         scratch_shapes=[
             block,
             pltpu.VMEM((5, HOME, PIX), BRAIN),
-            pltpu.VMEM((5, NP, PIX), BRAIN),
+            pltpu.VMEM((LIVE_CAP - 1, NP, PIX), BRAIN),
+            pltpu.VMEM((3, NP, PIX), BRAIN),
+            pltpu.VMEM((NP, PIX), BRAIN),
             pltpu.VMEM((3, 8, LANES), FLOAT),
             block,
             pltpu.SMEM((1,), FLOAT),
             pltpu.VMEM(spot_enc.shape, BRAIN),
             pltpu.VMEM(spot_dec.shape, FLOAT),
-            dma((2,)),
-            pltpu.VMEM((rows * LANES,), FLOAT),
+            dma((5,)),
+            pltpu.VMEM((lines * LANES,), FLOAT),
             pltpu.VMEM((rows + 8, LANES), FLOAT),
             pltpu.VMEM(patches.shape, BRAIN),
             pltpu.VMEM((3, HOME, PIX), BRAIN),
-            dma((out_copies,)),
-            dma((out_copies,)),
-            dma((2,)),
+            dma((copies,)),
+            dma((copies,)),
             dma((2, 3, 3)),
             dma((2, 3)),
-            pltpu.VMEM((plan.frame_rows, LANES), FLOAT),
+            pltpu.VMEM((plan.border + rows, LANES), FLOAT),
             pltpu.VMEM((plan.frame_rows + 8, LANES), FLOAT),
             pltpu.VMEM((48, E), FLOAT),
             pltpu.VMEM((LIVE_CAP, HOME, E), BRAIN),
@@ -1060,14 +1251,16 @@
             *weight_scratch(),
             *kept_scratch(1, LIVE_CAP * HOME, D, FF, HEADS),
             *kept_scratch(LIVE_CAP, ROWS, E, DFF, DHEADS),
-            pltpu.VMEM((outer, 2, 2, rows, LANES), BRAIN),
-            pltpu.VMEM((rows + 8, LANES), FLOAT),
-            pltpu.VMEM((8, 8, LANES), FLOAT),
+            pltpu.VMEM((outer, 2, 2, 2, rows, LANES), BRAIN),
+            pltpu.VMEM((outer, 8, rows, LANES), BRAIN),
+            pltpu.VMEM((outer, rows, LANES), BRAIN),
+            pltpu.VMEM((rows, LANES), FLOAT),
+            pltpu.VMEM((rows, LANES), FLOAT),
+            pltpu.VMEM((16, 8, LANES), FLOAT),
             pltpu.VMEM((outer, 8, LANES), FLOAT),
-            pltpu.VMEM((8, LANES), FLOAT),
-            dma((home_copies,)),
-            dma((home_copies,)),
-            *reduce_scratch(plan),
+            pltpu.VMEM((2, 8, LANES), FLOAT),
+            dma((outer, len(plan.parts))),
+            dma((outer, len(plan.parts))),
         ],
         compiler_params=pltpu.CompilerParams(
             collective_id=0, has_side_effects=True, vmem_limit_bytes=60 << 20

time: 124 us -> 101 us (0.81)
  Pallas kernels: 120 us -> 97 us
    pallas_call x1, Pallas kernels: 117 us -> 94.8 us  [whole_step(): pl.pallas_call(functools.partial(whole_body, plan), out_shape=(jax.ShapeD...]
where the time goes in v2:
time: 101 us
  Pallas kernels  97 us (96%)
  between operations  2.15 us (2%)
  local copies, waits for them, and re-layouts  1.61 us (2%)
    pallas_call x1, Pallas kernels, whole_step(): pl.pallas_call(functools.partial(whole_body, plan), out_shape=(jax.ShapeD...  94.8 us
    pallas_call x1, Pallas kernels, update(): pl.pallas_call(functools.partial(update_body, plan), out_shape=(flat, fla...  2.2 us

profile of v2, /device:TPU:0, one launch (start us, length us, event | category | flops | bytes accessed | tf_op | source)
XLA Modules:
  0.0 100.8 jit_solution(12653543727070073148)
XLA Ops:
  1.9 0.0 copy-start
  1.9 0.0 copy-start.1
  1.9 0.0 copy-start.2
  2.0 94.8 %shard_map.145 = (f32[400,128]{1,0:T(8,128)}, f32[1,128]{1,0:T(1,128)}) custom-call(s32[1,1]{1,0:T(1,128)S(6)} %copy.16.counts_ref, s32[6,49]{1,0:T(8,128)} %keep_ref.1, f32[50930]{0:T(1024)} %master_ref.1, bf16[6,196,768]{2,1,0:T(8,128)(2,1)} %patches_ref.1, bf16[6,196,768]{2,1,0:T(8,128)(2,1)} %targets_ref.1, ...), custom_call_target="tpu_custom_call" | custom-call | tf_op jit(solution)/shard_map/pallas_call | solution.py:1215
  96.8 0.0 copy-done
  96.8 0.0 copy-done.1
  96.8 0.0 copy-done.2
  96.8 0.0 copy-start.3
  96.8 0.9 copy-done.3
  97.7 0.0 copy-start.4
  97.7 0.7 copy-done.4
  98.4 2.2 %shard_map.146 = (f32[50930]{0:T(1024)}, f32[50930]{0:T(1024)}, f32[50930]{0:T(1024)}, bf16[50930]{0:T(1024)(128)(2,1)}, f32[1,1]{1,0:T(1,128)}, /*index=5*/f32[1,1]{1,0:T(1,128)}) custom-call(s32[1]{0:T(128)S(6)} %copy.17.step_ref, f32[400,128]{1,0:T(8,128)S(1)} %copy-done.3, f32[1,128]{1,0:T(1,128)S(1)} %copy-done.4, f32[50930]{0:T(1024)S(1)} %copy-done, ...), custom_call_target="tpu_custom_call" | custom-call | tf_op jit(solution)/shard_map/pallas_call | solution.py:594
Async XLA Ops:
  1.9 94.9 %copy-start = (f32[50930]{0:T(1024)S(1)}, f32[50930]{0:T(1024)}, u32[]{:S(2)}) copy-start(f32[50930]{0:T(1024)} %master_ref.1) | copy-start | bytes 611164
  1.9 94.9 %copy-start.1 = (f32[50930]{0:T(1024)S(1)}, f32[50930]{0:T(1024)}, u32[]{:S(2)}) copy-start(f32[50930]{0:T(1024)} %first_ref.1) | copy-start | bytes 611164
  1.9 94.9 %copy-start.2 = (f32[50930]{0:T(1024)S(1)}, f32[50930]{0:T(1024)}, u32[]{:S(2)}) copy-start(f32[50930]{0:T(1024)} %second_ref.1) | copy-start | bytes 611164
  96.8 0.9 copy-start.3
  97.7 0.7 copy-start.4

commit v3 on v2

--- a/solution.py
+++ b/solution.py
@@ -106,10 +106,17 @@
             self.parts = ((0, sizes[0]), (sizes[0], sizes[1]), (sizes[0] + sizes[1], sizes[2]))
             self.orders = ("LCB", "BLC", "CBL")
         self.first_late = -(-self.split // length)
-        self.edge = -(-self.split // (16 * length))
+        self.depths = count // 8
+        pieces = 4 if self.outer == 2 else 1
+        cuts = [self.rows // 16 * number // pieces * 16 for number in range(pieces + 1)]
+        self.halves = tuple((low, high - low) for low, high in zip(cuts, cuts[1:]))
+        self.ways = ("CB", "BC", "CB", "BC")[:pieces]
         last = self.first_late - 1
         self.border = (self.base(last) + self.used(last) + 1 + 7) // 8 * 8 + 8
         self.frame_rows = (length * count // LANES + 7) // 8 * 8 + self.rows + 16
+
+    def depths_from(self, name):
+        return min(-(-layout()[name][0] // (8 * self.length)), self.depths)
 
     def late(self, index):
         return index >= self.first_late
@@ -170,12 +177,32 @@
 
 
 def partners(place, outer):
+    digits = "rCBLH" if outer == 2 else "rCBL"
     group = []
-    for number in range(1, 16):
-        dims = [dim for bit, dim in enumerate("rCBL") if number >> bit & 1]
-        group.append(flipped(place, dims))
-    column = [moved(place, "H", lax.rem(place["H"] + step, outer)) for step in range(1, outer)]
+    for number in range(1, 1 << len(digits)):
+        group.append(flipped(place, [dim for bit, dim in enumerate(digits) if number >> bit & 1]))
+    column = []
+    if outer > 2:
+        column = [moved(place, "H", lax.rem(place["H"] + step, outer)) for step in range(1, outer)]
     return group, column
+
+
+def at_depth(place, depth):
+    return {**place, "H": depth // 2, "L": depth % 2}
+
+
+def depth_of(place):
+    return place["H"] * 2 + place["L"]
+
+
+def gates(place, plan):
+    group, column = partners(place, plan.outer)
+    if plan.outer > 2:
+        depth = depth_of(place)
+        column = column + [
+            at_depth(place, lax.rem(depth + step, plan.depths)) for step in range(1, plan.depths)
+        ]
+    return group + column
 
 
 def branches(order):
@@ -188,20 +215,42 @@
     return [(dims, onward) for reach, count, dims, onward in nodes]
 
 
+class Copy:
+    def __init__(self, recipe, send, recv, number):
+        self.recipe, self.send, self.recv, self.number = recipe, send, recv, number
+
+    def make(self):
+        source, target, place = self.recipe()
+        return pltpu.make_async_remote_copy(
+            src_ref=source,
+            dst_ref=target,
+            send_sem=self.send.at[self.number],
+            recv_sem=self.recv.at[self.number],
+            device_id=device_of(place),
+            device_id_type=MESH,
+        )
+
+    def start(self):
+        self.make().start()
+
+    def wait_recv(self):
+        self.make().wait_recv()
+
+    def wait_send(self):
+        self.make().wait_send()
+
+
 class Sender:
     def __init__(self, send, recv):
         self.send, self.recv, self.used = send, recv, 0
 
-    def start(self, source, target, place):
-        copy = pltpu.make_async_remote_copy(
-            src_ref=source,
-            dst_ref=target,
-            send_sem=self.send.at[self.used],
-            recv_sem=self.recv.at[self.used],
-            device_id=device_of(place),
-            device_id_type=MESH,
-        )
+    def plan(self, recipe):
+        copy = Copy(recipe, self.send, self.recv, self.used)
         self.used += 1
+        return copy
+
+    def start(self, recipe):
+        copy = self.plan(recipe)
         copy.start()
         return copy
 
@@ -293,67 +342,117 @@
     return jnp.where(lane_iota(rows) >= lead, upper, lower).astype(BRAIN)
 
 
-def gather_body(plan, place, out_ref, sender, between):
-    outer = plan.outer
-    high = place["H"]
-    sibling = flipped(place, "r")
-    count = len(plan.parts)
-
-    def region(value, part, fixed, free=""):
-        start, size = plan.parts[part]
+class Gather:
+    def __init__(self, plan, place, out_ref, sender, columns):
+        self.plan, self.place, self.out_ref, self.sender, self.columns = plan, place, out_ref, sender, columns
+        self.flights, self.onwards, self.siblings = {}, [], {}
+
+    def region(self, value, part, fixed, free=""):
+        start, size = self.plan.parts[part]
         index = [value]
         for dim in "LBC":
             if dim in free:
                 index.append(pl.ds(0, 2))
             else:
-                index.append(1 - place[dim] if dim in fixed else place[dim])
-        return out_ref.at[(*index, place["r"], pl.ds(start, size))]
-
-    column = []
-    for part in range(count):
-        for step in range(1, outer):
-            source = region(high, part, "")
-            target = moved(place, "H", lax.rem(high + step, outer))
-            column.append((step, part, sender.start(source, source, target)))
-    flights, onwards, siblings = {}, [], []
-
-    values = [lax.rem(high + outer - step, outer) for step in range(outer)]
-
-    def spread(number, part, dims, onward):
+                index.append(1 - self.place[dim] if dim in fixed else self.place[dim])
+        return self.out_ref.at[(*index, self.place["r"], pl.ds(start, size))]
+
+    def column(self, source, part, target):
+        send, recv = self.columns
+        ref = self.region(source, part, "")
+        return pltpu.make_async_remote_copy(
+            src_ref=ref,
+            dst_ref=ref,
+            send_sem=send.at[target, part],
+            recv_sem=recv.at[source, part],
+            device_id=device_of(moved(self.place, "H", target)),
+            device_id_type=MESH,
+        )
+
+    def over_column(self, act):
+        high = self.place["H"]
+        for target in range(self.plan.outer):
+
+            @pl.when(high != target)
+            def _(target=target):
+                for part in range(len(self.plan.parts)):
+                    act(self.column(high, part, target))
+
+    def begin(self):
+        self.over_column(lambda copy: copy.start())
+
+    def roots(self, meanwhile):
+        plan, place = self.plan, self.place
+        copies = {}
+        for value in range(plan.outer):
+            copies[value] = []
+            for part, order in enumerate(plan.orders):
+                copies[value].append(self.spread(value, part, "", order) + [self.give(value, part, -1)])
+
+        for value, groups in copies.items():
+
+            @pl.when(place["H"] == value)
+            def _(groups=groups):
+                for group in groups:
+                    for copy in group:
+                        copy.start()
+
+        meanwhile()
+        for value, groups in copies.items():
+
+            @pl.when(place["H"] != value)
+            def _(value=value, groups=groups):
+                for part, group in enumerate(groups):
+                    self.column(value, part, place["H"]).wait_recv()
+                    for copy in group:
+                        copy.start()
+
+    def spread(self, value, part, dims, onward):
+        def recipe(dim):
+            source = self.region(value, part, dims)
+            return source, source, flipped(self.place, dim)
+
+        copies = []
         for dim in onward:
-            source = region(values[number], part, dims)
-            copy = sender.start(source, source, flipped(place, dim))
-            flights[number, part, frozenset(dims + dim)] = copy
-            onwards.append(copy)
-
-    for number in range(outer):
-        for part in range(count):
-            if number > 0:
-                for step, which, copy in column:
-                    if step == number and which == part:
-                        copy.wait_recv()
-            spread(number, part, "", plan.orders[part])
-        between(number)
-    trees = [branches(order) for order in plan.orders]
-    for place_in_tree in range(len(trees[0])):
-        for number, value in enumerate(values):
-            for part in range(count):
-                dims, onward = trees[part][place_in_tree]
-                order = plan.orders[part]
-                if dims:
-                    flights[number, part, frozenset(dims)].wait_recv()
-                    spread(number, part, dims, onward)
-                reach = order.index(dims[-1]) if dims else -1
-                if place_in_tree + 1 == len(trees[0]) or (
-                    order.index(trees[part][place_in_tree + 1][0][-1]) > reach
-                ):
-                    fixed = order[reach] if dims else ""
-                    source = region(value, part, fixed, order[: max(reach, 0)])
-                    siblings.append(sender.start(source, source, sibling))
-        between(outer + place_in_tree)
-    for copy in siblings:
-        copy.wait_recv()
-    return [copy for step, part, copy in column] + onwards + siblings
+            copy = self.sender.plan(functools.partial(recipe, dim))
+            self.flights[value, part, frozenset(dims + dim)] = copy
+            copies.append(copy)
+        self.onwards += copies
+        return copies
+
+    def give(self, value, part, reach):
+        order = self.plan.orders[part]
+
+        def recipe():
+            source = self.region(value, part, order[reach] if reach >= 0 else "", order[: max(reach, 0)])
+            return source, source, flipped(self.place, "r")
+
+        copy = self.sender.plan(recipe)
+        self.siblings.setdefault(value, []).append(copy)
+        return copy
+
+    def stage(self, value, reach):
+        plan = self.plan
+        trees = []
+        for order in plan.orders:
+            trees.append([node for node in branches(order) if node[0] and reach == order.index(node[0][-1])])
+        for nodes in zip(*trees):
+            for part, (dims, onward) in enumerate(nodes):
+                self.flights.pop((value, part, frozenset(dims))).wait_recv()
+                for copy in self.spread(value, part, dims, onward):
+                    copy.start()
+        for part in range(len(plan.orders)):
+            self.give(value, part, reach).start()
+
+    def ready(self, value):
+        for copy in self.siblings[value]:
+            copy.wait_recv()
+
+    def close(self):
+        self.over_column(lambda copy: copy.wait_send())
+        for copies in [self.onwards] + list(self.siblings.values()):
+            for copy in copies:
+                copy.wait_send()
 
 
 class Reducer:
@@ -363,27 +462,31 @@
         self.column_in, self.own_ref, self.columns = column_in, own_ref, columns
         self.cores = {}
         self.pending = []
-        self.trees = [branches(order) for order in plan.orders]
+        self.trees = [branches(order) for order in plan.ways]
         self.flights = {}
 
     def share(self, value):
         place = self.place
-        for part, (start, size) in enumerate(self.plan.parts):
-            whole = (value, pl.ds(0, 2), pl.ds(0, 2), pl.ds(0, 2))
+
+        def recipe(start, size):
+            whole = (value, pl.ds(0, 2), pl.ds(0, 2))
             span = pl.ds(start, size)
-            copy = self.sender.start(
+            return (
                 self.grad_ref.at[(*whole, 1 - place["r"], span)],
                 self.core_in.at[(*whole, span)],
                 flipped(place, "r"),
             )
+
+        for part, (start, size) in enumerate(self.plan.halves):
+            copy = self.sender.start(functools.partial(recipe, start, size))
             self.cores[value, part] = copy
             self.pending.append(copy)
 
     def stage(self, value, reach):
         plan, place = self.plan, self.place
         steps = []
-        for part in range(len(plan.parts)):
-            order = plan.orders[part]
+        for part in range(len(plan.halves)):
+            order = plan.ways[part]
             nodes = [
                 (dims, onward)
                 for dims, onward in reversed(self.trees[part])
@@ -396,81 +499,85 @@
 
     def node(self, value, part, dims, onward):
         plan, place = self.plan, self.place
-        start, size = plan.parts[part]
+        start, size = plan.halves[part]
         span = pl.ds(start, size)
         if (value, part) in self.cores:
             self.cores.pop((value, part)).wait_recv()
         for dim in onward:
             self.flights.pop((value, part, frozenset(dims + dim))).wait_recv()
-        index = [value] + [1 - place[dim] if dim in dims else place[dim] for dim in "LBC"]
+        index = [value] + [1 - place[dim] if dim in dims else place[dim] for dim in "BC"]
         total = self.grad_ref[(*index, place["r"], span)].astype(FLOAT)
         total = total + self.core_in[(*index, span)].astype(FLOAT)
-        order = plan.orders[part]
 
         def number(dims):
-            return sum(1 << "LBC".index(dim) for dim in dims)
+            return sum(1 << "BC".index(dim) for dim in dims)
 
         for dim in onward:
             total = total + self.tree_in[value, number(dims + dim), span].astype(FLOAT)
-        mine = self.grad_ref.at[(*index, place["r"], span)]
+
+        def spot():
+            index = [value] + [1 - place[dim] if dim in dims else place[dim] for dim in "BC"]
+            return self.grad_ref.at[(*index, place["r"], span)]
+
+        def recipe():
+            return spot(), self.tree_in.at[value, number(dims), span], flipped(place, dims[-1])
+
         if dims:
-            mine[...] = total.astype(BRAIN)
-            copy = self.sender.start(
-                mine, self.tree_in.at[value, number(dims), span], flipped(place, dims[-1])
-            )
+            spot()[...] = total.astype(BRAIN)
+            copy = self.sender.start(recipe)
             self.flights[value, part, frozenset(dims)] = copy
             self.pending.append(copy)
             return
-        high = place["H"]
-
-        @pl.when(high == value)
+        depth = depth_of(place)
+
+        @pl.when(depth == value)
         def _():
             self.own_ref[span, :] = total
 
-        @pl.when(high != value)
+        @pl.when(depth != value)
         def _():
-            mine[...] = total.astype(BRAIN)
+            spot()[...] = total.astype(BRAIN)
             self.column(value, part).start()
 
     def column(self, value, part):
         plan, place = self.plan, self.place
-        start, size = plan.parts[part]
+        start, size = plan.halves[part]
         send, recv = self.columns
-        index = (value, place["L"], place["B"], place["C"], place["r"], pl.ds(start, size))
+        index = (value, place["B"], place["C"], place["r"], pl.ds(start, size))
         return pltpu.make_async_remote_copy(
             src_ref=self.grad_ref.at[index],
-            dst_ref=self.column_in.at[place["H"], pl.ds(start, size)],
+            dst_ref=self.column_in.at[depth_of(place), pl.ds(start, size)],
             send_sem=send.at[value, part],
-            recv_sem=recv.at[place["H"], part],
-            device_id=device_of(moved(place, "H", value)),
+            recv_sem=recv.at[depth_of(place), part],
+            device_id=device_of(at_depth(place, value)),
             device_id_type=MESH,
         )
 
     def arrival(self, source, part):
         plan, place = self.plan, self.place
-        start, size = plan.parts[part]
+        start, size = plan.halves[part]
         send, recv = self.columns
         return pltpu.make_async_remote_copy(
             src_ref=self.own_in(part),
             dst_ref=self.column_in.at[source, pl.ds(start, size)],
             send_sem=send.at[source, part],
             recv_sem=recv.at[source, part],
-            device_id=device_of(moved(place, "H", source)),
+            device_id=device_of(at_depth(place, source)),
             device_id_type=MESH,
         )
 
     def own_in(self, part):
         place = self.place
-        start, size = self.plan.parts[part]
-        index = (0, place["L"], place["B"], place["C"], place["r"], pl.ds(start, size))
+        start, size = self.plan.halves[part]
+        index = (0, place["B"], place["C"], place["r"], pl.ds(start, size))
         return self.grad_ref.at[index]
 
     def finish(self):
         plan, place = self.plan, self.place
-        for part, (start, size) in enumerate(plan.parts):
-            for source in range(plan.outer):
-
-                @pl.when(place["H"] != source)
+        for part, (start, size) in enumerate(plan.halves):
+            for source in range(plan.depths):
+
+                @pl.when(depth_of(place) != source)
                 def _(part=part, source=source, start=start, size=size):
                     self.arrival(source, part).wait_recv()
                     span = pl.ds(start, size)
@@ -480,10 +587,10 @@
         plan, place = self.plan, self.place
         for copy in self.pending:
             copy.wait_send()
-        for part in range(len(plan.parts)):
-            for value in range(plan.outer):
-
-                @pl.when(place["H"] != value)
+        for part in range(len(plan.halves)):
+            for value in range(plan.depths):
+
+                @pl.when(depth_of(place) != value)
                 def _(part=part, value=value):
                     self.column(value, part).wait_send()
 
@@ -503,23 +610,33 @@
     stats = jnp.where(lane == 0, squares, 0.0)
     stats = jnp.where(lane == 1, held_ref[0, 0].astype(FLOAT), stats)
     mine[0] = jnp.where(lane == 2, loss_ref[0], stats)
-    spot = ((place["L"] * 2 + place["B"]) * 2 + place["C"]) * 2 + place["r"]
+    count = len(group) + 1
+    spot = lax.rem(index_of(place), count)
     near[spot] = mine[0]
-    nears = [sender.start(mine.at[0], near.at[spot], other) for other in group]
+    nears = [
+        sender.start(functools.partial(lambda other: (mine.at[0], near.at[spot], other), other))
+        for other in group
+    ]
     total_out[...] = total
     for copy in nears:
         copy.wait_recv()
     together = near[0]
-    for other in range(1, 16):
+    for other in range(1, count):
         together = together + near[other]
-    far[place["H"]] = together
-    mine[1] = together
-    fars = [sender.start(mine.at[1], far.at[place["H"]], other) for other in column]
-    for copy in fars:
-        copy.wait_recv()
-    whole = far[0]
-    for other in range(1, outer):
-        whole = whole + far[other]
+    fars = []
+    whole = together
+    if column:
+        far[place["H"]] = together
+        mine[1] = together
+        fars = [
+            sender.start(functools.partial(lambda other: (mine.at[1], far.at[place["H"]], other), other))
+            for other in column
+        ]
+        for copy in fars:
+            copy.wait_recv()
+        whole = far[0]
+        for other in range(1, outer):
+            whole = whole + far[other]
     row = whole[0:1, :]
     lane = lane[0:1]
     held = jnp.sum(jnp.where(lane == 1, row, 0.0))
@@ -601,23 +718,28 @@
     )(step, total, scalars, master, first, second)
 
 
-def assemble(plan, slots, even, odd):
-    filled = 0
-    for index in range(plan.count):
+class Frames:
+    def __init__(self, plan, slots, even, odd):
+        self.plan, self.slots, self.even, self.odd = plan, slots, even, odd
+        self.filled = 0
+
+    def add(self, index):
+        plan, even = self.plan, self.even
         if index == plan.first_late:
-            even[pl.ds(filled, plan.border - filled), :] = jnp.zeros((plan.border - filled, LANES), FLOAT)
-            half_turn(plan, even, odd)
-            filled = plan.border
-        frame = odd if plan.late(index) else even
+            rest = plan.border - self.filled
+            even[pl.ds(self.filled, rest), :] = jnp.zeros((rest, LANES), FLOAT)
+            half_turn(plan, even, self.odd)
+            self.filled = plan.border
+        frame = self.odd if plan.late(index) else even
         start = plan.base(index) // 8 * 8
         rows = -(-(plan.base(index) - start + plan.used(index)) // 8) * 8
-        block = slots[(*spot_of(index), pl.ds(0, plan.rows))].astype(FLOAT)
-        if start < filled:
+        block = self.slots[(*spot_of(index), pl.ds(0, plan.rows))].astype(FLOAT)
+        if start < self.filled:
             frame[pl.ds(start, 8), :] += block[:8]
             frame[pl.ds(start + 8, rows - 8), :] = block[8:rows]
         else:
             frame[pl.ds(start, rows), :] = block[:rows]
-        filled = start + rows
+        self.filled = start + rows
 
 
 def half_turn(plan, even, odd):
@@ -718,9 +840,9 @@
     odd[pl.ds(final, odd.shape[0] - final), :] = jnp.zeros((odd.shape[0] - final, LANES), FLOAT)
 
 
-def emit_slots(plan, even, odd, slots, values):
+def emit_slots(plan, even, odd, slots, depths):
     rows = plan.rows
-    for index in range(values[0] * 16, values[-1] * 16 + 16):
+    for index in [depth * 8 + number for depth in depths for number in range(8)]:
         start = plan.base(index) // 8 * 8
         if plan.late(index):
             block = odd[pl.ds(start + 8, rows), :]
@@ -728,7 +850,7 @@
             here = pltpu.roll(odd[pl.ds(start + 8, rows), :], 64, 1)
             above = pltpu.roll(odd[pl.ds(start + 7, rows), :], 64, 1)
             block = even[pl.ds(start, rows), :] + jnp.where(lane_iota(rows) < 64, above, here)
-        slots[spot_of(index)] = block.astype(BRAIN)
+        slots[(index // 8, index // 4 % 2, index // 2 % 2, index % 2)] = block.astype(BRAIN)
 
 
 def dot(left, right, dims=(((1,), (0,)), ((), ()))):
@@ -831,21 +953,24 @@
         return self.refs[name][...]
 
 
-def block_ahead(hidden, keep, weights, prefix, heads, usable):
+def block_open(hidden, keep, weights, prefix):
     width = hidden.shape[1]
     keep["x"][...] = hidden
     unit, unused = norm_parts(hidden)
     normed = (unit * weights(prefix + "ln1g") + weights(prefix + "ln1b")).astype(BRAIN)
     keep["a"][...] = normed
     bias = weights(prefix + "qvb")
-    t_ref = keep["t"]
     for part in range(3):
         cols = pl.ds(part * width, width)
         value = dot(normed, weights.refs[prefix + "qkv"][:, cols])
         if part != 1:
             value = value + bias[:, (part // 2) * width : (part // 2 + 1) * width]
-        t_ref[:, cols] = value.astype(BRAIN)
-    mixed = attend(t_ref, keep["p"], usable, width, heads)
+        keep["t"][:, cols] = value.astype(BRAIN)
+
+
+def block_middle(hidden, keep, weights, prefix, heads, usable):
+    width = hidden.shape[1]
+    mixed = attend(keep["t"], keep["p"], usable, width, heads)
     keep["o"][...] = mixed
     middle = hidden + (dot(mixed, weights(prefix + "proj")) + weights(prefix + "projb"))
     keep["m"][...] = middle
@@ -856,16 +981,21 @@
     active, slope = gelu_parts(inner)
     keep["s"][...] = slope
     keep["g"][...] = active.astype(BRAIN)
-    return middle + (dot(keep["g"][...], weights(prefix + "fc2")) + weights(prefix + "fc2b"))
-
-
-def block_home(grad, keep, weights, prefix, heads, sums):
-    width = grad.shape[1]
+
+
+def block_shut(keep, weights, prefix):
+    return keep["m"][...] + (dot(keep["g"][...], weights(prefix + "fc2")) + weights(prefix + "fc2b"))
+
+
+def home_open(grad, keep, weights, prefix):
     d_branch = grad.astype(BRAIN)
     keep["dz"][...] = d_branch
-    d_inner = (dot(d_branch, weights(prefix + "fc2"), PAIR) * keep["s"][...]).astype(BRAIN)
-    keep["du"][...] = d_inner
-    d_second = dot(d_inner, weights(prefix + "fc1"), PAIR)
+    keep["du"][...] = (dot(d_branch, weights(prefix + "fc2"), PAIR) * keep["s"][...]).astype(BRAIN)
+
+
+def home_middle(grad, keep, weights, prefix, heads, sums):
+    width = grad.shape[1]
+    d_second = dot(keep["du"][...], weights(prefix + "fc1"), PAIR)
     d_middle, d_gain, d_shift = norm_back(d_second, keep["m"][...], weights(prefix + "ln2g"))
     sums(prefix + "ln2g", d_gain)
     sums(prefix + "ln2b", d_shift)
@@ -881,50 +1011,49 @@
     return d_middle + d_hidden
 
 
-def kept_shapes(count, rows, width, hidden, heads):
+def kept_shapes(rows, width, hidden, heads):
     return {
-        "x": (False, (rows, width), FLOAT),
-        "a": (True, (rows, width), BRAIN),
-        "t": (False, (rows, 3 * width), BRAIN),
-        "p": (False, (heads, rows, rows), FLOAT),
-        "o": (True, (rows, width), BRAIN),
-        "m": (False, (rows, width), FLOAT),
-        "b": (True, (rows, width), BRAIN),
-        "s": (False, (rows, hidden), FLOAT),
-        "g": (True, (rows, hidden), BRAIN),
-        "dz": (True, (rows, width), BRAIN),
-        "du": (True, (rows, hidden), BRAIN),
-        "dy": (True, (rows, width), BRAIN),
-        "dt": (True, (rows, 3 * width), BRAIN),
+        "x": ((rows, width), FLOAT),
+        "a": ((rows, width), BRAIN),
+        "t": ((rows, 3 * width), BRAIN),
+        "p": ((heads, rows, rows), FLOAT),
+        "o": ((rows, width), BRAIN),
+        "m": ((rows, width), FLOAT),
+        "b": ((rows, width), BRAIN),
+        "s": ((rows, hidden), FLOAT),
+        "g": ((rows, hidden), BRAIN),
+        "dz": ((rows, width), BRAIN),
+        "du": ((rows, hidden), BRAIN),
+        "dy": ((rows, width), BRAIN),
+        "dt": ((rows, 3 * width), BRAIN),
     }
 
 
-def kept_scratch(count, rows, width, hidden, heads):
-    shapes = []
-    for every, shape, kind in kept_shapes(count, rows, width, hidden, heads).values():
-        shapes.append(pltpu.VMEM(((count,) + shape) if every and count > 1 else shape, kind))
-    return shapes
-
-
-def kept_view(refs, count, rows, width, hidden, heads, image=None):
-    view = {}
-    table = kept_shapes(count, rows, width, hidden, heads)
-    for ref, (name, (every, shape, kind)) in zip(refs, table.items()):
-        view[name] = ref.at[image] if every and count > 1 and image is not None else ref
-    return view
-
-
-def block_grads(keep, prefix, emit):
+def kept_scratch(count, *sizes):
+    lead = (count,) if count else ()
+    return [pltpu.VMEM(lead + shape, kind) for shape, kind in kept_shapes(*sizes).values()]
+
+
+def kept_view(refs, image=None):
+    names = kept_shapes(1, 1, 1, 1)
+    return {name: ref if image is None else ref.at[image] for name, ref in zip(names, refs)}
+
+
+LAYERS = {
+    "fc2": ("g", "dz", "fc2b"),
+    "fc1": ("b", "du", "fc1b"),
+    "proj": ("o", "dy", "projb"),
+    "qkv": ("a", "dt", "qvb"),
+}
+
+
+def block_grads(keep, prefix, names, emit):
     def rows_of(name):
         value = keep[name][...]
         return value.reshape(-1, value.shape[-1])
 
-    for left, right, name, bias in (
-        ("g", "dz", "fc2", "fc2b"),
-        ("b", "du", "fc1", "fc1b"),
-        ("o", "dy", "proj", "projb"),
-        ("a", "dt", "qkv", "qvb"),
-    ):
+    for name in names:
+        left, right, bias = LAYERS[name]
         emit(prefix + name, prefix + bias, rows_of(left), rows_of(right))
 
 
@@ -986,10 +1115,11 @@
     slots, seen_ref, tgt_own, tgt_ref, wanted, meta_ref, grad_ref, loss_ref = take(8)
     spot_enc, spot_dec, local = take(3)
     line, rolled, pixels, spare, send, recv, hand, taken = take(8)
-    even, odd, sums_ref, y_hi, y_lo, dy_home, final_all, dpred_all = take(8)
+    even, odd, sums_ref, y_hi, y_lo, dy_home, final_all, dpred_all, d_out = take(9)
     weights = Weights(take(len(names)))
     enc_refs, dec_refs = take(13), take(13)
-    core_in, tree_in, column_in, own_ref, turned, near, far, mine, column_send, column_recv = take(10)
+    core_in, tree_in, column_in, own_ref, turned, near, far, mine = take(8)
+    spread_send, spread_recv, column_send, column_recv = take(4)
 
     place = position()
     device = index_of(place)
@@ -1007,14 +1137,11 @@
     slots[(place["H"], place["L"], place["B"], place["C"], place["r"])] = own_block(
         plan, device, x_ref, line, rolled
     )
-    group, column = partners(place, plan.outer)
-    meet(group + column)
+    meet(gates(place, plan))
     sender = Sender(send, recv)
     handing = Handing(place, spare, seen_ref, meta_ref, targets_ref, tgt_ref, hand, taken)
 
-    def between(stage):
-        if stage:
-            return
+    def choose_images():
         lane = lane_iota(8)
         row = lax.broadcasted_iota(jnp.int32, (8, LANES), 0)
         held = counts_ref[0, 0].astype(FLOAT)
@@ -1035,17 +1162,34 @@
         for image in range(LIVE_CAP):
             seen_ref[image] = visible(image)
 
-    pending = gather_body(plan, place, slots, sender, between)
-    handing.start((2,))
+    early = min(-(-layout()["dec_qkv"][0] // (16 * plan.length)), plan.outer)
+    first_values, last_values = range(early), range(early, plan.outer)
+    gather = Gather(plan, place, slots, sender, (spread_send, spread_recv))
+    frames = Frames(plan, slots, even, odd)
+
+    def spread(values, reach):
+        for value in values:
+            gather.stage(value, reach)
+
+    def fetch(values, wanted_names):
+        for value in values:
+            gather.ready(value)
+            for index in range(value * 16, value * 16 + 16):
+                frames.add(index)
+        for name in wanted_names:
+            read_param(even, odd, name, weights.refs[name])
+
+    gather.begin()
+    gather.roots(choose_images)
+    for reach in (0, 1):
+        spread(first_values, reach)
+        spread(last_values, reach)
+    spread(first_values, 2)
+    divide = names.index("dec_qkv")
+    fetch(first_values, names[:divide])
     handing.receive((0, 1))
     for copy in copies[1:]:
         copy.wait()
-
-    assemble(plan, slots, even, odd)
-    for name in names:
-        read_param(even, odd, name, weights.refs[name])
-    clear_frames(plan, even, odd)
-    view = odd.at[pl.ds(8, plan.frame_rows)]
     sums_ref[...] = jnp.zeros_like(sums_ref)
     order = {name: number for number, name in enumerate(names)}
 
@@ -1063,13 +1207,14 @@
     visible = jnp.concatenate(visible, axis=0)
     begin = jnp.concatenate(begin, axis=0)
     enc_rows = LIVE_CAP * HOME
-    enc_shape = (1, enc_rows, D, FF, HEADS)
-    enc = kept_view(enc_refs, *enc_shape)
+    enc = kept_view(enc_refs)
     down = lax.broadcasted_iota(jnp.int32, (enc_rows, enc_rows), 0)
     over = lax.broadcasted_iota(jnp.int32, (enc_rows, enc_rows), 1)
     usable = (down // HOME == over // HOME) & (down % HOME < VIS)
     first_in = dot(visible, weights("patch")) + weights("patchb") + begin
-    encoded = block_ahead(first_in, enc, weights, "enc_", HEADS, usable)
+    block_open(first_in, enc, weights, "enc_")
+    block_middle(first_in, enc, weights, "enc_", HEADS, usable)
+    encoded = block_shut(enc, weights, "enc_")
     unit, unused = norm_parts(encoded)
     encoder_out = (unit * weights("encg") + weights("encb")).astype(BRAIN)
     embedded = dot(encoder_out, weights("embed")) + weights("embedb")
@@ -1077,19 +1222,34 @@
     for image in range(LIVE_CAP):
         y_hi[image] = upper[image * HOME : (image + 1) * HOME]
         y_lo[image] = lower[image * HOME : (image + 1) * HOME]
-    dec_shape = (LIVE_CAP, ROWS, E, DFF, DHEADS)
+    spread(last_values, 2)
+    handing.start((2,))
+    fetch(last_values, names[divide:])
+    clear_frames(plan, even, odd)
+    view = odd.at[pl.ds(8, plan.frame_rows)]
     real = lax.broadcasted_iota(jnp.int32, (ROWS, 1), 0) < NP
     usable_dec = lax.broadcasted_iota(jnp.int32, (ROWS, ROWS), 0) < NP
 
+    def seen_of(kept):
+        where = placement(kept, ROWS)
+        return where.astype(BRAIN), jnp.sum(where, axis=1, keepdims=True)
+
+    @pl.loop(0, LIVE_CAP)
+    def _(image):
+        source, kept, live = pick(image)
+        where, seen = seen_of(kept)
+        grid_in = dot(where, y_hi[image]) + dot(where, y_lo[image])
+        grid_in = grid_in + (1.0 - seen) * weights("mask") + spot_dec[...]
+        keep = kept_view(dec_refs, image)
+        block_open(grid_in, keep, weights, "dec_")
+        block_middle(grid_in, keep, weights, "dec_", DHEADS, usable_dec)
+
+
     def one_image(image, total):
         source, kept, live = pick(image)
-        where = placement(kept, ROWS)
-        seen = jnp.sum(where, axis=1, keepdims=True)
-        where = where.astype(BRAIN)
-        grid_in = dot(where, y_hi[image]) + dot(where, y_lo[image])
-        grid_in = grid_in + (1.0 - seen) * weights("mask") + spot_dec[...]
-        keep = kept_view(dec_refs, *dec_shape, image)
-        decoded = block_ahead(grid_in, keep, weights, "dec_", DHEADS, usable_dec)
+        where, seen = seen_of(kept)
+        keep = kept_view(dec_refs, image)
+        decoded = block_shut(keep, weights, "dec_")
         unit, unused = norm_parts(decoded)
         final = (unit * weights("decg") + weights("decb")).astype(BRAIN)
         final_all[image] = final
@@ -1114,9 +1274,8 @@
         d_decoded, d_gain, d_shift = norm_back(d_final, decoded, weights("decg"))
         add_sum("decg", d_gain)
         add_sum("decb", d_shift)
-        d_grid = block_home(d_decoded, keep, weights, "dec_", DHEADS, add_sum)
-        add_sum("mask", jnp.sum((1.0 - seen) * d_grid, axis=0, keepdims=True))
-        dy_home[image] = dot(where, d_grid.astype(BRAIN), DEEP).astype(BRAIN)
+        d_out[image] = d_decoded
+        home_open(d_decoded, keep, weights, "dec_")
         return total
 
     total = lax.fori_loop(0, LIVE_CAP, one_image, jnp.zeros((1, PIX), FLOAT))
@@ -1132,51 +1291,85 @@
         turned = left.T
         write_grad(even, view, name, lambda start, size: dot(turned, right[:, start : start + size]))
 
-    def emit_norms(prefixes):
-        for name in names:
-            if name.endswith(NORMS) and name.startswith(prefixes):
-                row = pl.ds(order[name], 1)
-                write_grad(even, view, name, lambda start, size, row=row: sums_ref[row, pl.ds(start, size)])
-
-    d_embedded = dy_home[...].reshape(enc_rows, E)
-    emit("embed", "embedb", encoder_out, d_embedded)
-    block_grads(kept_view(dec_refs, *dec_shape), "dec_", emit)
-    emit("head", "headb", final_all[...].reshape(-1, E), dpred_all[...].reshape(-1, PIX))
-    emit_norms(("dec", "mask"))
-    late_values = list(range(plan.edge, plan.outer))
-    early_values = list(range(plan.edge))
-    emit_slots(plan, even, odd, grad_ref, late_values)
+    def emit_norms(wanted_names):
+        for name in wanted_names:
+            row = pl.ds(order[name], 1)
+            write_grad(even, view, name, lambda start, size, row=row: sums_ref[row, pl.ds(start, size)])
+
     reducer = Reducer(
         plan, place, grad_ref, core_in, tree_in, column_in, own_ref, sender, (column_send, column_recv)
     )
-
-    def stage(values, reach):
-        for value in values:
-            reducer.stage(value, reach)
-
-    for value in late_values:
-        reducer.share(value)
+    floors = [plan.depths_from(name) for name in ("dec_fc2", "embed", "enc_fc1")]
+    waves = [range(low, high) for low, high in zip(floors + [0], [plan.depths] + floors)]
+
+    def leave(wave):
+        emit_slots(plan, even, odd, grad_ref, waves[wave])
+        for depth in waves[wave]:
+            reducer.share(depth)
+
+    def collect(wave, reach):
+        for depth in waves[wave]:
+            reducer.stage(depth, reach)
+
+    dec = kept_view(dec_refs)
+    emit("head", "headb", final_all[...].reshape(-1, E), dpred_all[...].reshape(-1, PIX))
+    block_grads(dec, "dec_", ("fc2",), emit)
+    emit_norms(("decg", "decb"))
+    leave(0)
+    block_grads(dec, "dec_", ("fc1",), emit)
+
+    @pl.loop(0, LIVE_CAP)
+    def _(image):
+        @pl.when(image == 1)
+        def _():
+            collect(0, 1)
+
+        @pl.when(image == 2)
+        def _():
+            collect(0, 0)
+
+        source, kept, live = pick(image)
+        where, seen = seen_of(kept)
+        d_grid = home_middle(
+            d_out[image], kept_view(dec_refs, image), weights, "dec_", DHEADS, add_sum
+        )
+        add_sum("mask", jnp.sum((1.0 - seen) * d_grid, axis=0, keepdims=True))
+        dy_home[image] = dot(where, d_grid.astype(BRAIN), DEEP).astype(BRAIN)
+
+    collect(0, -1)
+    block_grads(dec, "dec_", ("proj", "qkv"), emit)
+    d_embedded = dy_home[...].reshape(enc_rows, E)
+    emit("embed", "embedb", encoder_out, d_embedded)
+    emit_norms(("mask", "dec_ln1g", "dec_ln1b", "dec_ln2g", "dec_ln2b"))
+    leave(1)
+
     d_seen = dot(d_embedded, weights("embed"), PAIR).astype(BRAIN).astype(FLOAT)
     d_encoded, d_gain, d_shift = norm_back(d_seen, encoded, weights("encg"))
     add_sum("encg", d_gain)
     add_sum("encb", d_shift)
-    stage(late_values, 2)
-    d_first = block_home(d_encoded, enc, weights, "enc_", HEADS, add_sum).astype(BRAIN)
-    stage(late_values, 1)
+    home_open(d_encoded, enc, weights, "enc_")
+    block_grads(enc, "enc_", ("fc2", "fc1"), emit)
+    emit_norms(("encg", "encb"))
+    leave(2)
+    collect(1, 1)
+    d_first = home_middle(d_encoded, enc, weights, "enc_", HEADS, add_sum).astype(BRAIN)
+    collect(2, 1)
+    collect(1, 0)
     emit("patch", "patchb", visible, d_first)
-    stage(late_values, 0)
-    block_grads(enc, "enc_", emit)
-    emit_norms(("enc",))
-    stage(late_values, -1)
-    emit_slots(plan, even, odd, grad_ref, early_values)
-    for value in early_values:
-        reducer.share(value)
-    for reach in (2, 1, 0, -1):
-        stage(early_values, reach)
+    block_grads(enc, "enc_", ("proj", "qkv"), emit)
+    emit_norms(("enc_ln1g", "enc_ln1b", "enc_ln2g", "enc_ln2b"))
+    leave(3)
+    collect(2, 0)
+    collect(1, -1)
+    collect(3, 1)
+    collect(2, -1)
+    collect(3, 0)
+    collect(3, -1)
     reducer.finish()
-    pending += finish_body(
+    pending = finish_body(
         plan, place, counts_ref, loss_ref, own_ref, total_out, scalars_out, turned, near, far, mine, sender
     )
+    gather.close()
     reducer.close()
     handing.finish((0, 1, 2))
     for copy in pending:
@@ -1194,14 +1387,13 @@
 
 
 def copies_used(plan):
-    parts = len(plan.parts)
-    spread = parts * (plan.outer - 1) + parts * plan.outer * (7 + 4)
-    home = parts * plan.outer * (1 + 7)
-    return spread + home + 15 + plan.outer - 1
+    spread = len(plan.parts) * plan.outer * (7 + 4)
+    home = len(plan.halves) * plan.depths * (1 + 3)
+    return spread + home + 31 + plan.outer
 
 
 def whole_step(counts, keep, master, patches, targets, plan):
-    outer, rows, lines = plan.outer, plan.rows, plan.lines
+    outer, depths, rows, lines = plan.outer, plan.depths, plan.rows, plan.lines
     vmem = pl.BlockSpec(memory_space=pltpu.VMEM)
     smem = pl.BlockSpec(memory_space=pltpu.SMEM)
     far = pl.BlockSpec(memory_space=pl.ANY)
@@ -1227,7 +1419,7 @@
             pltpu.VMEM((3, NP, PIX), BRAIN),
             pltpu.VMEM((NP, PIX), BRAIN),
             pltpu.VMEM((3, 8, LANES), FLOAT),
-            block,
+            pltpu.VMEM((depths, 2, 2, 2, rows, LANES), BRAIN),
             pltpu.SMEM((1,), FLOAT),
             pltpu.VMEM(spot_enc.shape, BRAIN),
             pltpu.VMEM(spot_dec.shape, FLOAT),
@@ -1248,19 +1440,22 @@
             pltpu.VMEM((LIVE_CAP, HOME, E), BRAIN),
             pltpu.VMEM((LIVE_CAP, ROWS, E), BRAIN),
             pltpu.VMEM((LIVE_CAP, ROWS, PIX), BRAIN),
+            pltpu.VMEM((LIVE_CAP, ROWS, E), FLOAT),
             *weight_scratch(),
-            *kept_scratch(1, LIVE_CAP * HOME, D, FF, HEADS),
+            *kept_scratch(0, LIVE_CAP * HOME, D, FF, HEADS),
             *kept_scratch(LIVE_CAP, ROWS, E, DFF, DHEADS),
-            pltpu.VMEM((outer, 2, 2, 2, rows, LANES), BRAIN),
-            pltpu.VMEM((outer, 8, rows, LANES), BRAIN),
-            pltpu.VMEM((outer, rows, LANES), BRAIN),
+            pltpu.VMEM((depths, 2, 2, rows, LANES), BRAIN),
+            pltpu.VMEM((depths, 4, rows, LANES), BRAIN),
+            pltpu.VMEM((depths, rows, LANES), BRAIN),
             pltpu.VMEM((rows, LANES), FLOAT),
             pltpu.VMEM((rows, LANES), FLOAT),
-            pltpu.VMEM((16, 8, LANES), FLOAT),
+            pltpu.VMEM((32, 8, LANES), FLOAT),
             pltpu.VMEM((outer, 8, LANES), FLOAT),
             pltpu.VMEM((2, 8, LANES), FLOAT),
             dma((outer, len(plan.parts))),
             dma((outer, len(plan.parts))),
+            dma((depths, len(plan.halves))),
+            dma((depths, len(plan.halves))),
         ],
         compiler_params=pltpu.CompilerParams(
             collective_id=0, has_side_effects=True, vmem_limit_bytes=60 << 20

time: 101 us -> 98.9 us (0.979)
  Pallas kernels: 97 us -> 94.9 us
    pallas_call x1, Pallas kernels: 94.8 us -> 92.7 us  [whole_step(): pl.pallas_call(functools.partial(whole_body, plan), out_shape=(jax.ShapeD...]
where the time goes in v3:
time: 98.9 us; the launch traced here: 98.7 us
  Pallas kernels  94.9 us (96%)
  between operations  2.15 us (2%)
  local copies, waits for them, and re-layouts  1.61 us (2%)
    pallas_call x1, Pallas kernels, whole_step(): pl.pallas_call(functools.partial(whole_body, plan), out_shape=(jax.ShapeD...  92.7 us
    pallas_call x1, Pallas kernels, update(): pl.pallas_call(functools.partial(update_body, plan), out_shape=(flat, fla...  2.2 us

profile of v3, /device:TPU:0, one launch (start us, length us, event | category | flops | bytes accessed | tf_op | source)
XLA Modules:
  0.0 98.7 jit_solution(16781572563340464925)
XLA Ops:
  1.9 0.0 copy-start
  1.9 0.0 copy-start.1
  1.9 0.0 copy-start.2
  2.0 92.7 %shard_map.145 = (f32[400,128]{1,0:T(8,128)}, f32[1,128]{1,0:T(1,128)}) custom-call(s32[1,1]{1,0:T(1,128)S(6)} %copy.16.counts_ref, s32[6,49]{1,0:T(8,128)} %keep_ref.1, f32[50930]{0:T(1024)} %master_ref.1, bf16[6,196,768]{2,1,0:T(8,128)(2,1)} %patches_ref.1, bf16[6,196,768]{2,1,0:T(8,128)(2,1)} %targets_ref.1, ...), custom_call_target="tpu_custom_call" | custom-call | tf_op jit(solution)/shard_map/pallas_call | solution.py:1407
  94.7 0.0 copy-done
  94.7 0.0 copy-done.1
  94.7 0.0 copy-done.2
  94.7 0.0 copy-start.3
  94.7 0.9 copy-done.3
  95.7 0.0 copy-start.4
  95.7 0.7 copy-done.4
  96.3 2.2 %shard_map.146 = (f32[50930]{0:T(1024)}, f32[50930]{0:T(1024)}, f32[50930]{0:T(1024)}, bf16[50930]{0:T(1024)(128)(2,1)}, f32[1,1]{1,0:T(1,128)}, /*index=5*/f32[1,1]{1,0:T(1,128)}) custom-call(s32[1]{0:T(128)S(6)} %copy.17.step_ref, f32[400,128]{1,0:T(8,128)S(1)} %copy-done.3, f32[1,128]{1,0:T(1,128)S(1)} %copy-done.4, f32[50930]{0:T(1024)S(1)} %copy-done, ...), custom_call_target="tpu_custom_call" | custom-call | tf_op jit(solution)/shard_map/pallas_call | solution.py:711
Async XLA Ops:
  1.9 92.8 %copy-start = (f32[50930]{0:T(1024)S(1)}, f32[50930]{0:T(1024)}, u32[]{:S(2)}) copy-start(f32[50930]{0:T(1024)} %master_ref.1) | copy-start | bytes 611164
  1.9 92.8 %copy-start.1 = (f32[50930]{0:T(1024)S(1)}, f32[50930]{0:T(1024)}, u32[]{:S(2)}) copy-start(f32[50930]{0:T(1024)} %first_ref.1) | copy-start | bytes 611164
  1.9 92.8 %copy-start.2 = (f32[50930]{0:T(1024)S(1)}, f32[50930]{0:T(1024)}, u32[]{:S(2)}) copy-start(f32[50930]{0:T(1024)} %second_ref.1) | copy-start | bytes 611164
  94.7 0.9 copy-start.3
  95.7 0.7 copy-start.4

commit v4 on v3

--- a/solution.py
+++ b/solution.py
@@ -196,13 +196,9 @@
 
 
 def gates(place, plan):
-    group, column = partners(place, plan.outer)
-    if plan.outer > 2:
-        depth = depth_of(place)
-        column = column + [
-            at_depth(place, lax.rem(depth + step, plan.depths)) for step in range(1, plan.depths)
-        ]
-    return group + column
+    near = [flipped(place, dims) for dims in ("r", "L", "B", "C", "BC")]
+    steps = range(1, plan.outer)
+    return near + [moved(place, "H", lax.rem(place["H"] + step, plan.outer)) for step in steps]
 
 
 def branches(order):
@@ -595,7 +591,7 @@
                     self.column(value, part).wait_send()
 
 
-def finish_body(plan, place, held_ref, loss_ref, own_ref, total_out, scalars_out, turned, near, far, mine, sender):
+def finish_body(plan, place, held_ref, loss_ref, own_ref, total_out, turned, near, far, mine, sender):
     outer, rows, lines = plan.outer, plan.rows, plan.lines
     group, column = partners(place, outer)
     skip, lead = plan.own(index_of(place))
@@ -617,7 +613,7 @@
         sender.start(functools.partial(lambda other: (mine.at[0], near.at[spot], other), other))
         for other in group
     ]
-    total_out[...] = total
+    total_out[pl.ds(0, lines), :] = total
     for copy in nears:
         copy.wait_recv()
     together = near[0]
@@ -639,11 +635,14 @@
             whole = whole + far[other]
     row = whole[0:1, :]
     lane = lane[0:1]
-    held = jnp.sum(jnp.where(lane == 1, row, 0.0))
-    weights = jnp.full((1, LANES), held * (0.1 * VIS + (NP - VIS)))
-    norms = jnp.sqrt(jnp.full((1, LANES), jnp.sum(jnp.where(lane == 0, row, 0.0)))) / weights
-    losses = jnp.full((1, LANES), jnp.sum(jnp.where(lane == 2, row, 0.0))) / weights
-    scalars_out[...] = jnp.where(lane == 0, losses, jnp.where(lane == 1, norms, weights))
+
+    def across(number):
+        return jnp.full((1, LANES), jnp.sum(jnp.where(lane == number, row, 0.0)))
+
+    weights = across(1) * (0.1 * VIS + (NP - VIS))
+    total_out[pl.ds(lines, 1), :] = across(2) / weights
+    total_out[pl.ds(lines + 1, 1), :] = jnp.sqrt(across(0)) / weights
+    total_out[pl.ds(lines + 2, 1), :] = weights
     return nears + fars
 
 
@@ -665,7 +664,7 @@
 
 
 def update_body(
-    plan, step_ref, total_ref, scalars_ref, master_ref, first_ref, second_ref,
+    plan, step_ref, total_ref, master_ref, first_ref, second_ref,
     master_out, first_out, second_out, copy_out, loss_out, norm_out, line
 ):
     rows, length = plan.lines, plan.length
@@ -683,11 +682,10 @@
     first = line[...].reshape(rows, LANES)
     line[pl.ds(0, length)] = second_ref[...]
     second = line[...].reshape(rows, LANES)
-    loss_out[0, 0] = scalars_ref[0, 0]
-    norm_out[0, 0] = scalars_ref[0, 1]
-    norms = jnp.full((1, LANES), scalars_ref[0, 1])
-    weights = jnp.full((1, LANES), scalars_ref[0, 2])
-    gradient = total_ref[...] / weights
+    norms = total_ref[pl.ds(rows + 1, 1), :]
+    loss_out[0, 0] = jnp.max(total_ref[pl.ds(rows, 1), :])
+    norm_out[0, 0] = jnp.max(norms)
+    gradient = total_ref[pl.ds(0, rows), :] / total_ref[pl.ds(rows + 2, 1), :]
     clipped = gradient * jnp.minimum(1.0, CLIP / norms)
     fade = 1.0 / jnp.full((1, LANES), lax.shift_left(1, step_ref[0]).astype(FLOAT))
     new_first = BETA_ONE * first + (1.0 - BETA_ONE) * clipped
@@ -703,7 +701,7 @@
     copy_out[...] = new_master.reshape(rows * LANES)[:length].astype(BRAIN)
 
 
-def update(step, total, scalars, master, first, second, plan):
+def update(step, total, master, first, second, plan):
     vmem = pl.BlockSpec(memory_space=pltpu.VMEM)
     smem = pl.BlockSpec(memory_space=pltpu.SMEM)
     flat = jax.ShapeDtypeStruct((plan.length,), FLOAT)
@@ -711,11 +709,11 @@
     return pl.pallas_call(
         functools.partial(update_body, plan),
         out_shape=(flat, flat, flat, jax.ShapeDtypeStruct((plan.length,), BRAIN), single, single),
-        in_specs=[smem, vmem, smem, vmem, vmem, vmem],
+        in_specs=[smem, vmem, vmem, vmem, vmem],
         out_specs=(vmem, vmem, vmem, vmem, smem, smem),
         scratch_shapes=[pltpu.VMEM((plan.lines * LANES,), FLOAT)],
         compiler_params=pltpu.CompilerParams(vmem_limit_bytes=16 << 20),
-    )(step, total, scalars, master, first, second)
+    )(step, total, master, first, second)
 
 
 class Frames:
@@ -903,15 +901,18 @@
     return jnp.where(inside, value, jnp.zeros_like(value))
 
 
-def attend(t_ref, chance_ref, usable, width, heads):
+def attend(t_ref, chance_ref, stack_ref, usable, width, heads):
     size = width // heads
-    query, keys = t_ref[:, pl.ds(0, width)], t_ref[:, pl.ds(width, width)]
+    rows = t_ref.shape[0]
+    query, keys = t_ref[:, pl.ds(0, width)].T, t_ref[:, pl.ds(width, width)]
     values = t_ref[:, pl.ds(2 * width, width)].T
     factor = size ** (-0.5) * LOG_TWO_E
     mixed = []
     for head in range(heads):
-        raw = dot(head_only(keys, head, size), query, PAIR)
-        raw = jnp.where(usable, raw, -1e30)
+        stack_ref[pl.ds(head * rows, rows), :] = head_only(keys, head, size)
+    scores = dot(stack_ref[...], query)
+    for head in range(heads):
+        raw = jnp.where(usable, scores[head * rows : (head + 1) * rows], -1e30)
         top = jnp.max(raw, axis=0, keepdims=True)
         power = jnp.exp2((raw - top) * factor)
         chance = power * (1.0 / jnp.sum(power, axis=0, keepdims=True))
@@ -920,25 +921,27 @@
     return jnp.concatenate(mixed, axis=0).astype(BRAIN).T
 
 
-def attend_back(d_mixed, t_ref, dt_ref, chance_ref, width, heads):
+def attend_back(d_mixed, t_ref, dt_ref, chance_ref, stack_ref, width, heads):
     size = width // heads
+    rows = t_ref.shape[0]
     scale = size ** (-0.5)
-    query, keys = t_ref[:, pl.ds(0, width)], t_ref[:, pl.ds(width, width)]
+    query, keys = t_ref[:, pl.ds(0, width)], t_ref[:, pl.ds(width, width)].T
     values = t_ref[:, pl.ds(2 * width, width)]
-    across = keys.T
     d_query = []
     d_keys = d_values = None
     for head in range(heads):
+        stack_ref[pl.ds(head * rows, rows), :] = head_only(values, head, size)
+    d_chances = dot(stack_ref[...], d_mixed.T)
+    for head in range(heads):
         chance = chance_ref[head]
-        d_here = head_only(d_mixed, head, size)
-        d_chance = dot(head_only(values, head, size), d_mixed, PAIR)
+        d_chance = d_chances[head * rows : (head + 1) * rows]
         along = jnp.sum(chance * d_chance, axis=0, keepdims=True)
         d_scores = (chance * (d_chance - along)).astype(BRAIN)
-        part = dot(chance.astype(BRAIN), d_here)
+        part = dot(chance.astype(BRAIN), head_only(d_mixed, head, size))
         d_values = part if d_values is None else d_values + part
         part = dot(d_scores, head_only(query, head, size))
         d_keys = part if d_keys is None else d_keys + part
-        d_query.append(dot(across[head * size : (head + 1) * size], d_scores))
+        d_query.append(dot(keys[head * size : (head + 1) * size], d_scores))
     d_query = (jnp.concatenate(d_query, axis=0) * scale).astype(BRAIN).T
     dt_ref[:, pl.ds(0, width)] = d_query
     dt_ref[:, pl.ds(width, width)] = (d_keys * scale).astype(BRAIN)
@@ -970,7 +973,7 @@
 
 def block_middle(hidden, keep, weights, prefix, heads, usable):
     width = hidden.shape[1]
-    mixed = attend(keep["t"], keep["p"], usable, width, heads)
+    mixed = attend(keep["t"], keep["p"], keep["k"], usable, width, heads)
     keep["o"][...] = mixed
     middle = hidden + (dot(mixed, weights(prefix + "proj")) + weights(prefix + "projb"))
     keep["m"][...] = middle
@@ -1003,7 +1006,7 @@
     d_output = d_middle.astype(BRAIN)
     keep["dy"][...] = d_output
     d_mixed = dot(d_output, weights(prefix + "proj"), PAIR).astype(BRAIN)
-    attend_back(d_mixed, keep["t"], keep["dt"], keep["p"], width, heads)
+    attend_back(d_mixed, keep["t"], keep["dt"], keep["p"], keep["k"], width, heads)
     d_normed = dot(keep["dt"][...], weights(prefix + "qkv"), PAIR)
     d_hidden, d_gain, d_shift = norm_back(d_normed, keep["x"][...], weights(prefix + "ln1g"))
     sums(prefix + "ln1g", d_gain)
@@ -1017,6 +1020,7 @@
         "a": ((rows, width), BRAIN),
         "t": ((rows, 3 * width), BRAIN),
         "p": ((heads, rows, rows), FLOAT),
+        "k": ((heads * rows, width), BRAIN),
         "o": ((rows, width), BRAIN),
         "m": ((rows, width), FLOAT),
         "b": ((rows, width), BRAIN),
@@ -1031,12 +1035,17 @@
 
 def kept_scratch(count, *sizes):
     lead = (count,) if count else ()
-    return [pltpu.VMEM(lead + shape, kind) for shape, kind in kept_shapes(*sizes).values()]
+    return [
+        pltpu.VMEM(shape if name == "k" else lead + shape, kind)
+        for name, (shape, kind) in kept_shapes(*sizes).items()
+    ]
 
 
 def kept_view(refs, image=None):
     names = kept_shapes(1, 1, 1, 1)
-    return {name: ref if image is None else ref.at[image] for name, ref in zip(names, refs)}
+    return {
+        name: ref if image is None or name == "k" else ref.at[image] for name, ref in zip(names, refs)
+    }
 
 
 LAYERS = {
@@ -1102,7 +1111,7 @@
 
 def whole_body(
     plan, counts_ref, keep_ref, x_ref, patches_ref, targets_ref, enc_table, dec_table,
-    total_out, scalars_out, *scratch
+    total_out, *scratch
 ):
     scratch = list(scratch)
 
@@ -1117,7 +1126,7 @@
     line, rolled, pixels, spare, send, recv, hand, taken = take(8)
     even, odd, sums_ref, y_hi, y_lo, dy_home, final_all, dpred_all, d_out = take(9)
     weights = Weights(take(len(names)))
-    enc_refs, dec_refs = take(13), take(13)
+    enc_refs, dec_refs = take(14), take(14)
     core_in, tree_in, column_in, own_ref, turned, near, far, mine = take(8)
     spread_send, spread_recv, column_send, column_recv = take(4)
 
@@ -1367,7 +1376,7 @@
     collect(3, -1)
     reducer.finish()
     pending = finish_body(
-        plan, place, counts_ref, loss_ref, own_ref, total_out, scalars_out, turned, near, far, mine, sender
+        plan, place, counts_ref, loss_ref, own_ref, total_out, turned, near, far, mine, sender
     )
     gather.close()
     reducer.close()
@@ -1406,12 +1415,9 @@
     copies = copies_used(plan)
     return pl.pallas_call(
         functools.partial(whole_body, plan),
-        out_shape=(
-            jax.ShapeDtypeStruct((lines, LANES), FLOAT),
-            jax.ShapeDtypeStruct((1, LANES), FLOAT),
-        ),
+        out_shape=jax.ShapeDtypeStruct((lines + 8, LANES), FLOAT),
         in_specs=[smem, vmem, vmem, far, far, far, far],
-        out_specs=(vmem, vmem),
+        out_specs=vmem,
         scratch_shapes=[
             block,
             pltpu.VMEM((5, HOME, PIX), BRAIN),
@@ -1465,8 +1471,8 @@
 
 def on_device(patches, targets, keep, counts, step, master, first, second):
     plan = Plan(master.shape[0], lax.axis_size(("dp", "rep")))
-    total, scalars = whole_step(counts, keep, master, patches, targets, plan)
-    outs = update(step, total, scalars, master, first, second, plan)
+    total = whole_step(counts, keep, master, patches, targets, plan)
+    outs = update(step, total, master, first, second, plan)
     return (*outs[:4], outs[4].reshape(()), outs[5].reshape(()))
 
 

time: 98.9 us -> 94.4 us (0.954)
  Pallas kernels: 94.9 us -> 91.1 us
    pallas_call x1, Pallas kernels: 92.7 us -> 89.4 us  [whole_step(): pl.pallas_call(functools.partial(whole_body, plan), out_shape=jax.ShapeDt...]
where the time goes in v4:
time: 94.4 us; the launch traced here: 94.2 us
  Pallas kernels  91.1 us (97%)
  between operations  2.15 us (2%)
    pallas_call x1, Pallas kernels, whole_step(): pl.pallas_call(functools.partial(whole_body, plan), out_shape=jax.ShapeDt...  89.4 us

profile of v4, /device:TPU:0, one launch (start us, length us, event | category | flops | bytes accessed | tf_op | source)
XLA Modules:
  0.0 94.2 jit_solution(16117656233232307957)
XLA Ops:
  1.9 0.0 copy-start.1
  1.9 0.0 copy-start.2
  1.9 0.0 copy-start.3
  2.0 89.4 %shard_map.145.total_ref = f32[408,128]{1,0:T(8,128)} custom-call(s32[1,1]{1,0:T(1,128)S(6)} %copy.16.counts_ref, s32[6,49]{1,0:T(8,128)} %keep_ref.1, f32[50930]{0:T(1024)} %master_ref.1, bf16[6,196,768]{2,1,0:T(8,128)(2,1)} %patches_ref.1, bf16[6,196,768]{2,1,0:T(8,128)(2,1)} %targets_ref.1, bf16[2,208,192]{2,1,0:T(8,128)(2,1)} %constant.4.clone.enc_table, ...), custom_call_target="tpu_custom_call" | custom-call | tf_op jit(solution)/shard_map/pallas_call | solution.py:1416
  91.4 0.0 copy-done.1
  91.4 0.0 copy-done.2
  91.4 0.0 copy-done.3
  91.4 0.0 copy-start
  91.4 0.9 copy-done
  92.4 1.7 %shard_map.146 = (f32[50930]{0:T(1024)}, f32[50930]{0:T(1024)}, f32[50930]{0:T(1024)}, bf16[50930]{0:T(1024)(128)(2,1)}, f32[1,1]{1,0:T(1,128)}, /*index=5*/f32[1,1]{1,0:T(1,128)}) custom-call(s32[1]{0:T(128)S(6)} %copy.17.step_ref, f32[408,128]{1,0:T(8,128)S(1)} %copy-done, f32[50930]{0:T(1024)S(1)} %copy-done.1, f32[50930]{0:T(1024)S(1)} %copy-done.2, ...), custom_call_target="tpu_custom_call" | custom-call | tf_op jit(solution)/shard_map/pallas_call | solution.py:709
Async XLA Ops:
  1.9 89.5 %copy-start.1 = (f32[50930]{0:T(1024)S(1)}, f32[50930]{0:T(1024)}, u32[]{:S(2)}) copy-start(f32[50930]{0:T(1024)} %master_ref.1) | copy-start | bytes 611164
  1.9 89.5 %copy-start.2 = (f32[50930]{0:T(1024)S(1)}, f32[50930]{0:T(1024)}, u32[]{:S(2)}) copy-start(f32[50930]{0:T(1024)} %first_ref.1) | copy-start | bytes 611164
  1.9 89.5 %copy-start.3 = (f32[50930]{0:T(1024)S(1)}, f32[50930]{0:T(1024)}, u32[]{:S(2)}) copy-start(f32[50930]{0:T(1024)} %second_ref.1) | copy-start | bytes 611164
  91.4 0.9 copy-start

commit v5 on v4

--- a/solution.py
+++ b/solution.py
@@ -100,11 +100,9 @@
         if self.outer > 2:
             self.parts, self.orders = ((0, self.rows),), ("LCB",)
         else:
-            units = self.rows // 16
-            first, second = round(0.385 * units), round(0.346 * units)
-            sizes = (first * 16, second * 16, (units - first - second) * 16)
-            self.parts = ((0, sizes[0]), (sizes[0], sizes[1]), (sizes[0] + sizes[1], sizes[2]))
-            self.orders = ("LCB", "BLC", "CBL")
+            half = self.rows // 32 * 16
+            self.parts = ((0, half), (half, self.rows - half))
+            self.orders = ("LCB", "BCL")
         self.first_late = -(-self.split // length)
         self.depths = count // 8
         pieces = 4 if self.outer == 2 else 1
@@ -176,14 +174,12 @@
     pl.semaphore_wait(barrier, len(places))
 
 
-def partners(place, outer):
-    digits = "rCBLH" if outer == 2 else "rCBL"
+def partners(place, plan):
     group = []
-    for number in range(1, 1 << len(digits)):
-        group.append(flipped(place, [dim for bit, dim in enumerate(digits) if number >> bit & 1]))
-    column = []
-    if outer > 2:
-        column = [moved(place, "H", lax.rem(place["H"] + step, outer)) for step in range(1, outer)]
+    for number in range(1, 8):
+        group.append(flipped(place, [dim for bit, dim in enumerate("rCB") if number >> bit & 1]))
+    depth = depth_of(place)
+    column = [at_depth(place, lax.rem(depth + step, plan.depths)) for step in range(1, plan.depths)]
     return group, column
 
 
@@ -592,8 +588,8 @@
 
 
 def finish_body(plan, place, held_ref, loss_ref, own_ref, total_out, turned, near, far, mine, sender):
-    outer, rows, lines = plan.outer, plan.rows, plan.lines
-    group, column = partners(place, outer)
+    rows, lines = plan.rows, plan.lines
+    group, column = partners(place, plan)
     skip, lead = plan.own(index_of(place))
     position_in = lax.broadcasted_iota(jnp.int32, (lines, LANES), 0) * LANES + lane_iota(lines)
     shift = lax.rem(LANES - lead, LANES)
@@ -619,20 +615,18 @@
     together = near[0]
     for other in range(1, count):
         together = together + near[other]
-    fars = []
-    whole = together
-    if column:
-        far[place["H"]] = together
-        mine[1] = together
-        fars = [
-            sender.start(functools.partial(lambda other: (mine.at[1], far.at[place["H"]], other), other))
-            for other in column
-        ]
-        for copy in fars:
-            copy.wait_recv()
-        whole = far[0]
-        for other in range(1, outer):
-            whole = whole + far[other]
+    depth = depth_of(place)
+    far[depth] = together
+    mine[1] = together
+    fars = [
+        sender.start(functools.partial(lambda other: (mine.at[1], far.at[depth], other), other))
+        for other in column
+    ]
+    for copy in fars:
+        copy.wait_recv()
+    whole = far[0]
+    for other in range(1, plan.depths):
+        whole = whole + far[other]
     row = whole[0:1, :]
     lane = lane[0:1]
 
@@ -971,11 +965,25 @@
         keep["t"][:, cols] = value.astype(BRAIN)
 
 
+def each_group(keep, act):
+    count, rows = keep["p"].shape[0], keep["p"].shape[2]
+    if count == 1:
+        act(0, pl.ds(0, rows))
+        return
+
+    @pl.loop(0, count)
+    def _(group):
+        act(group, pl.ds(pl.multiple_of(group * rows, rows), rows))
+
+
 def block_middle(hidden, keep, weights, prefix, heads, usable):
     width = hidden.shape[1]
-    mixed = attend(keep["t"], keep["p"], keep["k"], usable, width, heads)
-    keep["o"][...] = mixed
-    middle = hidden + (dot(mixed, weights(prefix + "proj")) + weights(prefix + "projb"))
+
+    def mix(group, rows):
+        keep["o"][rows, :] = attend(keep["t"].at[rows], keep["p"].at[group], keep["k"], usable, width, heads)
+
+    each_group(keep, mix)
+    middle = hidden + (dot(keep["o"][...], weights(prefix + "proj")) + weights(prefix + "projb"))
     keep["m"][...] = middle
     unit, unused = norm_parts(middle)
     second = (unit * weights(prefix + "ln2g") + weights(prefix + "ln2b")).astype(BRAIN)
@@ -996,7 +1004,7 @@
     keep["du"][...] = (dot(d_branch, weights(prefix + "fc2"), PAIR) * keep["s"][...]).astype(BRAIN)
 
 
-def home_middle(grad, keep, weights, prefix, heads, sums):
+def home_middle(grad, keep, weights, prefix, heads, sums, meanwhile=None):
     width = grad.shape[1]
     d_second = dot(keep["du"][...], weights(prefix + "fc1"), PAIR)
     d_middle, d_gain, d_shift = norm_back(d_second, keep["m"][...], weights(prefix + "ln2g"))
@@ -1005,8 +1013,17 @@
     d_middle = d_middle + grad
     d_output = d_middle.astype(BRAIN)
     keep["dy"][...] = d_output
-    d_mixed = dot(d_output, weights(prefix + "proj"), PAIR).astype(BRAIN)
-    attend_back(d_mixed, keep["t"], keep["dt"], keep["p"], keep["k"], width, heads)
+    keep["do"][...] = dot(d_output, weights(prefix + "proj"), PAIR).astype(BRAIN)
+
+    def unmix(group, rows):
+        if meanwhile is not None:
+            meanwhile(group)
+        d_mixed = keep["do"][rows, :]
+        attend_back(
+            d_mixed, keep["t"].at[rows], keep["dt"].at[rows], keep["p"].at[group], keep["k"], width, heads
+        )
+
+    each_group(keep, unmix)
     d_normed = dot(keep["dt"][...], weights(prefix + "qkv"), PAIR)
     d_hidden, d_gain, d_shift = norm_back(d_normed, keep["x"][...], weights(prefix + "ln1g"))
     sums(prefix + "ln1g", d_gain)
@@ -1014,38 +1031,33 @@
     return d_middle + d_hidden
 
 
-def kept_shapes(rows, width, hidden, heads):
+def kept_shapes(groups, rows, width, hidden, heads):
+    every = groups * rows
     return {
-        "x": ((rows, width), FLOAT),
-        "a": ((rows, width), BRAIN),
-        "t": ((rows, 3 * width), BRAIN),
-        "p": ((heads, rows, rows), FLOAT),
+        "x": ((every, width), FLOAT),
+        "a": ((every, width), BRAIN),
+        "t": ((every, 3 * width), BRAIN),
+        "p": ((groups, heads, rows, rows), FLOAT),
         "k": ((heads * rows, width), BRAIN),
-        "o": ((rows, width), BRAIN),
-        "m": ((rows, width), FLOAT),
-        "b": ((rows, width), BRAIN),
-        "s": ((rows, hidden), FLOAT),
-        "g": ((rows, hidden), BRAIN),
-        "dz": ((rows, width), BRAIN),
-        "du": ((rows, hidden), BRAIN),
-        "dy": ((rows, width), BRAIN),
-        "dt": ((rows, 3 * width), BRAIN),
+        "o": ((every, width), BRAIN),
+        "m": ((every, width), FLOAT),
+        "b": ((every, width), BRAIN),
+        "s": ((every, hidden), FLOAT),
+        "g": ((every, hidden), BRAIN),
+        "dz": ((every, width), BRAIN),
+        "du": ((every, hidden), BRAIN),
+        "dy": ((every, width), BRAIN),
+        "do": ((every, width), BRAIN),
+        "dt": ((every, 3 * width), BRAIN),
     }
 
 
-def kept_scratch(count, *sizes):
-    lead = (count,) if count else ()
-    return [
-        pltpu.VMEM(shape if name == "k" else lead + shape, kind)
-        for name, (shape, kind) in kept_shapes(*sizes).items()
-    ]
-
-
-def kept_view(refs, image=None):
-    names = kept_shapes(1, 1, 1, 1)
-    return {
-        name: ref if image is None or name == "k" else ref.at[image] for name, ref in zip(names, refs)
-    }
+def kept_scratch(*sizes):
+    return [pltpu.VMEM(shape, kind) for shape, kind in kept_shapes(*sizes).values()]
+
+
+def kept_view(refs):
+    return dict(zip(kept_shapes(1, 1, 1, 1, 1), refs))
 
 
 LAYERS = {
@@ -1057,13 +1069,9 @@
 
 
 def block_grads(keep, prefix, names, emit):
-    def rows_of(name):
-        value = keep[name][...]
-        return value.reshape(-1, value.shape[-1])
-
     for name in names:
         left, right, bias = LAYERS[name]
-        emit(prefix + name, prefix + bias, rows_of(left), rows_of(right))
+        emit(prefix + name, prefix + bias, keep[left][...], keep[right][...])
 
 
 NORMS = ("ln1g", "ln1b", "ln2g", "ln2b", "encg", "encb", "decg", "decb", "mask")
@@ -1121,12 +1129,12 @@
         return taken
 
     names = list(layout())
-    slots, seen_ref, tgt_own, tgt_ref, wanted, meta_ref, grad_ref, loss_ref = take(8)
+    slots, seen_ref, tgt_own, tgt_ref, meta_ref, grad_ref, loss_ref = take(7)
     spot_enc, spot_dec, local = take(3)
     line, rolled, pixels, spare, send, recv, hand, taken = take(8)
-    even, odd, sums_ref, y_hi, y_lo, dy_home, final_all, dpred_all, d_out = take(9)
+    even, odd, sums_ref, y_hi, y_lo, dy_home, final_all, dpred_all = take(8)
     weights = Weights(take(len(names)))
-    enc_refs, dec_refs = take(14), take(14)
+    enc_refs, dec_refs = take(15), take(15)
     core_in, tree_in, column_in, own_ref, turned, near, far, mine = take(8)
     spread_send, spread_recv, column_send, column_recv = take(4)
 
@@ -1194,6 +1202,8 @@
         spread(first_values, reach)
         spread(last_values, reach)
     spread(first_values, 2)
+    spread(last_values, 2)
+    handing.start((2,))
     divide = names.index("dec_qkv")
     fetch(first_values, names[:divide])
     handing.receive((0, 1))
@@ -1231,63 +1241,52 @@
     for image in range(LIVE_CAP):
         y_hi[image] = upper[image * HOME : (image + 1) * HOME]
         y_lo[image] = lower[image * HOME : (image + 1) * HOME]
-    spread(last_values, 2)
-    handing.start((2,))
     fetch(last_values, names[divide:])
     clear_frames(plan, even, odd)
     view = odd.at[pl.ds(8, plan.frame_rows)]
     real = lax.broadcasted_iota(jnp.int32, (ROWS, 1), 0) < NP
     usable_dec = lax.broadcasted_iota(jnp.int32, (ROWS, ROWS), 0) < NP
 
-    def seen_of(kept):
+    dec = kept_view(dec_refs)
+    dec_rows = [pl.ds(image * ROWS, ROWS) for image in range(LIVE_CAP)]
+    wheres, seens, lives = [], [], []
+    for image in range(LIVE_CAP):
+        source, kept, live = pick(image)
         where = placement(kept, ROWS)
-        return where.astype(BRAIN), jnp.sum(where, axis=1, keepdims=True)
-
-    @pl.loop(0, LIVE_CAP)
-    def _(image):
-        source, kept, live = pick(image)
-        where, seen = seen_of(kept)
-        grid_in = dot(where, y_hi[image]) + dot(where, y_lo[image])
-        grid_in = grid_in + (1.0 - seen) * weights("mask") + spot_dec[...]
-        keep = kept_view(dec_refs, image)
-        block_open(grid_in, keep, weights, "dec_")
-        block_middle(grid_in, keep, weights, "dec_", DHEADS, usable_dec)
-
-
-    def one_image(image, total):
-        source, kept, live = pick(image)
-        where, seen = seen_of(kept)
-        keep = kept_view(dec_refs, image)
-        decoded = block_shut(keep, weights, "dec_")
-        unit, unused = norm_parts(decoded)
-        final = (unit * weights("decg") + weights("decb")).astype(BRAIN)
-        final_all[image] = final
-        predicted = dot(final, weights("head")) + weights("headb")
-        weight = jnp.where(real, (1.0 - 0.9 * seen) * live, 0.0)
-
-        @pl.when(image == LIVE_CAP - 1)
-        def _():
-            handing.receive((2,))
-            wanted[...] = tgt_ref[pick.third - 2]
-
-        @pl.when(image < LIVE_CAP - 1)
-        def _():
-            wanted[...] = tgt_own[image]
-
-        error = predicted[:NP] - wanted[...].astype(FLOAT)
+        wheres.append(where.astype(BRAIN))
+        seens.append(jnp.sum(where, axis=1, keepdims=True))
+        lives.append(live)
+
+    def unseen(image):
+        return 1.0 - seens[image]
+
+    grid_in = []
+    for image in range(LIVE_CAP):
+        where = wheres[image]
+        value = dot(where, y_hi[image]) + dot(where, y_lo[image])
+        grid_in.append(value + unseen(image) * weights("mask") + spot_dec[...])
+    grid_in = jnp.concatenate(grid_in, axis=0)
+    block_open(grid_in, dec, weights, "dec_")
+    block_middle(grid_in, dec, weights, "dec_", DHEADS, usable_dec)
+    decoded = block_shut(dec, weights, "dec_")
+    unit, unused = norm_parts(decoded)
+    final_all[...] = (unit * weights("decg") + weights("decb")).astype(BRAIN)
+    handing.receive((2,))
+    total = jnp.zeros((1, PIX), FLOAT)
+    for image in range(LIVE_CAP):
+        predicted = dot(final_all[dec_rows[image], :], weights("head")) + weights("headb")
+        weight = jnp.where(real, (1.0 - 0.9 * seens[image]) * lives[image], 0.0)
+        wanted = tgt_ref[pick.third - 2] if image == LIVE_CAP - 1 else tgt_own[image]
+        error = predicted[:NP] - wanted.astype(FLOAT)
         weighted = error * weight[:NP]
         total = total + jnp.sum(weighted * error, axis=0, keepdims=True)
-        dpred_all[image, pl.ds(0, NP)] = (weighted * (2.0 / PIX)).astype(BRAIN)
-        dpred_all[image, pl.ds(NP, ROWS - NP)] = jnp.zeros((ROWS - NP, PIX), BRAIN)
-        d_final = dot(dpred_all[image], weights("head"), PAIR)
-        d_decoded, d_gain, d_shift = norm_back(d_final, decoded, weights("decg"))
-        add_sum("decg", d_gain)
-        add_sum("decb", d_shift)
-        d_out[image] = d_decoded
-        home_open(d_decoded, keep, weights, "dec_")
-        return total
-
-    total = lax.fori_loop(0, LIVE_CAP, one_image, jnp.zeros((1, PIX), FLOAT))
+        dpred_all[pl.ds(image * ROWS, NP), :] = (weighted * (2.0 / PIX)).astype(BRAIN)
+        dpred_all[pl.ds(image * ROWS + NP, ROWS - NP), :] = jnp.zeros((ROWS - NP, PIX), BRAIN)
+    d_final = dot(dpred_all[...], weights("head"), PAIR)
+    d_decoded, d_gain, d_shift = norm_back(d_final, decoded, weights("decg"))
+    add_sum("decg", d_gain)
+    add_sum("decb", d_shift)
+    home_open(d_decoded, dec, weights, "dec_")
     loss_ref[0] = jnp.sum(total) * (1.0 / PIX)
 
     def emit(name, bias, left, right):
@@ -1320,31 +1319,28 @@
         for depth in waves[wave]:
             reducer.stage(depth, reach)
 
-    dec = kept_view(dec_refs)
-    emit("head", "headb", final_all[...].reshape(-1, E), dpred_all[...].reshape(-1, PIX))
+    emit("head", "headb", final_all[...], dpred_all[...])
     block_grads(dec, "dec_", ("fc2",), emit)
     emit_norms(("decg", "decb"))
     leave(0)
     block_grads(dec, "dec_", ("fc1",), emit)
 
-    @pl.loop(0, LIVE_CAP)
-    def _(image):
-        @pl.when(image == 1)
+    def meanwhile(group):
+        @pl.when(group == 1)
         def _():
             collect(0, 1)
 
-        @pl.when(image == 2)
+        @pl.when(group == 2)
         def _():
             collect(0, 0)
 
-        source, kept, live = pick(image)
-        where, seen = seen_of(kept)
-        d_grid = home_middle(
-            d_out[image], kept_view(dec_refs, image), weights, "dec_", DHEADS, add_sum
-        )
-        add_sum("mask", jnp.sum((1.0 - seen) * d_grid, axis=0, keepdims=True))
-        dy_home[image] = dot(where, d_grid.astype(BRAIN), DEEP).astype(BRAIN)
-
+    d_grid = home_middle(d_decoded, dec, weights, "dec_", DHEADS, add_sum, meanwhile)
+    d_mask = jnp.zeros((1, E), FLOAT)
+    for image in range(LIVE_CAP):
+        part = d_grid[image * ROWS : (image + 1) * ROWS]
+        d_mask = d_mask + jnp.sum(unseen(image) * part, axis=0, keepdims=True)
+        dy_home[image] = dot(wheres[image], part.astype(BRAIN), DEEP).astype(BRAIN)
+    add_sum("mask", d_mask)
     collect(0, -1)
     block_grads(dec, "dec_", ("proj", "qkv"), emit)
     d_embedded = dy_home[...].reshape(enc_rows, E)
@@ -1398,7 +1394,7 @@
 def copies_used(plan):
     spread = len(plan.parts) * plan.outer * (7 + 4)
     home = len(plan.halves) * plan.depths * (1 + 3)
-    return spread + home + 31 + plan.outer
+    return spread + home + 7 + plan.depths
 
 
 def whole_step(counts, keep, master, patches, targets, plan):
@@ -1423,7 +1419,6 @@
             pltpu.VMEM((5, HOME, PIX), BRAIN),
             pltpu.VMEM((LIVE_CAP - 1, NP, PIX), BRAIN),
             pltpu.VMEM((3, NP, PIX), BRAIN),
-            pltpu.VMEM((NP, PIX), BRAIN),
             pltpu.VMEM((3, 8, LANES), FLOAT),
             pltpu.VMEM((depths, 2, 2, 2, rows, LANES), BRAIN),
             pltpu.SMEM((1,), FLOAT),
@@ -1444,19 +1439,18 @@
             pltpu.VMEM((LIVE_CAP, HOME, E), BRAIN),
             pltpu.VMEM((LIVE_CAP, HOME, E), BRAIN),
             pltpu.VMEM((LIVE_CAP, HOME, E), BRAIN),
-            pltpu.VMEM((LIVE_CAP, ROWS, E), BRAIN),
-            pltpu.VMEM((LIVE_CAP, ROWS, PIX), BRAIN),
-            pltpu.VMEM((LIVE_CAP, ROWS, E), FLOAT),
+            pltpu.VMEM((LIVE_CAP * ROWS, E), BRAIN),
+            pltpu.VMEM((LIVE_CAP * ROWS, PIX), BRAIN),
             *weight_scratch(),
-            *kept_scratch(0, LIVE_CAP * HOME, D, FF, HEADS),
+            *kept_scratch(1, LIVE_CAP * HOME, D, FF, HEADS),
             *kept_scratch(LIVE_CAP, ROWS, E, DFF, DHEADS),
             pltpu.VMEM((depths, 2, 2, rows, LANES), BRAIN),
             pltpu.VMEM((depths, 4, rows, LANES), BRAIN),
             pltpu.VMEM((depths, rows, LANES), BRAIN),
             pltpu.VMEM((rows, LANES), FLOAT),
             pltpu.VMEM((rows, LANES), FLOAT),
-            pltpu.VMEM((32, 8, LANES), FLOAT),
-            pltpu.VMEM((outer, 8, LANES), FLOAT),
+            pltpu.VMEM((8, 8, LANES), FLOAT),
+            pltpu.VMEM((depths, 8, LANES), FLOAT),
             pltpu.VMEM((2, 8, LANES), FLOAT),
             dma((outer, len(plan.parts))),
             dma((outer, len(plan.parts))),

time: 94.4 us -> 86.7 us (0.918)
  Pallas kernels: 91.1 us -> 83.4 us
    pallas_call x1, Pallas kernels: 89.4 us -> 81.7 us  [whole_step(): pl.pallas_call(functools.partial(whole_body, plan), out_shape=jax.ShapeDt...]
where the time goes in v5:
time: 86.7 us; the launch traced here: 86.5 us
  Pallas kernels  83.4 us (96%)
  between operations  2.15 us (2%)
  local copies, waits for them, and re-layouts  0.94 us (1%)
    pallas_call x1, Pallas kernels, whole_step(): pl.pallas_call(functools.partial(whole_body, plan), out_shape=jax.ShapeDt...  81.7 us

profile of v5, /device:TPU:0, one launch (start us, length us, event | category | flops | bytes accessed | tf_op | source)
XLA Modules:
  0.0 86.5 jit_solution(9257171497701049852)
XLA Ops:
  1.9 0.0 copy-start.1
  1.9 0.0 copy-start.2
  1.9 0.0 copy-start.3
  2.0 81.7 %shard_map.145.total_ref = f32[408,128]{1,0:T(8,128)} custom-call(s32[1,1]{1,0:T(1,128)S(6)} %copy.16.counts_ref, s32[6,49]{1,0:T(8,128)} %keep_ref.1, f32[50930]{0:T(1024)} %master_ref.1, bf16[6,196,768]{2,1,0:T(8,128)(2,1)} %patches_ref.1, bf16[6,196,768]{2,1,0:T(8,128)(2,1)} %targets_ref.1, bf16[2,208,192]{2,1,0:T(8,128)(2,1)} %constant.4.clone.enc_table, ...), custom_call_target="tpu_custom_call" | custom-call | tf_op jit(solution)/shard_map/pallas_call | solution.py:1412
  83.7 0.0 copy-done.1
  83.7 0.0 copy-done.2
  83.7 0.0 copy-done.3
  83.7 0.0 copy-start
  83.7 0.9 %copy-done = f32[408,128]{1,0:T(8,128)S(1)} copy-done((f32[408,128]{1,0:T(8,128)S(1)}, f32[408,128]{1,0:T(8,128)}, u32[]{:S(2)}) %copy-start) | copy-done | bytes 208920
  84.7 1.7 %shard_map.146 = (f32[50930]{0:T(1024)}, f32[50930]{0:T(1024)}, f32[50930]{0:T(1024)}, bf16[50930]{0:T(1024)(128)(2,1)}, f32[1,1]{1,0:T(1,128)}, /*index=5*/f32[1,1]{1,0:T(1,128)}) custom-call(s32[1]{0:T(128)S(6)} %copy.17.step_ref, f32[408,128]{1,0:T(8,128)S(1)} %copy-done, f32[50930]{0:T(1024)S(1)} %copy-done.1, f32[50930]{0:T(1024)S(1)} %copy-done.2, ...), custom_call_target="tpu_custom_call" | custom-call | tf_op jit(solution)/shard_map/pallas_call | solution.py:703
Async XLA Ops:
  1.9 81.8 %copy-start.1 = (f32[50930]{0:T(1024)S(1)}, f32[50930]{0:T(1024)}, u32[]{:S(2)}) copy-start(f32[50930]{0:T(1024)} %master_ref.1) | copy-start | bytes 611164
  1.9 81.8 %copy-start.2 = (f32[50930]{0:T(1024)S(1)}, f32[50930]{0:T(1024)}, u32[]{:S(2)}) copy-start(f32[50930]{0:T(1024)} %first_ref.1) | copy-start | bytes 611164
  1.9 81.8 %copy-start.3 = (f32[50930]{0:T(1024)S(1)}, f32[50930]{0:T(1024)}, u32[]{:S(2)}) copy-start(f32[50930]{0:T(1024)} %second_ref.1) | copy-start | bytes 611164
  83.7 0.9 %copy-start = (f32[408,128]{1,0:T(8,128)S(1)}, f32[408,128]{1,0:T(8,128)}, u32[]{:S(2)}) copy-start(f32[408,128]{1,0:T(8,128)} %shard_map.145.total_ref) | copy-start | bytes 626692

commit v6 on v5

--- a/solution.py
+++ b/solution.py
@@ -502,7 +502,7 @@
         total = total + self.core_in[(*index, span)].astype(FLOAT)
 
         def number(dims):
-            return sum(1 << "BC".index(dim) for dim in dims)
+            return sum(1 << "BC".index(dim) for dim in dims) - 1
 
         for dim in onward:
             total = total + self.tree_in[value, number(dims + dim), span].astype(FLOAT)
@@ -1132,10 +1132,10 @@
     slots, seen_ref, tgt_own, tgt_ref, meta_ref, grad_ref, loss_ref = take(7)
     spot_enc, spot_dec, local = take(3)
     line, rolled, pixels, spare, send, recv, hand, taken = take(8)
-    even, odd, sums_ref, y_hi, y_lo, dy_home, final_all, dpred_all = take(8)
+    even, odd, grad_even, grad_odd, sums_ref, y_hi, y_lo, dy_home, final_all, dpred_all = take(10)
     weights = Weights(take(len(names)))
     enc_refs, dec_refs = take(15), take(15)
-    core_in, tree_in, column_in, own_ref, turned, near, far, mine = take(8)
+    core_in, tree_in, column_in, own_ref, near, far, mine = take(7)
     spread_send, spread_recv, column_send, column_recv = take(4)
 
     place = position()
@@ -1178,6 +1178,8 @@
         handing.start((0, 1))
         for image in range(LIVE_CAP):
             seen_ref[image] = visible(image)
+        clear_frames(plan, grad_even, grad_odd)
+        sums_ref[...] = jnp.zeros_like(sums_ref)
 
     early = min(-(-layout()["dec_qkv"][0] // (16 * plan.length)), plan.outer)
     first_values, last_values = range(early), range(early, plan.outer)
@@ -1201,30 +1203,31 @@
     for reach in (0, 1):
         spread(first_values, reach)
         spread(last_values, reach)
+    handing.receive((0, 1))
+    for copy in copies[1:]:
+        copy.wait()
+    pick = Images(place, counts_ref, meta_ref)
+    visible, begin, wheres, seens, lives = [], [], [], [], []
+    for image in range(LIVE_CAP):
+        source, kept, live = pick(image)
+        where = placement(kept, ROWS)
+        wheres.append(where.astype(BRAIN))
+        seens.append(jnp.sum(where, axis=1, keepdims=True))
+        lives.append(live)
+        visible.append(seen_ref[source])
+        begin.append(dot(wheres[image], spot_enc[0], DEEP) + dot(wheres[image], spot_enc[1], DEEP))
+    visible = jnp.concatenate(visible, axis=0)
+    begin = jnp.concatenate(begin, axis=0)
     spread(first_values, 2)
     spread(last_values, 2)
     handing.start((2,))
     divide = names.index("dec_qkv")
     fetch(first_values, names[:divide])
-    handing.receive((0, 1))
-    for copy in copies[1:]:
-        copy.wait()
-    sums_ref[...] = jnp.zeros_like(sums_ref)
     order = {name: number for number, name in enumerate(names)}
 
     def add_sum(name, value):
         sums_ref[pl.ds(order[name], 1), pl.ds(0, value.shape[1])] += value
 
-    pick = Images(place, counts_ref, meta_ref)
-
-    visible, begin = [], []
-    for image in range(LIVE_CAP):
-        source, kept, live = pick(image)
-        where = placement(kept, ROWS).astype(BRAIN)
-        visible.append(seen_ref[source])
-        begin.append(dot(where, spot_enc[0], DEEP) + dot(where, spot_enc[1], DEEP))
-    visible = jnp.concatenate(visible, axis=0)
-    begin = jnp.concatenate(begin, axis=0)
     enc_rows = LIVE_CAP * HOME
     enc = kept_view(enc_refs)
     down = lax.broadcasted_iota(jnp.int32, (enc_rows, enc_rows), 0)
@@ -1242,21 +1245,12 @@
         y_hi[image] = upper[image * HOME : (image + 1) * HOME]
         y_lo[image] = lower[image * HOME : (image + 1) * HOME]
     fetch(last_values, names[divide:])
-    clear_frames(plan, even, odd)
-    view = odd.at[pl.ds(8, plan.frame_rows)]
+    view = grad_odd.at[pl.ds(8, plan.frame_rows)]
     real = lax.broadcasted_iota(jnp.int32, (ROWS, 1), 0) < NP
     usable_dec = lax.broadcasted_iota(jnp.int32, (ROWS, ROWS), 0) < NP
 
     dec = kept_view(dec_refs)
     dec_rows = [pl.ds(image * ROWS, ROWS) for image in range(LIVE_CAP)]
-    wheres, seens, lives = [], [], []
-    for image in range(LIVE_CAP):
-        source, kept, live = pick(image)
-        where = placement(kept, ROWS)
-        wheres.append(where.astype(BRAIN))
-        seens.append(jnp.sum(where, axis=1, keepdims=True))
-        lives.append(live)
-
     def unseen(image):
         return 1.0 - seens[image]
 
@@ -1295,14 +1289,14 @@
         if bias.endswith("qvb"):
             width = summed.shape[1] // 3
             summed = jnp.concatenate([summed[:, :width], summed[:, 2 * width :]], axis=1)
-        write_grad(even, view, bias, lambda start, size: summed[:, start : start + size])
+        write_grad(grad_even, view, bias, lambda start, size: summed[:, start : start + size])
         turned = left.T
-        write_grad(even, view, name, lambda start, size: dot(turned, right[:, start : start + size]))
+        write_grad(grad_even, view, name, lambda start, size: dot(turned, right[:, start : start + size]))
 
     def emit_norms(wanted_names):
         for name in wanted_names:
             row = pl.ds(order[name], 1)
-            write_grad(even, view, name, lambda start, size, row=row: sums_ref[row, pl.ds(start, size)])
+            write_grad(grad_even, view, name, lambda start, size, row=row: sums_ref[row, pl.ds(start, size)])
 
     reducer = Reducer(
         plan, place, grad_ref, core_in, tree_in, column_in, own_ref, sender, (column_send, column_recv)
@@ -1311,7 +1305,7 @@
     waves = [range(low, high) for low, high in zip(floors + [0], [plan.depths] + floors)]
 
     def leave(wave):
-        emit_slots(plan, even, odd, grad_ref, waves[wave])
+        emit_slots(plan, grad_even, grad_odd, grad_ref, waves[wave])
         for depth in waves[wave]:
             reducer.share(depth)
 
@@ -1372,7 +1366,7 @@
     collect(3, -1)
     reducer.finish()
     pending = finish_body(
-        plan, place, counts_ref, loss_ref, own_ref, total_out, turned, near, far, mine, sender
+        plan, place, counts_ref, loss_ref, own_ref, total_out, rolled, near, far, mine, sender
     )
     gather.close()
     reducer.close()
@@ -1433,6 +1427,8 @@
             dma((copies,)),
             dma((2, 3, 3)),
             dma((2, 3)),
+            pltpu.VMEM((plan.border + 8, LANES), FLOAT),
+            pltpu.VMEM((plan.frame_rows, LANES), FLOAT),
             pltpu.VMEM((plan.border + rows, LANES), FLOAT),
             pltpu.VMEM((plan.frame_rows + 8, LANES), FLOAT),
             pltpu.VMEM((48, E), FLOAT),
@@ -1445,9 +1441,8 @@
             *kept_scratch(1, LIVE_CAP * HOME, D, FF, HEADS),
             *kept_scratch(LIVE_CAP, ROWS, E, DFF, DHEADS),
             pltpu.VMEM((depths, 2, 2, rows, LANES), BRAIN),
-            pltpu.VMEM((depths, 4, rows, LANES), BRAIN),
+            pltpu.VMEM((depths, 3, rows, LANES), BRAIN),
             pltpu.VMEM((depths, rows, LANES), BRAIN),
-            pltpu.VMEM((rows, LANES), FLOAT),
             pltpu.VMEM((rows, LANES), FLOAT),
             pltpu.VMEM((8, 8, LANES), FLOAT),
             pltpu.VMEM((depths, 8, LANES), FLOAT),
@@ -1458,7 +1453,7 @@
             dma((depths, len(plan.halves))),
         ],
         compiler_params=pltpu.CompilerParams(
-            collective_id=0, has_side_effects=True, vmem_limit_bytes=60 << 20
+            collective_id=0, has_side_effects=True, vmem_limit_bytes=62 << 20
         ),
     )(counts, keep, master, patches, targets, spot_enc, spot_dec)
 

time: 86.7 us -> 86.4 us (level)
  no operation moved by 1% of the time
where the time goes in v6:
time: 86.4 us; the launch traced here: 86.2 us
  Pallas kernels  83.1 us (96%)
  between operations  2.15 us (2%)
  local copies, waits for them, and re-layouts  0.94 us (1%)
    pallas_call x1, Pallas kernels, whole_step(): pl.pallas_call(functools.partial(whole_body, plan), out_shape=jax.ShapeDt...  81.4 us

profile of v6, /device:TPU:0, one launch (start us, length us, event | category | flops | bytes accessed | tf_op | source)
XLA Modules:
  0.0 86.2 jit_solution(13041562102611450176)
XLA Ops:
  1.9 0.0 copy-start.1
  1.9 0.0 copy-start.2
  1.9 0.0 copy-start.3
  2.0 81.4 %shard_map.145.total_ref = f32[408,128]{1,0:T(8,128)} custom-call(s32[1,1]{1,0:T(1,128)S(6)} %copy.16.counts_ref, s32[6,49]{1,0:T(8,128)} %keep_ref.1, f32[50930]{0:T(1024)} %master_ref.1, bf16[6,196,768]{2,1,0:T(8,128)(2,1)} %patches_ref.1, bf16[6,196,768]{2,1,0:T(8,128)(2,1)} %targets_ref.1, bf16[2,208,192]{2,1,0:T(8,128)(2,1)} %constant.4.clone.enc_table, ...), custom_call_target="tpu_custom_call" | custom-call | tf_op jit(solution)/shard_map/pallas_call | solution.py:1406
  83.4 0.0 copy-done.1
  83.4 0.0 copy-done.2
  83.4 0.0 copy-done.3
  83.4 0.0 copy-start
  83.4 0.9 %copy-done = f32[408,128]{1,0:T(8,128)S(1)} copy-done((f32[408,128]{1,0:T(8,128)S(1)}, f32[408,128]{1,0:T(8,128)}, u32[]{:S(2)}) %copy-start) | copy-done | bytes 208920
  84.4 1.7 %shard_map.146 = (f32[50930]{0:T(1024)}, f32[50930]{0:T(1024)}, f32[50930]{0:T(1024)}, bf16[50930]{0:T(1024)(128)(2,1)}, f32[1,1]{1,0:T(1,128)}, /*index=5*/f32[1,1]{1,0:T(1,128)}) custom-call(s32[1]{0:T(128)S(6)} %copy.17.step_ref, f32[408,128]{1,0:T(8,128)S(1)} %copy-done, f32[50930]{0:T(1024)S(1)} %copy-done.1, f32[50930]{0:T(1024)S(1)} %copy-done.2, ...), custom_call_target="tpu_custom_call" | custom-call | tf_op jit(solution)/shard_map/pallas_call | solution.py:703
Async XLA Ops:
  1.9 81.5 %copy-start.1 = (f32[50930]{0:T(1024)S(1)}, f32[50930]{0:T(1024)}, u32[]{:S(2)}) copy-start(f32[50930]{0:T(1024)} %master_ref.1) | copy-start | bytes 611164
  1.9 81.5 %copy-start.2 = (f32[50930]{0:T(1024)S(1)}, f32[50930]{0:T(1024)}, u32[]{:S(2)}) copy-start(f32[50930]{0:T(1024)} %first_ref.1) | copy-start | bytes 611164
  1.9 81.5 %copy-start.3 = (f32[50930]{0:T(1024)S(1)}, f32[50930]{0:T(1024)}, u32[]{:S(2)}) copy-start(f32[50930]{0:T(1024)} %second_ref.1) | copy-start | bytes 611164
  83.4 0.9 %copy-start = (f32[408,128]{1,0:T(8,128)S(1)}, f32[408,128]{1,0:T(8,128)}, u32[]{:S(2)}) copy-start(f32[408,128]{1,0:T(8,128)} %shard_map.145.total_ref) | copy-start | bytes 626692

commit v7 on v6

--- a/solution.py
+++ b/solution.py
@@ -1349,8 +1349,8 @@
     home_open(d_encoded, enc, weights, "enc_")
     block_grads(enc, "enc_", ("fc2", "fc1"), emit)
     emit_norms(("encg", "encb"))
+    collect(1, 1)
     leave(2)
-    collect(1, 1)
     d_first = home_middle(d_encoded, enc, weights, "enc_", HEADS, add_sum).astype(BRAIN)
     collect(2, 1)
     collect(1, 0)

time: 86.4 us -> 86.5 us (level)
  no operation moved by 1% of the time
where the time goes in v7:
time: 86.5 us; the launch traced here: 86.3 us
  Pallas kernels  83.2 us (96%)
  between operations  2.15 us (2%)
  local copies, waits for them, and re-layouts  0.94 us (1%)
    pallas_call x1, Pallas kernels, whole_step(): pl.pallas_call(functools.partial(whole_body, plan), out_shape=jax.ShapeDt...  81.6 us

profile of v7, /device:TPU:0, one launch (start us, length us, event | category | flops | bytes accessed | tf_op | source)
XLA Modules:
  0.0 86.3 jit_solution(6842354955876510453)
XLA Ops:
  1.9 0.0 copy-start.1
  1.9 0.0 copy-start.2
  1.9 0.0 copy-start.3
  2.0 81.6 %shard_map.145.total_ref = f32[408,128]{1,0:T(8,128)} custom-call(s32[1,1]{1,0:T(1,128)S(6)} %copy.16.counts_ref, s32[6,49]{1,0:T(8,128)} %keep_ref.1, f32[50930]{0:T(1024)} %master_ref.1, bf16[6,196,768]{2,1,0:T(8,128)(2,1)} %patches_ref.1, bf16[6,196,768]{2,1,0:T(8,128)(2,1)} %targets_ref.1, bf16[2,208,192]{2,1,0:T(8,128)(2,1)} %constant.4.clone.enc_table, ...), custom_call_target="tpu_custom_call" | custom-call | tf_op jit(solution)/shard_map/pallas_call | solution.py:1406
  83.5 0.0 copy-done.1
  83.5 0.0 copy-done.2
  83.5 0.0 copy-done.3
  83.5 0.0 copy-start
  83.6 0.9 %copy-done = f32[408,128]{1,0:T(8,128)S(1)} copy-done((f32[408,128]{1,0:T(8,128)S(1)}, f32[408,128]{1,0:T(8,128)}, u32[]{:S(2)}) %copy-start) | copy-done | bytes 208920
  84.5 1.7 %shard_map.146 = (f32[50930]{0:T(1024)}, f32[50930]{0:T(1024)}, f32[50930]{0:T(1024)}, bf16[50930]{0:T(1024)(128)(2,1)}, f32[1,1]{1,0:T(1,128)}, /*index=5*/f32[1,1]{1,0:T(1,128)}) custom-call(s32[1]{0:T(128)S(6)} %copy.17.step_ref, f32[408,128]{1,0:T(8,128)S(1)} %copy-done, f32[50930]{0:T(1024)S(1)} %copy-done.1, f32[50930]{0:T(1024)S(1)} %copy-done.2, ...), custom_call_target="tpu_custom_call" | custom-call | tf_op jit(solution)/shard_map/pallas_call | solution.py:703
Async XLA Ops:
  1.9 81.6 %copy-start.1 = (f32[50930]{0:T(1024)S(1)}, f32[50930]{0:T(1024)}, u32[]{:S(2)}) copy-start(f32[50930]{0:T(1024)} %master_ref.1) | copy-start | bytes 611164
  1.9 81.6 %copy-start.2 = (f32[50930]{0:T(1024)S(1)}, f32[50930]{0:T(1024)}, u32[]{:S(2)}) copy-start(f32[50930]{0:T(1024)} %first_ref.1) | copy-start | bytes 611164
  1.9 81.6 %copy-start.3 = (f32[50930]{0:T(1024)S(1)}, f32[50930]{0:T(1024)}, u32[]{:S(2)}) copy-start(f32[50930]{0:T(1024)} %second_ref.1) | copy-start | bytes 611164
  83.5 0.9 %copy-start = (f32[408,128]{1,0:T(8,128)S(1)}, f32[408,128]{1,0:T(8,128)}, u32[]{:S(2)}) copy-start(f32[408,128]{1,0:T(8,128)} %shard_map.145.total_ref) | copy-start | bytes 626692
